TPU v7x, 512 devices: a whole 4x4x16 slice. The times are simulated.
512 devices in a mesh: ctx: 16 (over x, y_hi, core), exp: 32 (over y_lo, z).
Axes of the slice: x: 4, y: 4 (y_hi: 2, y_lo: 2; y = y_hi * 2 + y_lo), z: 16, core: 2. Of those that a mesh axis runs over, the one named last changes fastest.
Arguments:
- hidden_in: bfloat16 [3072, 4096], P('ctx', 'exp'), may hold values from -5 to 5
- query_nope: bfloat16 [3072, 4096], P('ctx', 'exp'), may hold values from -200 to 200
- query_rope: bfloat16 [3072, 2048], P('ctx', 'exp'), may hold values from -6 to 6
- key_nope: bfloat16 [3072, 4096], P('ctx', 'exp'), may hold values from -200 to 200
- key_rope: bfloat16 [3072, 32], P('ctx'), may hold values from -6 to 6
- values: bfloat16 [3072, 4096], P('ctx', 'exp'), may hold values from -6 to 6
- norm_gain: float32 [4096], P('exp'), may hold values from 0.5 to 1.5
- expert_route: int32 [3072], P('ctx'), may hold values from 0 to 31, as said below
- affinity: float32 [3072, 8], P('ctx'), may hold values from 0.05 to 1
- gate_weight: bfloat16 [32, 4096, 2048], P('exp', None, 'ctx'), may hold values from -0.09375 to 0.09375
- up_weight: bfloat16 [32, 4096, 2048], P('exp', None, 'ctx'), may hold values from -0.09375 to 0.09375
- down_weight: bfloat16 [32, 2048, 4096], P('exp', 'ctx'), may hold values from -0.125 to 0.125
- cotangent: bfloat16 [3072, 4096], P('ctx', 'exp'), may hold values from -6 to 6
Outputs:
- layer_out: bfloat16 [3072, 4096], P('ctx', 'exp')
- grad_hidden: bfloat16 [3072, 4096], P('ctx', 'exp')
- grad_query_nope: bfloat16 [3072, 4096], P('ctx', 'exp')
- grad_query_rope: bfloat16 [3072, 2048], P('ctx', 'exp')
- grad_key_nope: bfloat16 [3072, 4096], P('ctx', 'exp')
- grad_key_rope: bfloat16 [3072, 32], P('ctx')
- grad_values: bfloat16 [3072, 4096], P('ctx', 'exp')
Inputs may be any that keep to these rules, and one draw needn't show every extreme that they name: `expert_route`: among the 192 positions of one block (block k holds positions k * 192 to (k + 1) * 192 - 1), at most 12 name one expert, and some expert is named exactly 12 times in every block.
All inputs are finite; a program needn't handle non-finite values.
Results may differ from a plain program's by a relative error of at most 0.03.
Values may be sent and summed in bfloat16 or wider, within the bound.
No kernel may reach another device: no remote copies, remote signals or barrier semaphores. Data moves between devices by JAX's collectives and lax.ppermute only.
A program may use at most 64 MiB of HBM per device.

v0:
```python
import math

import jax
import jax.numpy as jnp
from jax import lax
from jax.sharding import PartitionSpec as P

NOPE = 64
ROPE = 32
VDIM = 64
D = 4096


norm_eps = 1e-06
route_scale = 2.5
masked_low = -1e30


def shifted(block, axis, distance):
    devices = range(lax.axis_size(axis))
    route = [(i - distance, i) for i in devices if i - distance in devices]
    return lax.ppermute(block, axis, route)


def shifted_2(value, axis, steps):
    count = lax.axis_size(axis)
    pairs = [(source, (source + steps) % count) for source in range(count)]
    return lax.ppermute(value, axis, pairs)


def head_scores(query_heads, query_rot, key_heads, key_rot, query_places, key_places):
    score_scale = 1.0 / math.sqrt(NOPE + ROPE)
    first_part = jnp.einsum(
        "thd,uhd->htu", query_heads, key_heads, preferred_element_type=jnp.float32
    )
    second_part = jnp.einsum("thr,ur->htu", query_rot, key_rot, preferred_element_type=jnp.float32)
    visible = key_places[None, :] <= query_places[:, None]
    return (jnp.where(visible[None], (first_part + second_part) * score_scale, masked_low), visible)


def split_block(key_block, row_count, head_count):
    nope_width = head_count * NOPE
    key_heads = key_block[:, :nope_width].reshape(row_count, head_count, NOPE)
    key_rot = key_block[:, nope_width : nope_width + ROPE]
    value_heads = key_block[:, nope_width + ROPE :].reshape(row_count, head_count, VDIM)
    return (key_heads, key_rot, value_heads)


def attention_forward(query_heads, query_rot, own_keys, ctx_index):
    ctx_count = lax.axis_size("ctx")
    row_count, head_count = (query_heads.shape[0], query_heads.shape[1])
    query_places = ctx_index * row_count + jnp.arange(row_count)

    def absorb(softmax_state, key_block, source_index):
        running_max, running_sum, running_acc = softmax_state
        key_heads, key_rot, value_heads = split_block(key_block, row_count, head_count)
        key_places = source_index * row_count + jnp.arange(row_count)
        scores, visible = head_scores(
            query_heads, query_rot, key_heads, key_rot, query_places, key_places
        )
        new_max = jnp.maximum(running_max, jnp.max(scores, -1))
        weights = jnp.where(visible[None], jnp.exp(scores - new_max[..., None]), 0.0)
        factor = jnp.exp(running_max - new_max)
        new_sum = running_sum * factor + jnp.sum(weights, -1)
        new_acc = running_acc * factor[..., None] + jnp.einsum(
            "htu,uhv->htv",
            weights.astype(jnp.bfloat16),
            value_heads,
            preferred_element_type=jnp.float32,
        )
        return (new_max, new_sum, new_acc)

    start_state = (
        jnp.full((head_count, row_count), masked_low, jnp.float32),
        jnp.zeros((head_count, row_count), jnp.float32),
        jnp.zeros((head_count, row_count, VDIM), jnp.float32),
    )
    first_state = absorb(start_state, own_keys, ctx_index)
    stored = jnp.zeros((ctx_count,) + own_keys.shape, own_keys.dtype).at[0].set(own_keys)

    def turn_step(turn_index, carried):
        key_block, stored_blocks, softmax_state = carried
        key_block = shifted(key_block, "ctx", 1)
        stored_blocks = lax.dynamic_update_index_in_dim(stored_blocks, key_block, turn_index, 0)
        source_index = (ctx_index - turn_index) % ctx_count
        return (key_block, stored_blocks, absorb(softmax_state, key_block, source_index))

    key_block, stored, final_state = lax.fori_loop(
        1, ctx_count, turn_step, (own_keys, stored, first_state)
    )
    running_max, running_sum, running_acc = final_state
    mixed_heads = running_acc / running_sum[..., None]
    attended = (
        mixed_heads.transpose(1, 0, 2).reshape(row_count, head_count * VDIM).astype(jnp.bfloat16)
    )
    return (attended, running_max + jnp.log(running_sum), stored)


def attention_backward(query_heads, query_rot, stored, grad_heads, log_total, row_dot, ctx_index):
    ctx_count = lax.axis_size("ctx")
    row_count, head_count = (query_heads.shape[0], query_heads.shape[1])
    score_scale = 1.0 / math.sqrt(NOPE + ROPE)
    query_places = ctx_index * row_count + jnp.arange(row_count)

    def contribute(key_block, source_index):
        key_heads, key_rot, value_heads = split_block(key_block, row_count, head_count)
        key_places = source_index * row_count + jnp.arange(row_count)
        scores, visible = head_scores(
            query_heads, query_rot, key_heads, key_rot, query_places, key_places
        )
        probs = jnp.where(visible[None], jnp.exp(scores - log_total[..., None]), 0.0)
        grad_vals = jnp.einsum(
            "htu,thv->uhv",
            probs.astype(jnp.bfloat16),
            grad_heads,
            preferred_element_type=jnp.float32,
        )
        grad_probs = jnp.einsum(
            "thv,uhv->htu", grad_heads, value_heads, preferred_element_type=jnp.float32
        )
        grad_scores = (probs * (grad_probs - row_dot[..., None])).astype(jnp.bfloat16)
        gq_nope = score_scale * jnp.einsum(
            "htu,uhd->thd", grad_scores, key_heads, preferred_element_type=jnp.float32
        )
        gq_rope = score_scale * jnp.einsum(
            "htu,ur->thr", grad_scores, key_rot, preferred_element_type=jnp.float32
        )
        gk_nope = score_scale * jnp.einsum(
            "htu,thd->uhd", grad_scores, query_heads, preferred_element_type=jnp.float32
        )
        gk_rope = score_scale * jnp.einsum(
            "htu,thr->ur", grad_scores, query_rot, preferred_element_type=jnp.float32
        )
        grad_keys = jnp.concatenate(
            [gk_nope.reshape(row_count, -1), gk_rope, grad_vals.reshape(row_count, -1)], 1
        )
        return (gq_nope, gq_rope, grad_keys)

    gq_nope, gq_rope, grad_keys = contribute(stored[0], ctx_index)

    def turn_step(turn_index, carried):
        moving_grads, nope_total, rope_total = carried
        moving_grads = shifted_2(moving_grads.astype(jnp.bfloat16), "ctx", 1).astype(
            moving_grads.dtype
        )
        key_block = lax.dynamic_index_in_dim(stored, turn_index, 0, keepdims=False)
        source_index = (ctx_index - turn_index) % ctx_count
        more_nope, more_rope, more_keys = contribute(key_block, source_index)
        return (moving_grads + more_keys, nope_total + more_nope, rope_total + more_rope)

    grad_keys, gq_nope, gq_rope = lax.fori_loop(
        1, ctx_count, turn_step, (grad_keys, gq_nope, gq_rope)
    )
    grad_keys = shifted_2(grad_keys.astype(jnp.bfloat16), "ctx", 1).astype(grad_keys.dtype)
    return (gq_nope.reshape(row_count, -1), gq_rope.reshape(row_count, -1), grad_keys)


def route_tables(expert_route, expert_count, slot_count):
    expert_hits = (expert_route[:, None] == jnp.arange(expert_count)[None, :]).astype(jnp.int32)
    rank_within = jnp.sum((jnp.cumsum(expert_hits, 0) - expert_hits) * expert_hits, 1)
    slot_index = expert_route * slot_count + rank_within
    return slot_index[None, :] == jnp.arange(expert_count * slot_count)[:, None]


def apply_table(table_in, payload):
    return jnp.dot(
        table_in.astype(jnp.bfloat16), payload, preferred_element_type=jnp.float32
    ).astype(jnp.bfloat16)


def expert_forward(gathered, gate_mat, up_mat, down_mat):
    gate_val = jnp.dot(gathered, gate_mat, preferred_element_type=jnp.float32)
    up_val = jnp.dot(gathered, up_mat, preferred_element_type=jnp.float32)
    active = (jax.nn.silu(gate_val) * up_val).astype(jnp.bfloat16)
    return (jnp.dot(active, down_mat, preferred_element_type=jnp.float32), gate_val, up_val)


def expert_backward(gathered_grad, gate_val, up_val, gate_mat, up_mat, down_mat):
    contract_dims = (((1,), (1,)), ((), ()))
    grad_active = lax.dot_general(
        gathered_grad, down_mat, contract_dims, preferred_element_type=jnp.float32
    )
    sigmoid_gate = jax.nn.sigmoid(gate_val)
    grad_gate = (
        grad_active * up_val * (sigmoid_gate * (1.0 + gate_val * (1.0 - sigmoid_gate)))
    ).astype(jnp.bfloat16)
    grad_up = (grad_active * jax.nn.silu(gate_val)).astype(jnp.bfloat16)
    return lax.dot_general(
        grad_gate, gate_mat, contract_dims, preferred_element_type=jnp.float32
    ) + lax.dot_general(grad_up, up_mat, contract_dims, preferred_element_type=jnp.float32)


def mixture(normed, grad_expert, expert_route, gate_mat, up_mat, down_mat):
    row_count, local_width = normed.shape
    expert_count = lax.axis_size("exp")
    slot_count = 2 * row_count // expert_count
    chosen = route_tables(expert_route, expert_count, slot_count)
    send_normed = apply_table(chosen, normed).reshape(expert_count, slot_count, local_width)
    send_grad = apply_table(chosen, grad_expert).reshape(expert_count, slot_count, local_width)
    recv_normed = lax.all_to_all(send_normed, "exp", split_axis=0, concat_axis=2, tiled=True)
    all_normed = lax.all_gather(recv_normed[0], "ctx", axis=0, tiled=True)
    partial_out, gate_val, up_val = expert_forward(all_normed, gate_mat, up_mat, down_mat)
    summed_out = lax.psum_scatter(
        partial_out.astype(jnp.bfloat16), "ctx", scatter_dimension=0, tiled=True
    )
    home_out = lax.all_to_all(summed_out[None], "exp", split_axis=2, concat_axis=0, tiled=True)
    recv_grad = lax.all_to_all(send_grad, "exp", split_axis=0, concat_axis=2, tiled=True)
    all_grad = lax.all_gather(recv_grad[0], "ctx", axis=0, tiled=True)
    partial_grad = expert_backward(all_grad, gate_val, up_val, gate_mat, up_mat, down_mat)
    summed_grad = lax.psum_scatter(
        partial_grad.astype(jnp.bfloat16), "ctx", scatter_dimension=0, tiled=True
    )
    home_grad = lax.all_to_all(summed_grad[None], "exp", split_axis=2, concat_axis=0, tiled=True)
    chosen_low = chosen.T.astype(jnp.bfloat16)
    token_out = jnp.dot(
        chosen_low, home_out.reshape(-1, local_width), preferred_element_type=jnp.float32
    )
    token_grad = jnp.dot(
        chosen_low, home_grad.reshape(-1, local_width), preferred_element_type=jnp.float32
    )
    return (token_out, token_grad)


def per_device(
    hidden_in,
    query_nope,
    query_rope,
    key_nope,
    key_rope,
    values,
    norm_gain,
    expert_route,
    affinity,
    gate_weight,
    up_weight,
    down_weight,
    cotangent,
):
    row_count, local_width = hidden_in.shape
    head_count = query_nope.shape[1] // NOPE
    ctx_index = lax.axis_index("ctx")
    query_heads = query_nope.reshape(row_count, head_count, NOPE)
    query_rot = query_rope.reshape(row_count, head_count, ROPE)
    own_keys = jnp.concatenate([key_nope, key_rope, values], 1)
    attended, log_total, stored = attention_forward(query_heads, query_rot, own_keys, ctx_index)
    hidden = hidden_in.astype(jnp.float32) + attended.astype(jnp.float32)
    square_sum = lax.psum(jnp.sum(hidden * hidden, -1), "exp")
    inverse = lax.rsqrt(square_sum / D + norm_eps)
    normed = (hidden * inverse[:, None] * norm_gain).astype(jnp.bfloat16)
    gate_share = route_scale * affinity[:, 0] / jnp.sum(affinity, -1)
    grad_in = cotangent.astype(jnp.float32)
    grad_expert = (gate_share[:, None] * grad_in).astype(jnp.bfloat16)
    token_out, token_grad = mixture(
        normed, grad_expert, expert_route, gate_weight[0], up_weight[0], down_weight[0]
    )
    layer_out = (hidden + gate_share[:, None] * token_out).astype(jnp.bfloat16)
    scaled = token_grad * norm_gain
    cross_mean = lax.psum(jnp.sum(scaled * hidden, -1), "exp") / D
    grad_hidden = (
        grad_in + inverse[:, None] * (scaled - hidden * (inverse * inverse * cross_mean)[:, None])
    ).astype(jnp.bfloat16)
    grad_heads = grad_hidden.reshape(row_count, head_count, VDIM)
    out_heads = attended.reshape(row_count, head_count, VDIM)
    row_dot = jnp.sum(grad_heads.astype(jnp.float32) * out_heads.astype(jnp.float32), -1).T
    gq_nope, gq_rope, grad_keys = attention_backward(
        query_heads, query_rot, stored, grad_heads, log_total, row_dot, ctx_index
    )
    nope_width = head_count * NOPE
    grad_key_nope = grad_keys[:, :nope_width]
    rope_local = grad_keys[:, nope_width : nope_width + ROPE]
    grad_vals = grad_keys[:, nope_width + ROPE :]
    grad_key_rope = lax.psum(rope_local, "exp")
    return (
        layer_out,
        grad_hidden,
        gq_nope.astype(jnp.bfloat16),
        gq_rope.astype(jnp.bfloat16),
        grad_key_nope.astype(jnp.bfloat16),
        grad_key_rope.astype(jnp.bfloat16),
        grad_vals.astype(jnp.bfloat16),
    )


def solution(mesh):
    placed = (
        P("ctx", "exp"),
        P("ctx", "exp"),
        P("ctx", "exp"),
        P("ctx", "exp"),
        P("ctx", None),
        P("ctx", "exp"),
        P("exp"),
        P("ctx"),
        P("ctx", None),
        P("exp", None, "ctx"),
        P("exp", None, "ctx"),
        P("exp", "ctx", None),
        P("ctx", "exp"),
    )
    return jax.shard_map(
        per_device,
        mesh=mesh,
        in_specs=placed,
        out_specs=(
            P("ctx", "exp"),
            P("ctx", "exp"),
            P("ctx", "exp"),
            P("ctx", "exp"),
            P("ctx", "exp"),
            P("ctx", None),
            P("ctx", "exp"),
        ),
        check_vma=False,
    )
```

profile of v0, /device:TPU:8, one launch (start us, length us, event | category | flops | bytes accessed | tf_op | source)
XLA Modules:
  0.0 938.9 jit_solution(6574255397825715902)
XLA Ops:
  12.7 140.1 %while.49 = (s32[]{:T(128)}, bf16[192,288]{0,1:T(8,128)(2,1)S(1)}, bf16[16,192,288]{1,2,0:T(8,128)(2,1)}, f32[2,192]{1,0:T(2,128)S(1)}, f32[2,192]{1,0:T(2,128)S...) while((s32[]{:T(128)}, bf16[192,288]{0,1:T(8,128)(2,1)S(1)}, ...), condition=%wide.region_5.6_spmd.clone, body=%wide.region_2.5_spmd.clone.sunk | while | flops 24417424 | bytes 3161464 | solution.py:88
  17.2 5.6 collective-permute-start
  25.4 7.0 collective-permute-start
  34.9 7.0 collective-permute-start
  44.5 7.0 collective-permute-start
  54.1 7.0 collective-permute-start
  63.7 7.0 collective-permute-start
  73.2 7.0 collective-permute-start
  82.8 7.0 collective-permute-start
  92.3 7.0 collective-permute-start
  101.9 7.0 collective-permute-start
  111.5 7.4 collective-permute-start
  121.4 7.9 collective-permute-start
  131.9 7.9 collective-permute-start
  142.4 7.9 collective-permute-start
  153.1 69.3 %psum.21 = f32[192]{0:T(256)S(1)} all-reduce(f32[192]{0:T(256)S(1)} %multiply_reduce_fusion.1), channel_id=1, replica_groups=mesh['ctx'=16,'exp'=32] {'exp'}, use_global_device_ids=true, to_apply=%region_11.12 | all-reduce | flops 192 | bytes 1536 | tf_op jit(solution)/shard_map/psum | solution.py:247
  223.7 18.6 %all_to_all.60 = bf16[32,12,128]{2,1,0:T(8,128)(2,1)S(1)} all-to-all(bf16[32,12,128]{2,1,0:T(8,128)(2,1)S(1)} %reshape.317), channel_id=1, replica_groups=mesh['ctx'=16,'exp'=32] {'exp'}, dimensions={0} | all-to-all | bytes 196608 | tf_op jit(solution)/shard_map/all_to_all | solution.py:200
  243.6 18.6 %all_to_all.61 = bf16[32,12,128]{2,1,0:T(8,128)(2,1)S(1)} all-to-all(bf16[32,12,128]{2,1,0:T(8,128)(2,1)S(1)} %reshape.319), channel_id=1, replica_groups=mesh['ctx'=16,'exp'=32] {'exp'}, dimensions={0} | all-to-all | bytes 196608 | tf_op jit(solution)/shard_map/all_to_all | solution.py:207
  263.8 50.1 %all-gather.5.cloned.1.call-done = bf16[16,12,4096]{2,1,0:T(8,128)(2,1)} async-done(((bf16[1,12,4096]{2,1,0:T(8,128)(2,1)}), bf16[16,12,4096]{2,1,0:T(8,128)(2,1)}) %all-gather.5.cloned.1.call-update) | async-done | bytes 1572880 | tf_op jit(solution)/shard_map/all_gather | solution.py:201
  318.8 61.1 %all-gather.7.cloned.1.call-done = bf16[16,12,4096]{2,1,0:T(8,128)(2,1)} async-done(((bf16[1,12,4096]{2,1,0:T(8,128)(2,1)}), bf16[16,12,4096]{2,1,0:T(8,128)(2,1)}) %all-gather.7.cloned.1.call-update) | async-done | bytes 1572880 | tf_op jit(solution)/shard_map/all_gather | solution.py:208
  386.5 50.3 %fusion.91 = (bf16[16,4096]{1,0:T(8,128)(2,1)S(1)}, bf16[16,4096]{1,0:T(8,128)(2,1)S(1)}) fusion(bf16[192,4096]{1,0:T(8,128)(2,1)S(1)} %convolution_convert_fusion, bf16[192,4096]{1,0:T(8,128)(2,1)} %fusion.31), kind=kCustom, calls=%all-reduce-scatter.2 | all-reduce-scatter fusion | flops 2097153 | bytes 3409920
  440.3 5.7 collective-permute-start.4
  457.5 7.0 collective-permute-start.9
  480.5 23.4 %reduce.5 = bf16[4096,12]{1,0:T(8,128)(2,1)} reduce(bf16[4096,1,12]{2,1,0:T(2,128)(2,1)S(1)} %bitcast.316, bf16[]{:T(256)} %broadcast.322), dimensions={1}, to_apply=%bitcast.191.reduce_sub_computation | reduce | bytes 196610
  507.7 14.1 %all-to-all-start.3 = ((bf16[32,2,768]{2,1,0:T(2,128)(2,1)}), bf16[32,2,768]{2,1,0:T(2,128)(2,1)}, u32[]{:S(2)}, u32[]{:S(2)}) async-start(bf16[32,2,768]{2,1,0:T(2,128)(2,1)} %reshape.351), calls=%async_computation.3 | async-start | bytes 196608 | tf_op jit(solution)/shard_map/all_to_all | solution.py:213
  528.2 23.4 %reduce.4 = bf16[4096,12]{1,0:T(8,128)(2,1)} reduce(bf16[4096,1,12]{2,1,0:T(2,128)(2,1)S(1)} %bitcast.317, bf16[]{:T(256)} %broadcast.322), dimensions={1}, to_apply=%bitcast.189.reduce_sub_computation | reduce | bytes 196610
  555.4 13.2 %all-to-all-start.1 = ((bf16[32,2,768]{2,1,0:T(2,128)(2,1)}), bf16[32,2,768]{2,1,0:T(2,128)(2,1)}, u32[]{:S(2)}, u32[]{:S(2)}) async-start(bf16[32,2,768]{2,1,0:T(2,128)(2,1)} %reshape.349), calls=%async_computation.1 | async-start | bytes 196608 | tf_op jit(solution)/shard_map/all_to_all | solution.py:206
  578.1 62.6 %psum.22 = f32[192]{0:T(256)S(1)} all-reduce(f32[192]{0:T(256)S(1)} %get-tuple-element.879), channel_id=1, replica_groups=mesh['ctx'=16,'exp'=32] {'exp'}, use_global_device_ids=true, to_apply=%region_15.16 | all-reduce | flops 192 | bytes 1536 | tf_op jit(solution)/shard_map/psum | solution.py:258
  644.5 151.9 %while.50 = (s32[]{:T(128)}, bf16[192,288]{0,1:T(8,128)(2,1)S(1)}, f32[192,2,64]{0,2,1:T(8,128)S(1)}, f32[192,2,32]{0,2,1:T(8,128)S(1)}, s32[]{:T(128)}, /*index...) while((s32[]{:T(128)}, bf16[192,288]{0,1:T(8,128)(2,1)S(1)}, ...), condition=%wide.region_18.19_spmd.clone, body=%wide.region_17.18_spmd.clone.sunk | while | flops 62423440 | bytes 4721544 | solution.py:151
  659.4 5.4 collective-permute-done.1
  740.4 5.4 collective-permute-done.1
  811.3 118.4 %psum.23 = bf16[192,32]{1,0:T(8,128)(2,1)S(1)} all-reduce(f32[192,32]{1,0:T(8,128)S(1)} %slice_convert_fusion), channel_id=1, replica_groups=mesh['ctx'=16,'exp'=32] {'exp'}, use_global_device_ids=true, to_apply=%region_19.20 | all-reduce | flops 6144 | bytes 36864 | tf_op jit(solution)/shard_map/psum | solution.py:272
  (594 shorter events, 274.1 us)
Async XLA Ops:
  7.2 306.7 %all-gather.5.cloned.1.call-start = ((), (), s32[]{:S(2)}) async-start(), calls=%async_computation.4 | async-start | bytes 2228224 | tf_op jit(solution)/shard_map/all_gather | solution.py:201
  92.3 8.0 collective-permute-start
  111.5 8.4 collective-permute-start
  121.4 8.9 collective-permute-start
  131.9 8.9 collective-permute-start
  142.4 8.9 collective-permute-start
  243.1 136.8 %all-gather.7.cloned.1.call-start = ((), (), s32[]{:S(2)}) async-start(), calls=%async_computation.5 | async-start | bytes 2228224 | tf_op jit(solution)/shard_map/all_gather | solution.py:208
  436.9 20.6 %collective-permute-start.3 = (bf16[16,4096]{1,0:T(8,128)(2,1)S(1)}, bf16[16,4096]{1,0:T(8,128)(2,1)S(1)}, u32[]{:S(2)}, u32[]{:S(2)}) collective-permute-start(bf16[16,4096]{1,0:T(8,128)(2,1)S(1)} %get-tuple-element.857), channel_id=1, source_target_pairs={{0,32},{32,64},{64,96},{96,128},{128,160},{160,192},{192,224},{224... | collective-permute-start | bytes 393224
  440.3 24.3 %collective-permute-start.4 = (bf16[16,4096]{1,0:T(8,128)(2,1)S(1)}, bf16[16,4096]{1,0:T(8,128)(2,1)S(1)}, u32[]{:S(2)}, u32[]{:S(2)}) collective-permute-start(bf16[16,4096]{1,0:T(8,128)(2,1)S(1)} %get-tuple-element.857), channel_id=1, source_target_pairs={{0,64},{32,96},{64,128},{96,160},{128,192},{160,224},{192,256},{22... | collective-permute-start | bytes 393224
  446.0 8.6 collective-permute-start.6
  448.5 20.8 %collective-permute-start.5 = (bf16[16,4096]{1,0:T(8,128)(2,1)S(1)}, bf16[16,4096]{1,0:T(8,128)(2,1)S(1)}, u32[]{:S(2)}, u32[]{:S(2)}) collective-permute-start(bf16[16,4096]{1,0:T(8,128)(2,1)S(1)} %get-tuple-element.857), channel_id=1, source_target_pairs={{0,96},{32,128},{64,160},{96,192},{128,224},{160,256},{192,288},{2... | collective-permute-start | bytes 393224
  453.3 17.2 %collective-permute-start.7 = (bf16[16,4096]{1,0:T(8,128)(2,1)S(1)}, bf16[16,4096]{1,0:T(8,128)(2,1)S(1)}, u32[]{:S(2)}, u32[]{:S(2)}) collective-permute-start(bf16[16,4096]{1,0:T(8,128)(2,1)S(1)} %get-tuple-element.858), channel_id=1, source_target_pairs={{0,32},{32,64},{64,96},{96,128},{128,160},{160,192},{192,224},{224... | collective-permute-start | bytes 393224
  454.6 15.9 %collective-permute-start.8 = (bf16[16,4096]{1,0:T(8,128)(2,1)S(1)}, bf16[16,4096]{1,0:T(8,128)(2,1)S(1)}, u32[]{:S(2)}, u32[]{:S(2)}) collective-permute-start(bf16[16,4096]{1,0:T(8,128)(2,1)S(1)} %get-tuple-element.858), channel_id=1, source_target_pairs={{0,64},{32,96},{64,128},{96,160},{128,192},{160,224},{192,256},{22... | collective-permute-start | bytes 393224
  457.5 13.6 %collective-permute-start.9 = (bf16[16,4096]{1,0:T(8,128)(2,1)S(1)}, bf16[16,4096]{1,0:T(8,128)(2,1)}, u32[]{:S(2)}, u32[]{:S(2)}) collective-permute-start(bf16[16,4096]{1,0:T(8,128)(2,1)S(1)} %get-tuple-element.858), channel_id=1, source_target_pairs={{0,96},{32,128},{64,160},{96,192},{128,224},{160,256},{192,288},{2... | collective-permute-start | bytes 393224
  507.7 47.7 %all-to-all-start.3 = ((bf16[32,2,768]{2,1,0:T(2,128)(2,1)}), bf16[32,2,768]{2,1,0:T(2,128)(2,1)}, u32[]{:S(2)}, u32[]{:S(2)}) async-start(bf16[32,2,768]{2,1,0:T(2,128)(2,1)} %reshape.351), calls=%async_computation.3 | async-start | bytes 196608 | tf_op jit(solution)/shard_map/all_to_all | solution.py:213
  555.4 243.8 %all-to-all-start.1 = ((bf16[32,2,768]{2,1,0:T(2,128)(2,1)}), bf16[32,2,768]{2,1,0:T(2,128)(2,1)}, u32[]{:S(2)}, u32[]{:S(2)}) async-start(bf16[32,2,768]{2,1,0:T(2,128)(2,1)} %reshape.349), calls=%async_computation.1 | async-start | bytes 196608 | tf_op jit(solution)/shard_map/all_to_all | solution.py:206
  644.5 10.1 %collective-permute-start.1 = (bf16[192,288]{0,1:T(8,128)(2,1)S(1)}, bf16[192,288]{0,1:T(8,128)(2,1)S(1)}, u32[]{:S(2)}, u32[]{:S(2)}) collective-permute-start(bf16[192,288]{0,1:T(8,128)(2,1)S(1)} %get-tuple-element.1104), channel_id=1, source_target_pairs={{0,32},{32,64},{64,96},{96,128},{128,160},{160,192},{192,224},{224... | collective-permute-start | bytes 331784 | tf_op jit(solution)/shard_map/while/body/eval_jaxpr/ppermute | solution.py:28
  654.7 10.1 %collective-permute-start.1 = (bf16[192,288]{0,1:T(8,128)(2,1)S(1)}, bf16[192,288]{0,1:T(8,128)(2,1)S(1)}, u32[]{:S(2)}, u32[]{:S(2)}) collective-permute-start(bf16[192,288]{0,1:T(8,128)(2,1)S(1)} %get-tuple-element.1104), channel_id=1, source_target_pairs={{0,32},{32,64},{64,96},{96,128},{128,160},{160,192},{192,224},{224... | collective-permute-start | bytes 331784 | tf_op jit(solution)/shard_map/while/body/eval_jaxpr/ppermute | solution.py:28
  664.8 10.1 %collective-permute-start.1 = (bf16[192,288]{0,1:T(8,128)(2,1)S(1)}, bf16[192,288]{0,1:T(8,128)(2,1)S(1)}, u32[]{:S(2)}, u32[]{:S(2)}) collective-permute-start(bf16[192,288]{0,1:T(8,128)(2,1)S(1)} %get-tuple-element.1104), channel_id=1, source_target_pairs={{0,32},{32,64},{64,96},{96,128},{128,160},{160,192},{192,224},{224... | collective-permute-start | bytes 331784 | tf_op jit(solution)/shard_map/while/body/eval_jaxpr/ppermute | solution.py:28
  674.9 10.1 %collective-permute-start.1 = (bf16[192,288]{0,1:T(8,128)(2,1)S(1)}, bf16[192,288]{0,1:T(8,128)(2,1)S(1)}, u32[]{:S(2)}, u32[]{:S(2)}) collective-permute-start(bf16[192,288]{0,1:T(8,128)(2,1)S(1)} %get-tuple-element.1104), channel_id=1, source_target_pairs={{0,32},{32,64},{64,96},{96,128},{128,160},{160,192},{192,224},{224... | collective-permute-start | bytes 331784 | tf_op jit(solution)/shard_map/while/body/eval_jaxpr/ppermute | solution.py:28
  685.1 10.1 %collective-permute-start.1 = (bf16[192,288]{0,1:T(8,128)(2,1)S(1)}, bf16[192,288]{0,1:T(8,128)(2,1)S(1)}, u32[]{:S(2)}, u32[]{:S(2)}) collective-permute-start(bf16[192,288]{0,1:T(8,128)(2,1)S(1)} %get-tuple-element.1104), channel_id=1, source_target_pairs={{0,32},{32,64},{64,96},{96,128},{128,160},{160,192},{192,224},{224... | collective-permute-start | bytes 331784 | tf_op jit(solution)/shard_map/while/body/eval_jaxpr/ppermute | solution.py:28
  695.2 10.1 %collective-permute-start.1 = (bf16[192,288]{0,1:T(8,128)(2,1)S(1)}, bf16[192,288]{0,1:T(8,128)(2,1)S(1)}, u32[]{:S(2)}, u32[]{:S(2)}) collective-permute-start(bf16[192,288]{0,1:T(8,128)(2,1)S(1)} %get-tuple-element.1104), channel_id=1, source_target_pairs={{0,32},{32,64},{64,96},{96,128},{128,160},{160,192},{192,224},{224... | collective-permute-start | bytes 331784 | tf_op jit(solution)/shard_map/while/body/eval_jaxpr/ppermute | solution.py:28
  705.3 10.1 %collective-permute-start.1 = (bf16[192,288]{0,1:T(8,128)(2,1)S(1)}, bf16[192,288]{0,1:T(8,128)(2,1)S(1)}, u32[]{:S(2)}, u32[]{:S(2)}) collective-permute-start(bf16[192,288]{0,1:T(8,128)(2,1)S(1)} %get-tuple-element.1104), channel_id=1, source_target_pairs={{0,32},{32,64},{64,96},{96,128},{128,160},{160,192},{192,224},{224... | collective-permute-start | bytes 331784 | tf_op jit(solution)/shard_map/while/body/eval_jaxpr/ppermute | solution.py:28
  715.5 10.1 %collective-permute-start.1 = (bf16[192,288]{0,1:T(8,128)(2,1)S(1)}, bf16[192,288]{0,1:T(8,128)(2,1)S(1)}, u32[]{:S(2)}, u32[]{:S(2)}) collective-permute-start(bf16[192,288]{0,1:T(8,128)(2,1)S(1)} %get-tuple-element.1104), channel_id=1, source_target_pairs={{0,32},{32,64},{64,96},{96,128},{128,160},{160,192},{192,224},{224... | collective-permute-start | bytes 331784 | tf_op jit(solution)/shard_map/while/body/eval_jaxpr/ppermute | solution.py:28
  725.6 10.1 %collective-permute-start.1 = (bf16[192,288]{0,1:T(8,128)(2,1)S(1)}, bf16[192,288]{0,1:T(8,128)(2,1)S(1)}, u32[]{:S(2)}, u32[]{:S(2)}) collective-permute-start(bf16[192,288]{0,1:T(8,128)(2,1)S(1)} %get-tuple-element.1104), channel_id=1, source_target_pairs={{0,32},{32,64},{64,96},{96,128},{128,160},{160,192},{192,224},{224... | collective-permute-start | bytes 331784 | tf_op jit(solution)/shard_map/while/body/eval_jaxpr/ppermute | solution.py:28
  735.7 10.1 %collective-permute-start.1 = (bf16[192,288]{0,1:T(8,128)(2,1)S(1)}, bf16[192,288]{0,1:T(8,128)(2,1)S(1)}, u32[]{:S(2)}, u32[]{:S(2)}) collective-permute-start(bf16[192,288]{0,1:T(8,128)(2,1)S(1)} %get-tuple-element.1104), channel_id=1, source_target_pairs={{0,32},{32,64},{64,96},{96,128},{128,160},{160,192},{192,224},{224... | collective-permute-start | bytes 331784 | tf_op jit(solution)/shard_map/while/body/eval_jaxpr/ppermute | solution.py:28
  745.8 10.1 %collective-permute-start.1 = (bf16[192,288]{0,1:T(8,128)(2,1)S(1)}, bf16[192,288]{0,1:T(8,128)(2,1)S(1)}, u32[]{:S(2)}, u32[]{:S(2)}) collective-permute-start(bf16[192,288]{0,1:T(8,128)(2,1)S(1)} %get-tuple-element.1104), channel_id=1, source_target_pairs={{0,32},{32,64},{64,96},{96,128},{128,160},{160,192},{192,224},{224... | collective-permute-start | bytes 331784 | tf_op jit(solution)/shard_map/while/body/eval_jaxpr/ppermute | solution.py:28
  756.0 10.1 %collective-permute-start.1 = (bf16[192,288]{0,1:T(8,128)(2,1)S(1)}, bf16[192,288]{0,1:T(8,128)(2,1)S(1)}, u32[]{:S(2)}, u32[]{:S(2)}) collective-permute-start(bf16[192,288]{0,1:T(8,128)(2,1)S(1)} %get-tuple-element.1104), channel_id=1, source_target_pairs={{0,32},{32,64},{64,96},{96,128},{128,160},{160,192},{192,224},{224... | collective-permute-start | bytes 331784 | tf_op jit(solution)/shard_map/while/body/eval_jaxpr/ppermute | solution.py:28
  766.1 10.1 %collective-permute-start.1 = (bf16[192,288]{0,1:T(8,128)(2,1)S(1)}, bf16[192,288]{0,1:T(8,128)(2,1)S(1)}, u32[]{:S(2)}, u32[]{:S(2)}) collective-permute-start(bf16[192,288]{0,1:T(8,128)(2,1)S(1)} %get-tuple-element.1104), channel_id=1, source_target_pairs={{0,32},{32,64},{64,96},{96,128},{128,160},{160,192},{192,224},{224... | collective-permute-start | bytes 331784 | tf_op jit(solution)/shard_map/while/body/eval_jaxpr/ppermute | solution.py:28
  776.2 10.1 %collective-permute-start.1 = (bf16[192,288]{0,1:T(8,128)(2,1)S(1)}, bf16[192,288]{0,1:T(8,128)(2,1)S(1)}, u32[]{:S(2)}, u32[]{:S(2)}) collective-permute-start(bf16[192,288]{0,1:T(8,128)(2,1)S(1)} %get-tuple-element.1104), channel_id=1, source_target_pairs={{0,32},{32,64},{64,96},{96,128},{128,160},{160,192},{192,224},{224... | collective-permute-start | bytes 331784 | tf_op jit(solution)/shard_map/while/body/eval_jaxpr/ppermute | solution.py:28
  786.4 10.1 %collective-permute-start.1 = (bf16[192,288]{0,1:T(8,128)(2,1)S(1)}, bf16[192,288]{0,1:T(8,128)(2,1)S(1)}, u32[]{:S(2)}, u32[]{:S(2)}) collective-permute-start(bf16[192,288]{0,1:T(8,128)(2,1)S(1)} %get-tuple-element.1104), channel_id=1, source_target_pairs={{0,32},{32,64},{64,96},{96,128},{128,160},{160,192},{192,224},{224... | collective-permute-start | bytes 331784 | tf_op jit(solution)/shard_map/while/body/eval_jaxpr/ppermute | solution.py:28
  797.3 13.3 %collective-permute-start.2 = (bf16[192,288]{1,0:T(8,128)(2,1)}, bf16[192,288]{1,0:T(8,128)(2,1)}, u32[]{:S(2)}, u32[]{:S(2)}) collective-permute-start(bf16[192,288]{1,0:T(8,128)(2,1)} %copy.136), channel_id=1, source_target_pairs={{0,32},{32,64},{64,96},{96,128},{128,160},{160,192},{192,224},{224... | collective-permute-start | bytes 331784 | tf_op jit(solution)/shard_map/ppermute | solution.py:28
  (34 other events, 1646.9 us)
Sparse Core Ops, SparseCore 0:
  243.2 70.6 all-gather.4
  317.2 62.6 all-gather.6
where the time goes:
time: 943 us; the launch traced here: 939 us
  blocking collectives  338 us (36%)
  waiting for transfers between devices  204 us (22%)
  starting transfers between devices  188 us (20%)
  local copies, waits for them, and re-layouts  83.6 us (9%)
  other arithmetic  55.9 us (6%)
  matrix products  50.4 us (5%)
  between operations  15.5 us (2%)
    psum x1, blocking collectives, per_device(): grad_key_rope = lax.psum(rope_local, 'exp')  118 us
    ppermute x15, starting transfers between devices, shifted(): return lax.ppermute(block, axis, route)  101 us
    ppermute x16, waiting for transfers between devices, shifted_2(): return lax.ppermute(value, axis, pairs)  80.5 us
    psum x1, blocking collectives, per_device(): square_sum = lax.psum(jnp.sum(hidden * hidden, -1), 'exp')  69.3 us
    psum x1, blocking collectives, per_device(): cross_mean = lax.psum(jnp.sum(scaled * hidden, -1), 'exp') / D  62.6 us
    all_gather x1, waiting for transfers between devices, mixture(): all_grad = lax.all_gather(recv_grad[0], 'ctx', axis=0, tiled=True)  61.1 us
    unnamed x1, blocking collectives  50.3 us
    all_gather x1, waiting for transfers between devices, mixture(): all_normed = lax.all_gather(recv_normed[0], 'ctx', axis=0, tiled=True)  50.1 us
  transfers between devices with their start and end apart: 43, of which 32 were waited for; matrix products, arithmetic and copies ran while one was open for 12% of the time, Pallas kernels for 0%

commit v1 on v0

v1 whole, which is shorter than its diff:
```python
import functools
import math

import jax
import jax.numpy as jnp
from jax import lax
from jax.experimental import pallas as pl
from jax.experimental.pallas import tpu as pltpu
from jax.sharding import PartitionSpec as P

NOPE = 64
ROPE = 32
VDIM = 64
D = 4096
CAP = 12
SLOT = 16
LANES = 128

norm_eps = 1e-06
route_scale = 2.5
masked_low = -1e30
score_scale = 1.0 / math.sqrt(NOPE + ROPE)

bf16 = jnp.bfloat16
f32 = jnp.float32
VMEM_LIMIT = 56 * 1024 * 1024

KEY = slice(0, 256)
QUERY = slice(128, 384)
VALUE = slice(384, 512)


def nt_dot(a, b):
    return lax.dot_general(a, b, (((1,), (1,)), ((), ())), preferred_element_type=f32)


def nn_dot(a, b):
    return jnp.dot(a, b, preferred_element_type=f32)


def lanes_of(shape):
    return lax.broadcasted_iota(jnp.int32, shape, len(shape) - 1)


def pieces_of(value, count):
    pieces = []
    for _ in range(count):
        piece = value.astype(bf16).astype(f32)
        pieces.append(piece)
        value = value - piece
    return pieces


def own_query(block, head):
    rows = block.shape[0]
    lane = lanes_of((rows, LANES))
    zero = jnp.zeros((rows, LANES), bf16)
    nope = jnp.where(lane // NOPE == head, block[:, 256:384], zero)
    start = ROPE + head * ROPE
    rot = pltpu.roll(block[:, 128:256].astype(f32), LANES - start, 1)
    rot = jnp.where(lane < ROPE, rot, 0.0).astype(bf16)
    return jnp.concatenate([nope, rot], 1)


def own_key(block, head):
    rows = block.shape[0]
    lane = lanes_of((rows, LANES))
    zero = jnp.zeros((rows, LANES), bf16)
    nope = jnp.where(lane // NOPE == head, block[:, 0:128], zero)
    start = ROPE + head * ROPE
    rot = pltpu.roll(block[:, 128:256].astype(f32), start, 1)
    rot = jnp.where(lane // ROPE == 1 + head, rot, 0.0).astype(bf16)
    return jnp.concatenate([rot, nope], 1)


def pair_places(rows, core):
    lane = lanes_of((rows, 2 * rows))
    return lane - jnp.where(lane >= rows, 2 * rows, 0) * core


def slots_along_rows(route_row, experts):
    count = route_row.shape[1]
    hits = (lax.broadcasted_iota(jnp.int32, (experts, count), 0) == route_row).astype(f32)
    before = lax.broadcasted_iota(jnp.int32, (count, count), 0) < lanes_of((count, count))
    ranks = nn_dot(hits.astype(bf16), before.astype(f32).astype(bf16))
    rank = jnp.sum(ranks * hits, 0, keepdims=True)
    return route_row * SLOT + rank.astype(jnp.int32)


def slots_along_columns(route_column, experts):
    count = route_column.shape[0]
    hits = (lanes_of((count, experts)) == route_column).astype(f32)
    before = lanes_of((count, count)) < lax.broadcasted_iota(jnp.int32, (count, count), 0)
    ranks = nn_dot(before.astype(f32).astype(bf16), hits.astype(bf16))
    rank = jnp.sum(ranks * hits, 1, keepdims=True)
    return route_column * SLOT + rank.astype(jnp.int32)


def gate_share_of(affinity):
    return route_scale * affinity[:, 0:1] / jnp.sum(affinity, 1, keepdims=True)


def forward_kernel(
    experts,
    place_ref,
    same_ref,
    cross_ref,
    block_ref,
    hidden_ref,
    gain_ref,
    route_ref,
    affinity_ref,
    cotangent_ref,
    attended_ref,
    log_ref,
    send_ref,
    query_ref,
):
    rows = block_ref.shape[0]
    place = place_ref[0]
    pair, core = place // 2, place % 2
    for head in range(2):
        query_ref[head] = own_query(block_ref[...], head)

    def load(pair_index, columns):
        at = pl.multiple_of(pair_index * rows, rows)
        return jnp.concatenate(
            [same_ref[pl.ds(at, rows), columns], cross_ref[pl.ds(at, rows), columns]], 0
        )

    keys = load(pair, KEY)
    vals = load(pair, VALUE)
    visible = pair_places(rows, core) <= lax.broadcasted_iota(jnp.int32, (rows, 2 * rows), 0)
    state = []
    for head in range(2):
        scores = jnp.where(visible, nt_dot(query_ref[head], keys) * score_scale, masked_low)
        top = jnp.max(scores, 1, keepdims=True)
        weights = jnp.where(visible, jnp.exp(scores - top), 0.0)
        total = jnp.sum(weights, 1, keepdims=True)
        state.extend([top, total, nn_dot(weights.astype(bf16), vals)])

    def step(index, state):
        keys = load(index, KEY)
        vals = load(index, VALUE)
        after = []
        for head in range(2):
            top, total, mixed = state[3 * head : 3 * head + 3]
            scores = nt_dot(query_ref[head], keys) * score_scale
            new_top = jnp.maximum(top, jnp.max(scores, 1, keepdims=True))
            weights = jnp.exp(scores - new_top)
            factor = jnp.exp(top - new_top)
            total = total * factor + jnp.sum(weights, 1, keepdims=True)
            mixed = mixed * factor + nn_dot(weights.astype(bf16), vals)
            after.extend([new_top, total, mixed])
        return tuple(after)

    state = lax.fori_loop(0, pair, step, tuple(state))
    first = lanes_of((rows, LANES)) < VDIM
    attended = jnp.where(first, state[2] / state[1], state[5] / state[4]).astype(bf16)
    attended_ref[...] = attended
    log_ref[...] = jnp.where(
        first, state[0] + jnp.log(state[1]), state[3] + jnp.log(state[4])
    )
    hidden = hidden_ref[...].astype(f32) + attended.astype(f32)
    raised = (hidden * gain_ref[...]).astype(bf16)
    share = gate_share_of(affinity_ref[...])
    grad = (share * cotangent_ref[...].astype(f32)).astype(bf16)
    slots = slots_along_rows(route_ref[...], experts)
    table = lax.broadcasted_iota(jnp.int32, (experts * SLOT, rows), 0) == slots
    table = table.astype(f32).astype(bf16)
    row = lax.broadcasted_iota(jnp.int32, (SLOT, LANES), 0)
    gains = jnp.zeros((SLOT, LANES), f32)
    for index, piece in enumerate(pieces_of(gain_ref[...], 3)):
        gains = jnp.where(row == CAP + index, piece, gains)
    gains = jnp.broadcast_to(gains[None], (experts, SLOT, LANES)).reshape(-1, LANES)
    send_ref[:, 0:LANES] = (nn_dot(table, raised) + gains).astype(bf16)
    send_ref[:, LANES:] = nn_dot(table, grad).astype(bf16)


def gathered_rows(ref, count, slices, column):
    parts = []
    for index in range(slices):
        part = ref[:, index * SLOT : (index + 1) * SLOT, column : column + LANES]
        parts.append(part.reshape(count * SLOT, LANES))
    return jnp.concatenate(parts, 1)


def gain_of(raised):
    pieces = raised[CAP : CAP + 3].astype(f32)
    return pieces[0:1] + pieces[1:2] + pieces[2:3]


def inverse_of(raised, gain):
    hidden = raised.astype(f32) / gain
    return lax.rsqrt(jnp.sum(hidden * hidden, 1, keepdims=True) / D + norm_eps)


def expert_kernel(
    rows_ref,
    gate_own_ref,
    up_own_ref,
    down_own_ref,
    gate_other_ref,
    up_other_ref,
    down_other_ref,
    out_ref,
):
    count, depth, _ = rows_ref.shape
    slices = depth // SLOT
    raised = gathered_rows(rows_ref, count, slices, 0)
    grad = gathered_rows(rows_ref, count, slices, LANES)
    inverse = inverse_of(raised, gain_of(raised[0:SLOT]))
    pairs = (
        (gate_own_ref, up_own_ref, down_own_ref),
        (gate_other_ref, up_other_ref, down_other_ref),
    )
    made = []
    for gate_ref, up_ref, down_ref in pairs:
        gate_val = inverse * nn_dot(raised, gate_ref[...])
        up_val = inverse * nn_dot(raised, up_ref[...])
        grad_active = nt_dot(grad, down_ref[...])
        sig = 1.0 / (1.0 + jnp.exp(-gate_val))
        silu = gate_val * sig
        active = (silu * up_val).astype(bf16)
        grad_gate = (grad_active * up_val * (sig * (1.0 + gate_val * (1.0 - sig)))).astype(bf16)
        grad_up = (grad_active * silu).astype(bf16)
        made.append((active, grad_gate, grad_up))
    for index in range(slices):
        at = slice(index * LANES, (index + 1) * LANES)
        out = jnp.zeros((count * SLOT, LANES), f32)
        back = jnp.zeros((count * SLOT, LANES), f32)
        for (gate_ref, up_ref, down_ref), (active, grad_gate, grad_up) in zip(pairs, made):
            out = out + nn_dot(active, down_ref[:, at])
            back = back + nt_dot(grad_gate, gate_ref[at, :]) + nt_dot(grad_up, up_ref[at, :])
        span = slice(index * SLOT, (index + 1) * SLOT)
        out_ref[:, span, 0:LANES] = out.astype(bf16).reshape(count, SLOT, LANES)
        out_ref[:, span, LANES:] = back.astype(bf16).reshape(count, SLOT, LANES)


def reduce_kernel(terms_ref, rows_ref, out_ref):
    count, depth, _ = terms_ref.shape
    slices = depth // SLOT
    total = terms_ref[0].astype(f32)
    for index in range(1, count):
        total = total + terms_ref[index].astype(f32)
    raised = rows_ref[:, 0:LANES].astype(f32).reshape(slices, SLOT, LANES)
    back = total[:, LANES:].reshape(slices, SLOT, LANES)
    gain = jnp.sum(raised[:, CAP : CAP + 3, :], 1, keepdims=True)
    hidden = raised / gain
    squares = jnp.sum(jnp.sum(hidden * hidden, 0), 1, keepdims=True)
    inverse = lax.rsqrt(squares / D + norm_eps)
    cross = jnp.sum(jnp.sum(back * raised, 0), 1, keepdims=True) / D
    grad = inverse[None] * (back * gain - hidden * (inverse * inverse * cross)[None])
    row = lax.broadcasted_iota(jnp.int32, (slices, SLOT, LANES), 1)
    grad = jnp.where(row < CAP, grad, 0.0)
    out_ref[:, 0:LANES] = total[:, 0:LANES].astype(bf16)
    out_ref[:, LANES:] = grad.astype(bf16).reshape(depth, LANES)


def combine_kernel(
    experts,
    home_ref,
    hidden_ref,
    attended_ref,
    log_ref,
    route_ref,
    affinity_ref,
    cotangent_ref,
    layer_ref,
    grad_ref,
    stats_ref,
):
    rows = hidden_ref.shape[0]
    slots = slots_along_columns(route_ref[...], experts)
    table = (lanes_of((rows, experts * SLOT)) == slots).astype(f32).astype(bf16)
    token = nn_dot(table, home_ref[...])
    attended = attended_ref[...].astype(f32)
    hidden = hidden_ref[...].astype(f32) + attended
    share = gate_share_of(affinity_ref[...])
    layer_ref[...] = (hidden + share * token[:, 0:LANES]).astype(bf16)
    grad = (cotangent_ref[...].astype(f32) + token[:, LANES:]).astype(bf16)
    grad_ref[...] = grad
    product = grad.astype(f32) * attended
    lane = lanes_of((rows, LANES))
    columns = []
    for head in range(2):
        dot = jnp.sum(jnp.where(lane // VDIM == head, product, 0.0), 1, keepdims=True)
        columns += pieces_of(dot, 3)
        columns += pieces_of(log_ref[:, head * VDIM : head * VDIM + 1], 3)
    stats = jnp.zeros((rows, LANES), f32)
    for index, column in enumerate(columns):
        stats = jnp.where(lane == index, column, stats)
    stats_ref[:, 0:LANES] = grad
    stats_ref[:, LANES:] = stats.astype(bf16)


def backward_kernel(
    place_ref,
    same_ref,
    cross_ref,
    grad_same_ref,
    grad_cross_ref,
    block_ref,
    stats_ref,
    query_nope_ref,
    query_rope_ref,
    key_nope_ref,
    values_ref,
    rope_ref,
    query_ref,
    key_ref,
    grads_ref,
    vals_ref,
    dq_ref,
    dk_ref,
    dv_ref,
):
    rows = block_ref.shape[0]
    place = place_ref[0]
    pair, core = place // 2, place % 2
    lane = lanes_of((rows, LANES))
    zero = jnp.zeros((rows, LANES), bf16)
    one = jnp.ones((rows, LANES), f32)
    logs, ones_log = [], []
    for head in range(2):
        base = 6 * head
        query_ref[head] = own_query(block_ref[...], head)
        key_ref[head] = own_key(block_ref[...], head)
        minus = jnp.where((lane >= base) & (lane < base + 3), -one, 0.0).astype(bf16)
        of_log = jnp.where((lane >= base + 3) & (lane < base + 6), one, 0.0).astype(bf16)
        ones_log.append(of_log)
        mine = lane // VDIM == head
        stats = stats_ref[:, LANES:].astype(f32)
        own = jnp.where(mine, stats_ref[:, 0:LANES], zero)
        value = jnp.where(mine, block_ref[:, VALUE], zero)
        grads_ref[head] = own
        vals_ref[head] = jnp.concatenate([value, minus], 1)
        dot = jnp.sum(jnp.where((lane >= base) & (lane < base + 3), stats, 0.0), 1, keepdims=True)
        log = jnp.sum(
            jnp.where((lane >= base + 3) & (lane < base + 6), stats, 0.0), 1, keepdims=True
        )
        logs.append((log, dot))
    dq_ref[...] = jnp.zeros_like(dq_ref)
    dk_ref[...] = jnp.zeros_like(dk_ref)
    dv_ref[...] = jnp.zeros_like(dv_ref)

    def load(first, second, pair_index, columns):
        at = pl.multiple_of(pair_index * rows, rows)
        return jnp.concatenate(
            [first[pl.ds(at, rows), columns], second[pl.ds(at, rows), columns]], 0
        )

    def query_side(index, visible):
        keys = load(same_ref, cross_ref, index, KEY)
        vals = load(same_ref, cross_ref, index, VALUE)
        for head in range(2):
            log, dot = logs[head]
            prob = jnp.exp(nt_dot(query_ref[head], keys) * score_scale - log)
            if visible is not None:
                prob = jnp.where(visible, prob, 0.0)
            grad_prob = nt_dot(grads_ref[head], vals)
            grad_score = (prob * (grad_prob - dot)).astype(bf16)
            dq_ref[head] += nn_dot(grad_score, keys)

    def key_side(index, visible):
        queries = load(same_ref, cross_ref, index, QUERY)
        grads = load(grad_same_ref, grad_cross_ref, index, slice(0, 2 * LANES))
        for head in range(2):
            log = nt_dot(ones_log[head], grads[:, LANES:])
            prob = jnp.exp(nt_dot(key_ref[head], queries) * score_scale - log)
            if visible is not None:
                prob = jnp.where(visible, prob, 0.0)
            dv_ref[head] += nn_dot(prob.astype(bf16), grads[:, 0:LANES])
            grad_prob = nt_dot(vals_ref[head], grads)
            grad_score = (prob * grad_prob).astype(bf16)
            dk_ref[head] += nn_dot(grad_score, queries)

    places = pair_places(rows, core)
    line = lax.broadcasted_iota(jnp.int32, (rows, 2 * rows), 0)
    query_side(pair, places <= line)
    key_side(pair, places >= line)

    def query_step(index, carry):
        query_side(index, None)
        return carry

    def key_step(index, carry):
        key_side(index, None)
        return carry

    lax.fori_loop(0, pair, query_step, 0)
    lax.fori_loop(pair + 1, same_ref.shape[0] // rows, key_step, 0)

    first = lane < NOPE
    query_nope_ref[...] = (
        score_scale * jnp.where(first, dq_ref[0, :, 0:LANES], dq_ref[1, :, 0:LANES])
    ).astype(bf16)
    rot = jnp.where(
        lane < ROPE, dq_ref[0, :, LANES:], pltpu.roll(dq_ref[1, :, LANES:], ROPE, 1)
    )
    query_rope_ref[...] = (score_scale * rot).astype(bf16)[:, 0 : 2 * ROPE]
    key_nope_ref[...] = (
        score_scale * jnp.where(first, dk_ref[0, :, LANES:], dk_ref[1, :, LANES:])
    ).astype(bf16)
    values_ref[...] = jnp.where(lane < VDIM, dv_ref[0], dv_ref[1]).astype(bf16)
    shared = pltpu.roll(dk_ref[0, :, 0:LANES], LANES - ROPE, 1) + pltpu.roll(
        dk_ref[1, :, 0:LANES], LANES - 2 * ROPE, 1
    )
    quarter = rows // 4
    packed = jnp.zeros((quarter, LANES), f32)
    small = lanes_of((quarter, LANES))
    for index in range(4):
        part = shared[index * quarter : (index + 1) * quarter]
        if index:
            part = pltpu.roll(part, index * ROPE, 1)
        packed = jnp.where(small // ROPE == index, part, packed)
    rope_ref[...] = (score_scale * packed).astype(bf16)


def rope_kernel(terms_ref, out_ref):
    total = terms_ref[0].astype(f32)
    for index in range(1, terms_ref.shape[0]):
        total = total + terms_ref[index].astype(f32)
    quarter = total.shape[0]
    for index in range(4):
        part = total if index == 0 else pltpu.roll(total, LANES - index * ROPE, 1)
        out_ref[index * quarter : (index + 1) * quarter, :] = part[:, 0:ROPE].astype(bf16)


def call(body, outs, scratch=(), scalars=0, count=0):
    place = [pl.BlockSpec(memory_space=pltpu.SMEM)] * scalars
    return pl.pallas_call(
        body,
        out_shape=outs,
        in_specs=place + [pl.BlockSpec(memory_space=pltpu.VMEM)] * count,
        out_specs=jax.tree.map(lambda _: pl.BlockSpec(memory_space=pltpu.VMEM), outs),
        scratch_shapes=list(scratch),
        compiler_params=pltpu.CompilerParams(vmem_limit_bytes=VMEM_LIMIT),
    )


def shape_of(*dims, dtype=bf16):
    return jax.ShapeDtypeStruct(dims, dtype)


def exchange(blocks, axis, groups=None):
    return lax.all_to_all(blocks, axis, 0, 0, tiled=True, axis_index_groups=groups)


def per_device(
    hidden_in,
    query_nope,
    query_rope,
    key_nope,
    key_rope,
    values,
    norm_gain,
    expert_route,
    affinity,
    gate_weight,
    up_weight,
    down_weight,
    cotangent,
):
    rows, width = hidden_in.shape
    ctx_count, experts = lax.axis_size("ctx"), lax.axis_size("exp")
    half = ctx_count // 2
    groups = [[core + 2 * index for index in range(half)] for core in range(2)]
    across = [(index, index ^ 1) for index in range(ctx_count)]
    depth = experts * SLOT

    def swap(value):
        return lax.ppermute(value, "ctx", across)

    def spread(block):
        copies = jnp.broadcast_to(block[None], (half,) + block.shape)
        return exchange(copies, "ctx", groups)

    place = lax.axis_index("ctx").astype(jnp.int32).reshape(1)
    mine = (gate_weight[0], up_weight[0], down_weight[0])
    others = [swap(weight) for weight in mine]
    block = jnp.concatenate(
        [key_nope, key_rope, query_rope, jnp.zeros((rows, ROPE), bf16), query_nope, values], 1
    )
    same = spread(block).reshape(half * rows, -1)
    cross = swap(same)
    gain_row = norm_gain.reshape(1, width)

    attended, logs, send = call(
        functools.partial(forward_kernel, experts),
        (shape_of(rows, width), shape_of(rows, width, dtype=f32), shape_of(depth, 2 * width)),
        [pltpu.VMEM((2, rows, 2 * width), bf16)],
        1,
        8,
    )(
        place,
        same,
        cross,
        block,
        hidden_in,
        gain_row,
        expert_route.reshape(1, rows),
        affinity,
        cotangent,
    )
    received = exchange(send.reshape(experts, SLOT, 2 * width), "exp").reshape(depth, 2 * width)
    rows_all = spread(received)
    partial = call(expert_kernel, shape_of(half, depth, 2 * width), count=7)(
        rows_all, *mine, *others
    )
    terms = exchange(partial, "ctx", groups)
    back = call(reduce_kernel, shape_of(depth, 2 * width), count=2)(terms, received)
    home = exchange(back.reshape(experts, SLOT, 2 * width), "exp").reshape(depth, 2 * width)
    layer_out, grad_hidden, stats = call(
        functools.partial(combine_kernel, experts),
        (shape_of(rows, width), shape_of(rows, width), shape_of(rows, 2 * width)),
        count=7,
    )(home, hidden_in, attended, logs, expert_route.reshape(rows, 1), affinity, cotangent)
    grad_same = spread(stats).reshape(half * rows, -1)
    grad_cross = swap(grad_same)
    quarter = rows // 4
    gq_nope, gq_rope, gk_nope, g_values, rope_part = call(
        backward_kernel,
        (
            shape_of(rows, width),
            shape_of(rows, 2 * ROPE),
            shape_of(rows, width),
            shape_of(rows, width),
            shape_of(quarter, LANES),
        ),
        [
            pltpu.VMEM((2, rows, 2 * width), bf16),
            pltpu.VMEM((2, rows, 2 * width), bf16),
            pltpu.VMEM((2, rows, width), bf16),
            pltpu.VMEM((2, rows, 2 * width), bf16),
            pltpu.VMEM((2, rows, 2 * width), f32),
            pltpu.VMEM((2, rows, 2 * width), f32),
            pltpu.VMEM((2, rows, width), f32),
        ],
        1,
        6,
    )(place, same, cross, grad_same, grad_cross, block, stats)
    rope_terms = exchange(jnp.broadcast_to(rope_part[None], (experts, quarter, LANES)), "exp")
    gk_rope = call(rope_kernel, shape_of(rows, ROPE), count=1)(rope_terms)
    return (layer_out, grad_hidden, gq_nope, gq_rope, gk_nope, gk_rope, g_values)


def solution(mesh):
    placed = (
        P("ctx", "exp"),
        P("ctx", "exp"),
        P("ctx", "exp"),
        P("ctx", "exp"),
        P("ctx", None),
        P("ctx", "exp"),
        P("exp"),
        P("ctx"),
        P("ctx", None),
        P("exp", None, "ctx"),
        P("exp", None, "ctx"),
        P("exp", "ctx", None),
        P("ctx", "exp"),
    )
    return jax.shard_map(
        per_device,
        mesh=mesh,
        in_specs=placed,
        out_specs=(
            P("ctx", "exp"),
            P("ctx", "exp"),
            P("ctx", "exp"),
            P("ctx", "exp"),
            P("ctx", "exp"),
            P("ctx", None),
            P("ctx", "exp"),
        ),
        check_vma=False,
    )
```

time: 943 us -> 266 us (0.28)
  the two profiles are of different devices: /device:TPU:8 before, /device:TPU:1 now
where the time goes in v1:
time: 266 us; the launch traced here: 265 us
  blocking collectives  105 us (39%)
  waiting for transfers between devices  62.5 us (23%)
  starting transfers between devices  44.9 us (17%)
  Pallas kernels  33.6 us (13%)
  local copies, waits for them, and re-layouts  17.8 us (7%)
    all_to_all x4, blocking collectives, exchange(): lax.all_to_all(blocks, axis, 0, 0, tiled=True, axis_index_groups=groups)  105 us
    all_to_all x3, waiting for transfers between devices, exchange(): lax.all_to_all(blocks, axis, 0, 0, tiled=True, axis_index_groups=groups)  57.5 us
    ppermute x5, starting transfers between devices, swap(): return lax.ppermute(value, 'ctx', across)  23.6 us
    all_to_all x3, starting transfers between devices, exchange(): lax.all_to_all(blocks, axis, 0, 0, tiled=True, axis_index_groups=groups)  21.4 us
    pallas_call x1, Pallas kernels, per_device(): call(backward_kernel, (shape_of(rows, width), shape_of(rows, 2 * ROPE), s...  12.5 us
    unnamed x33, local copies, waits for them, and re-layouts  12 us
    pallas_call x1, Pallas kernels, per_device(): call(expert_kernel, shape_of(half, depth, 2 * width), count=7)  10 us
  transfers between devices with their start and end apart: 8, of which 7 were waited for; matrix products, arithmetic and copies ran while one was open for 1% of the time, Pallas kernels for 0%

profile of v1, /device:TPU:1, one launch (start us, length us, event | category | flops | bytes accessed | tf_op | source)
XLA Modules:
  0.0 264.9 jit_solution(13071012661462088854)
XLA Ops:
  2.4 1.0 concatenate.3.block_ref
  3.5 27.0 %all_to_all.35 = bf16[8,192,512]{2,1,0:T(8,128)(2,1)S(1)} all-to-all(bf16[8,192,512]{2,1,0:T(8,128)(2,1)S(1)} %broadcast_in_dim.13), channel_id=1, replica_groups={{0,64,128,192,256,320,384,448},{32,96,160,224,288,352,416,480},{1,65,12..., dimensions={0} | all-to-all | bytes 3145728 | tf_op jit(solution)/shard_map/all_to_all | solution.py:447
  30.5 5.6 %collective-permute-start = (bf16[1536,512]{1,0:T(8,128)(2,1)S(1)}, bf16[1536,512]{1,0:T(8,128)(2,1)S(1)}, u32[]{:S(2)}, u32[]{:S(2)}) collective-permute-start(bf16[1536,512]{1,0:T(8,128)(2,1)S(1)} %bitcast.13), channel_id=1, source_target_pairs={{0,32},{32,0},{64,96},{96,64},{128,160},{160,128},{192,224},{224,1... | collective-permute-start | bytes 4718600 | tf_op jit(solution)/shard_map/ppermute | solution.py:473
  36.9 2.2 collective-permute-done.cross_ref
  39.1 1.1 copy-done.2
  40.3 3.9 %shard_map.180 = (bf16[192,128]{1,0:T(8,128)(2,1)}, f32[192,128]{1,0:T(8,128)}, bf16[512,256]{1,0:T(8,128)(2,1)}) custom-call(s32[1]{0:T(128)} %bitcast.place_ref, bf16[1536,512]{1,0:T(8,128)(2,1)} %bitcast.14, bf16[1536,512]{1,0:T(8,128)(2,1)} %copy-done.2, bf16[192,512]{1,0:T(8,128)(2,1)} %copy-done.4, bf16[192,128]{1,0:T(8,128)(2,1)} %hidden_ref.3, ...), custom_call_target="tpu_custom_call" | custom-call | tf_op jit(solution)/shard_map/pallas_call | solution.py:489
  44.2 35.7 %all_to_all.36 = bf16[32,16,256]{2,1,0:T(8,128)(2,1)S(1)} all-to-all(bf16[32,16,256]{2,1,0:T(8,128)(2,1)} %bitcast.28), channel_id=1, replica_groups=mesh['ctx'=16,'exp'=32] {'exp'}, dimensions={0} | all-to-all | bytes 524288 | tf_op jit(solution)/shard_map/all_to_all | solution.py:447
  79.9 1.5 broadcast_in_dim.15
  81.3 9.4 %all-to-all-start.2 = ((bf16[8,512,256]{2,1,0:T(8,128)(2,1)}), bf16[8,512,256]{2,1,0:T(8,128)(2,1)S(1)}, u32[]{:S(2)}, u32[]{:S(2)}) async-start(bf16[8,512,256]{2,1,0:T(8,128)(2,1)} %broadcast_in_dim.15), calls=%async_computation.2 | async-start | bytes 4194304 | tf_op jit(solution)/shard_map/all_to_all | solution.py:447
  90.8 4.9 %collective-permute-start.1 = (bf16[4096,128]{1,0:T(8,128)(2,1)S(1)}, bf16[4096,128]{1,0:T(8,128)(2,1)S(1)}, u32[]{:S(2)}, u32[]{:S(2)}) collective-permute-start(bf16[4096,128]{1,0:T(8,128)(2,1)S(1)} %bitcast.21), channel_id=1, source_target_pairs={{0,32},{32,0},{64,96},{96,64},{128,160},{160,128},{192,224},{224,1... | collective-permute-start | bytes 3145736 | tf_op jit(solution)/shard_map/ppermute | solution.py:473
  95.7 1.9 collective-permute-start.2
  97.6 2.4 collective-permute-start.3
  101.2 1.1 copy-done.9
  102.7 16.4 %all-to-all-done.2.rows_ref = bf16[8,512,256]{2,1,0:T(8,128)(2,1)S(1)} async-done(((bf16[8,512,256]{2,1,0:T(8,128)(2,1)}), bf16[8,512,256]{2,1,0:T(8,128)(2,1)S(1)}, u32[]{:S(2)}, u32[]{:S(2)}) %all-to-all-start.2) | async-done | bytes 2097184 | tf_op jit(solution)/shard_map/all_to_all | solution.py:447
  119.1 1.3 copy-done.1
  120.4 10.0 %shard_map.181 = bf16[8,512,256]{2,1,0:T(8,128)(2,1)} custom-call(bf16[8,512,256]{2,1,0:T(8,128)(2,1)} %copy-done.1, bf16[4096,128]{1,0:T(8,128)(2,1)} %bitcast.20, bf16[4096,128]{1,0:T(8,128)(2,1)} %bitcast.23, bf16[128,4096]{1,0:T(8,128)(2,1)} %bitcast.25, bf16[4096,128]{1,0:T(8,128)(2,1)} %copy-done.8, bf16[4096,128]{1,0:T(8,128)(2,1)} %copy-done.9, ...), custom_call_target="tpu_custom_call" | custom-call | tf_op jit(solution)/shard_map/pallas_call | solution.py:508
  130.4 29.2 %all_to_all.37.terms_ref = bf16[8,512,256]{2,1,0:T(8,128)(2,1)} all-to-all(bf16[8,512,256]{2,1,0:T(8,128)(2,1)} %shard_map.181), channel_id=1, replica_groups={{0,64,128,192,256,320,384,448},{32,96,160,224,288,352,416,480},{1,65,12..., dimensions={0} | all-to-all | bytes 4194304 | tf_op jit(solution)/shard_map/all_to_all | solution.py:447
  159.5 2.9 %shard_map.182 = bf16[512,256]{1,0:T(8,128)(2,1)} custom-call(bf16[8,512,256]{2,1,0:T(8,128)(2,1)} %all_to_all.37.terms_ref, bf16[512,256]{1,0:T(8,128)(2,1)} %bitcast.19), custom_call_target="tpu_custom_call" | custom-call | tf_op jit(solution)/shard_map/pallas_call | solution.py:512
  162.4 8.1 %all-to-all-start.4 = ((bf16[32,16,256]{2,1,0:T(8,128)(2,1)}), bf16[32,16,256]{2,1,0:T(8,128)(2,1)S(1)}, u32[]{:S(2)}, u32[]{:S(2)}) async-start(bf16[32,16,256]{2,1,0:T(8,128)(2,1)} %bitcast.26), calls=%async_computation.4 | async-start | bytes 524288 | tf_op jit(solution)/shard_map/all_to_all | solution.py:447
  171.2 16.7 %all-to-all-done.4 = bf16[32,16,256]{2,1,0:T(8,128)(2,1)S(1)} async-done(((bf16[32,16,256]{2,1,0:T(8,128)(2,1)}), bf16[32,16,256]{2,1,0:T(8,128)(2,1)S(1)}, u32[]{:S(2)}, u32[]{:S(2)}) %all-to-all-start.4) | async-done | bytes 262176 | tf_op jit(solution)/shard_map/all_to_all | solution.py:447
  188.6 2.5 shard_map.183
  191.1 0.9 broadcast_in_dim.32
  192.0 13.4 %all_to_all.38 = bf16[8,192,256]{2,1,0:T(8,128)(2,1)S(1)} all-to-all(bf16[8,192,256]{2,1,0:T(8,128)(2,1)S(1)} %broadcast_in_dim.32), channel_id=1, replica_groups={{0,64,128,192,256,320,384,448},{32,96,160,224,288,352,416,480},{1,65,12..., dimensions={0} | all-to-all | bytes 1572864 | tf_op jit(solution)/shard_map/all_to_all | solution.py:447
  205.4 8.7 %collective-permute-start.4 = (bf16[1536,256]{1,0:T(8,128)(2,1)S(1)}, bf16[1536,256]{1,0:T(8,128)(2,1)S(1)}, u32[]{:S(2)}, u32[]{:S(2)}) collective-permute-start(bf16[1536,256]{1,0:T(8,128)(2,1)S(1)} %bitcast.16), channel_id=1, source_target_pairs={{0,32},{32,0},{64,96},{96,64},{128,160},{160,128},{192,224},{224,1... | collective-permute-start | bytes 2359304 | tf_op jit(solution)/shard_map/ppermute | solution.py:473
  214.2 1.9 collective-permute-done.4.grad_cross_ref
  217.0 12.5 %shard_map.184 = (bf16[192,128]{1,0:T(8,128)(2,1)}, bf16[192,64]{1,0:T(8,128)(2,1)}, bf16[192,128]{1,0:T(8,128)(2,1)}, bf16[192,128]{1,0:T(8,128)(2,1)}, bf16[48,128]{1,0:T(8,128)(2,1)}) custom-call(s32[1]{0:T(128)} %bitcast.place_ref, bf16[1536,512]{1,0:T(8,128)(2,1)} %bitcast.15, bf16[1536,512]{1,0:T(8,128)(2,1)} %copy-done.2, bf16[1536,256]{1,0:T(8,128)(2,1)} %bitcast.17, ...), custom_call_target="tpu_custom_call" | custom-call | tf_op jit(solution)/shard_map/pallas_call | solution.py:522
  229.5 1.5 broadcast_in_dim.33
  231.0 3.9 %all-to-all-start.6 = ((bf16[32,48,128]{2,1,0:T(8,128)(2,1)}), bf16[32,48,128]{2,1,0:T(8,128)(2,1)S(1)}, u32[]{:S(2)}, u32[]{:S(2)}) async-start(bf16[32,48,128]{2,1,0:T(8,128)(2,1)} %broadcast_in_dim.33), calls=%async_computation.6 | async-start | bytes 786432 | tf_op jit(solution)/shard_map/all_to_all | solution.py:447
  234.9 1.5 copy.31
  236.4 24.5 %all-to-all-done.6.terms_ref = bf16[32,48,128]{2,1,0:T(8,128)(2,1)S(1)} async-done(((bf16[32,48,128]{2,1,0:T(8,128)(2,1)}), bf16[32,48,128]{2,1,0:T(8,128)(2,1)S(1)}, u32[]{:S(2)}, u32[]{:S(2)}) %all-to-all-start.6) | async-done | bytes 393248 | tf_op jit(solution)/shard_map/all_to_all | solution.py:447
  261.6 1.8 shard_map.185
  263.4 1.5 copy.32
  (34 shorter events, 7.3 us)
Async XLA Ops:
  3.3 27.2 %copy-start.4 = (bf16[192,512]{1,0:T(8,128)(2,1)}, bf16[192,512]{1,0:T(8,128)(2,1)S(1)}, u32[]{:S(2)}) copy-start(bf16[192,512]{1,0:T(8,128)(2,1)S(1)} %concatenate.3.block_ref) | copy-start | bytes 589828
  3.3 32.8 %copy-start.12 = (f32[192,8]{0,1:T(8,128)S(1)}, f32[192,8]{0,1:T(8,128)}, u32[]{:S(2)}) copy-start(f32[192,8]{0,1:T(8,128)} %param.21) | copy-start | bytes 18436
  30.5 8.6 %copy-start = (bf16[8,192,512]{2,1,0:T(8,128)(2,1)}, bf16[8,192,512]{2,1,0:T(8,128)(2,1)S(1)}, u32[]{:S(2)}) copy-start(bf16[8,192,512]{2,1,0:T(8,128)(2,1)S(1)} %all_to_all.35) | copy-start | bytes 4718596
  30.5 8.6 %collective-permute-start = (bf16[1536,512]{1,0:T(8,128)(2,1)S(1)}, bf16[1536,512]{1,0:T(8,128)(2,1)S(1)}, u32[]{:S(2)}, u32[]{:S(2)}) collective-permute-start(bf16[1536,512]{1,0:T(8,128)(2,1)S(1)} %bitcast.13), channel_id=1, source_target_pairs={{0,32},{32,0},{64,96},{96,64},{128,160},{160,128},{192,224},{224,1... | collective-permute-start | bytes 4718600 | tf_op jit(solution)/shard_map/ppermute | solution.py:473
  39.1 1.1 copy-start.2
  79.9 1.5 copy-start.5
  81.3 9.4 %copy-start.7 = (bf16[1,4096,128]{2,1,0:T(8,128)(2,1)S(1)}, bf16[1,4096,128]{2,1,0:T(8,128)(2,1)}, u32[]{:S(2)}) copy-start(bf16[1,4096,128]{2,1,0:T(8,128)(2,1)} %param.22) | copy-start | bytes 3145732
  81.3 37.7 %all-to-all-start.2 = ((bf16[8,512,256]{2,1,0:T(8,128)(2,1)}), bf16[8,512,256]{2,1,0:T(8,128)(2,1)S(1)}, u32[]{:S(2)}, u32[]{:S(2)}) async-start(bf16[8,512,256]{2,1,0:T(8,128)(2,1)} %broadcast_in_dim.15), calls=%async_computation.2 | async-start | bytes 4194304 | tf_op jit(solution)/shard_map/all_to_all | solution.py:447
  90.8 9.3 %collective-permute-start.1 = (bf16[4096,128]{1,0:T(8,128)(2,1)S(1)}, bf16[4096,128]{1,0:T(8,128)(2,1)S(1)}, u32[]{:S(2)}, u32[]{:S(2)}) collective-permute-start(bf16[4096,128]{1,0:T(8,128)(2,1)S(1)} %bitcast.21), channel_id=1, source_target_pairs={{0,32},{32,0},{64,96},{96,64},{128,160},{160,128},{192,224},{224,1... | collective-permute-start | bytes 3145736 | tf_op jit(solution)/shard_map/ppermute | solution.py:473
  95.7 4.8 %collective-permute-start.2 = (bf16[4096,128]{1,0:T(8,128)(2,1)}, bf16[4096,128]{1,0:T(8,128)(2,1)S(1)}, u32[]{:S(2)}, u32[]{:S(2)}) collective-permute-start(bf16[4096,128]{1,0:T(8,128)(2,1)} %bitcast.22), channel_id=1, source_target_pairs={{0,32},{32,0},{64,96},{96,64},{128,160},{160,128},{192,224},{224,1... | collective-permute-start | bytes 3145736 | tf_op jit(solution)/shard_map/ppermute | solution.py:473
  97.6 5.0 %collective-permute-start.3 = (bf16[128,4096]{1,0:T(8,128)(2,1)}, bf16[128,4096]{1,0:T(8,128)(2,1)}, u32[]{:S(2)}, u32[]{:S(2)}) collective-permute-start(bf16[128,4096]{1,0:T(8,128)(2,1)} %bitcast.24), channel_id=1, source_target_pairs={{0,32},{32,0},{64,96},{96,64},{128,160},{160,128},{192,224},{224,1... | collective-permute-start | bytes 3145736 | tf_op jit(solution)/shard_map/ppermute | solution.py:473
  100.1 1.1 copy-start.8
  101.1 1.1 copy-start.9
  119.1 1.3 copy-start.1
  159.5 10.9 %copy-start.13 = (s32[192]{0:T(256)S(1)}, s32[192]{0:T(256)}, u32[]{:S(2)}) copy-start(s32[192]{0:T(256)} %param.20) | copy-start | bytes 2308
  162.4 25.5 %all-to-all-start.4 = ((bf16[32,16,256]{2,1,0:T(8,128)(2,1)}), bf16[32,16,256]{2,1,0:T(8,128)(2,1)S(1)}, u32[]{:S(2)}, u32[]{:S(2)}) async-start(bf16[32,16,256]{2,1,0:T(8,128)(2,1)} %bitcast.26), calls=%async_computation.4 | async-start | bytes 524288 | tf_op jit(solution)/shard_map/all_to_all | solution.py:447
  187.9 0.7 copy-start.10
  205.4 10.6 %copy-start.3 = (bf16[8,192,256]{2,1,0:T(8,128)(2,1)}, bf16[8,192,256]{2,1,0:T(8,128)(2,1)S(1)}, u32[]{:S(2)}) copy-start(bf16[8,192,256]{2,1,0:T(8,128)(2,1)S(1)} %all_to_all.38) | copy-start | bytes 2359300
  205.4 10.6 %collective-permute-start.4 = (bf16[1536,256]{1,0:T(8,128)(2,1)S(1)}, bf16[1536,256]{1,0:T(8,128)(2,1)S(1)}, u32[]{:S(2)}, u32[]{:S(2)}) collective-permute-start(bf16[1536,256]{1,0:T(8,128)(2,1)S(1)} %bitcast.16), channel_id=1, source_target_pairs={{0,32},{32,0},{64,96},{96,64},{128,160},{160,128},{192,224},{224,1... | collective-permute-start | bytes 2359304 | tf_op jit(solution)/shard_map/ppermute | solution.py:473
  216.1 0.9 copy-start.11
  231.0 29.8 %all-to-all-start.6 = ((bf16[32,48,128]{2,1,0:T(8,128)(2,1)}), bf16[32,48,128]{2,1,0:T(8,128)(2,1)S(1)}, u32[]{:S(2)}, u32[]{:S(2)}) async-start(bf16[32,48,128]{2,1,0:T(8,128)(2,1)} %broadcast_in_dim.33), calls=%async_computation.6 | async-start | bytes 786432 | tf_op jit(solution)/shard_map/all_to_all | solution.py:447
  260.9 0.7 copy-start.6

commit v2 on v1

--- a/solution.py
+++ b/solution.py
@@ -23,7 +23,7 @@
 
 bf16 = jnp.bfloat16
 f32 = jnp.float32
-VMEM_LIMIT = 56 * 1024 * 1024
+MIB = 1024 * 1024
 
 KEY = slice(0, 256)
 QUERY = slice(128, 384)
@@ -195,46 +195,57 @@
     return lax.rsqrt(jnp.sum(hidden * hidden, 1, keepdims=True) / D + norm_eps)
 
 
-def expert_kernel(
-    rows_ref,
-    gate_own_ref,
-    up_own_ref,
-    down_own_ref,
-    gate_other_ref,
-    up_other_ref,
-    down_other_ref,
-    out_ref,
-):
+def expert_kernel(rows_ref, *refs):
+    weight_refs, out_ref = refs[:-1], refs[-1]
     count, depth, _ = rows_ref.shape
     slices = depth // SLOT
+    wide = 2 * LANES
     raised = gathered_rows(rows_ref, count, slices, 0)
     grad = gathered_rows(rows_ref, count, slices, LANES)
     inverse = inverse_of(raised, gain_of(raised[0:SLOT]))
-    pairs = (
-        (gate_own_ref, up_own_ref, down_own_ref),
-        (gate_other_ref, up_other_ref, down_other_ref),
-    )
+    pairs = [weight_refs[at : at + 2] for at in range(0, len(weight_refs), 2)]
+
+    def side_by_side(pair, base, index):
+        at = slice(base + index * wide, base + (index + 1) * wide)
+        return jnp.concatenate([pair[0][at, :], pair[1][at, :]], 1)
+
+    def down_block(pair, index):
+        at = 2 * D + index * wide
+        halves = [
+            jnp.concatenate([ref[at : at + LANES, :], ref[at + LANES : at + wide, :]], 1)
+            for ref in pair
+        ]
+        return jnp.concatenate(halves, 0)
+
     made = []
-    for gate_ref, up_ref, down_ref in pairs:
-        gate_val = inverse * nn_dot(raised, gate_ref[...])
-        up_val = inverse * nn_dot(raised, up_ref[...])
-        grad_active = nt_dot(grad, down_ref[...])
+    for pair in pairs:
+        zero = jnp.zeros((count * SLOT, wide), f32)
+        gate_val, up_val, grad_active = zero, zero, zero
+        for index in range(slices // 2):
+            at = slice(index * wide, (index + 1) * wide)
+            gate_val = gate_val + nn_dot(raised[:, at], side_by_side(pair, 0, index))
+            up_val = up_val + nn_dot(raised[:, at], side_by_side(pair, D, index))
+            grad_active = grad_active + nt_dot(grad[:, at], down_block(pair, index))
+        gate_val, up_val = inverse * gate_val, inverse * up_val
         sig = 1.0 / (1.0 + jnp.exp(-gate_val))
         silu = gate_val * sig
         active = (silu * up_val).astype(bf16)
         grad_gate = (grad_active * up_val * (sig * (1.0 + gate_val * (1.0 - sig)))).astype(bf16)
         grad_up = (grad_active * silu).astype(bf16)
         made.append((active, grad_gate, grad_up))
-    for index in range(slices):
-        at = slice(index * LANES, (index + 1) * LANES)
-        out = jnp.zeros((count * SLOT, LANES), f32)
-        back = jnp.zeros((count * SLOT, LANES), f32)
-        for (gate_ref, up_ref, down_ref), (active, grad_gate, grad_up) in zip(pairs, made):
-            out = out + nn_dot(active, down_ref[:, at])
-            back = back + nt_dot(grad_gate, gate_ref[at, :]) + nt_dot(grad_up, up_ref[at, :])
-        span = slice(index * SLOT, (index + 1) * SLOT)
-        out_ref[:, span, 0:LANES] = out.astype(bf16).reshape(count, SLOT, LANES)
-        out_ref[:, span, LANES:] = back.astype(bf16).reshape(count, SLOT, LANES)
+    for index in range(slices // 2):
+        out = jnp.zeros((count * SLOT, wide), f32)
+        back = jnp.zeros((count * SLOT, wide), f32)
+        for pair, (active, grad_gate, grad_up) in zip(pairs, made):
+            out = out + nn_dot(active, down_block(pair, index))
+            back = back + nt_dot(grad_gate, side_by_side(pair, 0, index))
+            back = back + nt_dot(grad_up, side_by_side(pair, D, index))
+        out, back = out.astype(bf16), back.astype(bf16)
+        for part in range(2):
+            at = slice(part * LANES, (part + 1) * LANES)
+            span = slice((2 * index + part) * SLOT, (2 * index + part + 1) * SLOT)
+            out_ref[:, span, 0:LANES] = out[:, at].reshape(count, SLOT, LANES)
+            out_ref[:, span, LANES:] = back[:, at].reshape(count, SLOT, LANES)
 
 
 def reduce_kernel(terms_ref, rows_ref, out_ref):
@@ -427,7 +438,7 @@
         out_ref[index * quarter : (index + 1) * quarter, :] = part[:, 0:ROPE].astype(bf16)
 
 
-def call(body, outs, scratch=(), scalars=0, count=0):
+def call(body, limit, outs, scratch=(), scalars=0, count=0):
     place = [pl.BlockSpec(memory_space=pltpu.SMEM)] * scalars
     return pl.pallas_call(
         body,
@@ -435,7 +446,7 @@
         in_specs=place + [pl.BlockSpec(memory_space=pltpu.VMEM)] * count,
         out_specs=jax.tree.map(lambda _: pl.BlockSpec(memory_space=pltpu.VMEM), outs),
         scratch_shapes=list(scratch),
-        compiler_params=pltpu.CompilerParams(vmem_limit_bytes=VMEM_LIMIT),
+        compiler_params=pltpu.CompilerParams(vmem_limit_bytes=limit * MIB),
     )
 
 
@@ -464,30 +475,36 @@
 ):
     rows, width = hidden_in.shape
     ctx_count, experts = lax.axis_size("ctx"), lax.axis_size("exp")
-    half = ctx_count // 2
-    groups = [[core + 2 * index for index in range(half)] for core in range(2)]
-    across = [(index, index ^ 1) for index in range(ctx_count)]
+    half, quarter_ctx = ctx_count // 2, ctx_count // 4
+    by_core = [[core + 2 * index for index in range(half)] for core in range(2)]
+    by_four = [[part + 4 * index for index in range(quarter_ctx)] for part in range(4)]
     depth = experts * SLOT
 
-    def swap(value):
-        return lax.ppermute(value, "ctx", across)
-
-    def spread(block):
-        copies = jnp.broadcast_to(block[None], (half,) + block.shape)
+    def swap(value, distance=1):
+        route = [(index, index ^ distance) for index in range(ctx_count)]
+        return lax.ppermute(value, "ctx", route)
+
+    def spread(block, groups):
+        count = len(groups[0])
+        copies = jnp.broadcast_to(block[None], (count,) + block.shape)
         return exchange(copies, "ctx", groups)
 
     place = lax.axis_index("ctx").astype(jnp.int32).reshape(1)
-    mine = (gate_weight[0], up_weight[0], down_weight[0])
-    others = [swap(weight) for weight in mine]
+    down = down_weight[0].reshape(-1, D // LANES, LANES).transpose(1, 0, 2).reshape(-1, LANES)
+    weights = [jnp.concatenate([gate_weight[0], up_weight[0], down], 0)]
+    weights.append(swap(weights[0]))
     block = jnp.concatenate(
         [key_nope, key_rope, query_rope, jnp.zeros((rows, ROPE), bf16), query_nope, values], 1
     )
-    same = spread(block).reshape(half * rows, -1)
+    same = spread(block, by_core).reshape(half * rows, -1)
     cross = swap(same)
+    far, same = lax.optimization_barrier((weights[0], same))
+    weights.append(swap(far, 2))
     gain_row = norm_gain.reshape(1, width)
 
     attended, logs, send = call(
         functools.partial(forward_kernel, experts),
+        14,
         (shape_of(rows, width), shape_of(rows, width, dtype=f32), shape_of(depth, 2 * width)),
         [pltpu.VMEM((2, rows, 2 * width), bf16)],
         1,
@@ -504,23 +521,27 @@
         cotangent,
     )
     received = exchange(send.reshape(experts, SLOT, 2 * width), "exp").reshape(depth, 2 * width)
-    rows_all = spread(received)
-    partial = call(expert_kernel, shape_of(half, depth, 2 * width), count=7)(
-        rows_all, *mine, *others
-    )
-    terms = exchange(partial, "ctx", groups)
-    back = call(reduce_kernel, shape_of(depth, 2 * width), count=2)(terms, received)
+    far, received = lax.optimization_barrier((weights[2], received))
+    weights.append(swap(far))
+    rows_all = spread(received, by_four)
+    partial = call(expert_kernel, 32, shape_of(quarter_ctx, depth, 2 * width), count=5)(
+        rows_all, *weights
+    )
+    terms = exchange(partial, "ctx", by_four)
+    back = call(reduce_kernel, 10, shape_of(depth, 2 * width), count=2)(terms, received)
     home = exchange(back.reshape(experts, SLOT, 2 * width), "exp").reshape(depth, 2 * width)
     layer_out, grad_hidden, stats = call(
         functools.partial(combine_kernel, experts),
+        6,
         (shape_of(rows, width), shape_of(rows, width), shape_of(rows, 2 * width)),
         count=7,
     )(home, hidden_in, attended, logs, expert_route.reshape(rows, 1), affinity, cotangent)
-    grad_same = spread(stats).reshape(half * rows, -1)
+    grad_same = spread(stats, by_core).reshape(half * rows, -1)
     grad_cross = swap(grad_same)
     quarter = rows // 4
     gq_nope, gq_rope, gk_nope, g_values, rope_part = call(
         backward_kernel,
+        20,
         (
             shape_of(rows, width),
             shape_of(rows, 2 * ROPE),
@@ -541,7 +562,7 @@
         6,
     )(place, same, cross, grad_same, grad_cross, block, stats)
     rope_terms = exchange(jnp.broadcast_to(rope_part[None], (experts, quarter, LANES)), "exp")
-    gk_rope = call(rope_kernel, shape_of(rows, ROPE), count=1)(rope_terms)
+    gk_rope = call(rope_kernel, 4, shape_of(rows, ROPE), count=1)(rope_terms)
     return (layer_out, grad_hidden, gq_nope, gq_rope, gk_nope, gk_rope, g_values)
 
 

time: 266 us -> 273 us (1.026)
  blocking collectives: 105 us -> 29.9 us
  waiting for transfers between devices: 62.5 us -> 107 us
  starting transfers between devices: 44.9 us -> 73.2 us
  other arithmetic: 0 us -> 16.4 us
  Pallas kernels: 33.6 us -> 25.9 us
    all_to_all x4 -> x2, blocking collectives: 105 us -> 29.9 us  [exchange(): lax.all_to_all(blocks, axis, 0, 0, tiled=True, axis_index_groups=groups)]
    all_to_all x3 -> x5, waiting for transfers between devices: 57.5 us -> 102 us  [exchange(): lax.all_to_all(blocks, axis, 0, 0, tiled=True, axis_index_groups=groups)]
    all_to_all x3 -> x5, starting transfers between devices: 21.4 us -> 49.2 us  [exchange(): lax.all_to_all(blocks, axis, 0, 0, tiled=True, axis_index_groups=groups)]
    concatenate x0 -> x1, other arithmetic: none -> 16.4 us  [per_device(): weights = [jnp.concatenate([gate_weight[0], up_weight[0], down], 0)]]
    pallas_call x6, Pallas kernels: 33.6 us -> 25.9 us  [the longest x1 10.9 us: per_device(): call(expert_kernel, 32, shape_of(quarter_ctx, depth, 2 * width), count=5)]
    unnamed x33 -> x38, local copies, waits for them, and re-layouts: 12 us -> 12.7 us
  transfers between devices with their start and end apart: 8 -> 10, of which waited for: 7 -> 7; matrix products, arithmetic and copies ran while one was open for 1% -> 8% of each run, Pallas kernels for 0% -> 0%
where the time goes in v2:
time: 273 us; the launch traced here: 271 us
  waiting for transfers between devices  107 us (39%)
  starting transfers between devices  73.2 us (27%)
  blocking collectives  29.9 us (11%)
  Pallas kernels  25.9 us (9%)
  local copies, waits for them, and re-layouts  18.3 us (7%)
  other arithmetic  16.4 us (6%)
    all_to_all x5, waiting for transfers between devices, exchange(): lax.all_to_all(blocks, axis, 0, 0, tiled=True, axis_index_groups=groups)  102 us
    all_to_all x5, starting transfers between devices, exchange(): lax.all_to_all(blocks, axis, 0, 0, tiled=True, axis_index_groups=groups)  49.2 us
    all_to_all x2, blocking collectives, exchange(): lax.all_to_all(blocks, axis, 0, 0, tiled=True, axis_index_groups=groups)  29.9 us
    ppermute x5, starting transfers between devices, swap(): return lax.ppermute(value, 'ctx', route)  24 us
    concatenate x1, other arithmetic, per_device(): weights = [jnp.concatenate([gate_weight[0], up_weight[0], down], 0)]  16.4 us
    unnamed x38, local copies, waits for them, and re-layouts  12.7 us
    pallas_call x1, Pallas kernels, per_device(): call(expert_kernel, 32, shape_of(quarter_ctx, depth, 2 * width), count=5)  10.9 us
    pallas_call x1, Pallas kernels, per_device(): call(backward_kernel, 20, (shape_of(rows, width), shape_of(rows, 2 * ROPE...  10.1 us
  transfers between devices with their start and end apart: 10, of which 7 were waited for; matrix products, arithmetic and copies ran while one was open for 8% of the time, Pallas kernels for 0%

profile of v2, /device:TPU:1, one launch (start us, length us, event | category | flops | bytes accessed | tf_op | source)
XLA Modules:
  0.0 271.5 jit_solution(8131086763758605181)
XLA Ops:
  1.5 0.9 copy.29
  2.4 1.0 concatenate.7.block_ref
  3.3 1.3 broadcast_in_dim.11
  4.6 7.5 %all-to-all-start = ((bf16[8,192,512]{2,1,0:T(8,128)(2,1)}), bf16[8,192,512]{2,1,0:T(8,128)(2,1)S(1)}, u32[]{:S(2)}, u32[]{:S(2)}) async-start(bf16[8,192,512]{2,1,0:T(8,128)(2,1)} %broadcast_in_dim.11), calls=%async_computation | async-start | bytes 3145728 | tf_op jit(solution)/shard_map/all_to_all | solution.py:458
  12.1 1.6 copy.35
  14.2 16.4 %pad_maximum_fusion.refs_0_ = bf16[12288,128]{1,0:T(8,128)(2,1)} fusion(bf16[4096,128]{1,0:T(8,128)(2,1)S(1)} %bitcast.29, bf16[4096,128]{1,0:T(8,128)(2,1)S(1)} %bitcast.31, bf16[4096,128]{1,0:T(8,128)(2,1)S(1)} %bitcast.32), kind=kLoop, calls=%fused_computation | loop fusion | flops 9437184 | bytes 6291456 | tf_op jit(solution)/shard_map/concatenate | solution.py:494
  30.6 2.3 all-to-all-done
  32.9 2.6 collective-permute-start
  35.5 5.4 %collective-permute-start.1 = (bf16[1536,512]{1,0:T(8,128)(2,1)S(1)}, bf16[1536,512]{1,0:T(8,128)(2,1)S(1)}, u32[]{:S(2)}, u32[]{:S(2)}) collective-permute-start(bf16[1536,512]{1,0:T(8,128)(2,1)S(1)} %bitcast.18), channel_id=1, source_target_pairs={{0,32},{32,0},{64,96},{96,64},{128,160},{160,128},{192,224},{224,1... | collective-permute-start | bytes 4718600 | tf_op jit(solution)/shard_map/ppermute | solution.py:485
  41.0 2.9 %collective-permute-done.1.cross_ref = bf16[1536,512]{1,0:T(8,128)(2,1)S(1)} collective-permute-done((bf16[1536,512]{1,0:T(8,128)(2,1)S(1)}, bf16[1536,512]{1,0:T(8,128)(2,1)S(1)}, u32[]{:S(2)}, u32[]{:S(2)}) %collective-permute-start.1) | collective-permute-done | bytes 1572896 | tf_op jit(solution)/shard_map/ppermute | solution.py:485
  43.9 1.3 shard_map.180
  47.2 16.6 %all-to-all-start.1 = ((bf16[32,16,256]{2,1,0:T(8,128)(2,1)}), bf16[32,16,256]{2,1,0:T(8,128)(2,1)}, u32[]{:S(2)}, u32[]{:S(2)}) async-start(bf16[32,16,256]{2,1,0:T(8,128)(2,1)} %bitcast.24), calls=%async_computation.1 | async-start | bytes 524288 | tf_op jit(solution)/shard_map/all_to_all | solution.py:458
  63.8 2.6 collective-permute-start.2
  66.4 41.5 %all-to-all-done.1 = bf16[32,16,256]{2,1,0:T(8,128)(2,1)} async-done(((bf16[32,16,256]{2,1,0:T(8,128)(2,1)}), bf16[32,16,256]{2,1,0:T(8,128)(2,1)}, u32[]{:S(2)}, u32[]{:S(2)}) %all-to-all-start.1) | async-done | bytes 262176 | tf_op jit(solution)/shard_map/all_to_all | solution.py:458
  107.9 4.8 %collective-permute-start.3 = (bf16[12288,128]{1,0:T(8,128)(2,1)}, bf16[12288,128]{1,0:T(8,128)(2,1)}, u32[]{:S(2)}, u32[]{:S(2)}) collective-permute-start(bf16[12288,128]{1,0:T(8,128)(2,1)} %collective-permute-done.refs_2_), channel_id=1, source_target_pairs={{0,32},{32,0},{64,96},{96,64},{128,160},{160,128},{192,224},{224,1... | collective-permute-start | bytes 9437192 | tf_op jit(solution)/shard_map/ppermute | solution.py:485
  112.7 2.0 broadcast_in_dim.12
  114.7 4.3 %all-to-all-start.2 = ((bf16[4,512,256]{2,1,0:T(8,128)(2,1)}), bf16[4,512,256]{2,1,0:T(8,128)(2,1)}, u32[]{:S(2)}, u32[]{:S(2)}) async-start(bf16[4,512,256]{2,1,0:T(8,128)(2,1)} %broadcast_in_dim.12), calls=%async_computation.2 | async-start | bytes 2097152 | tf_op jit(solution)/shard_map/all_to_all | solution.py:458
  119.0 15.3 %all-to-all-done.2.rows_ref = bf16[4,512,256]{2,1,0:T(8,128)(2,1)} async-done(((bf16[4,512,256]{2,1,0:T(8,128)(2,1)}), bf16[4,512,256]{2,1,0:T(8,128)(2,1)}, u32[]{:S(2)}, u32[]{:S(2)}) %all-to-all-start.2) | async-done | bytes 1048608 | tf_op jit(solution)/shard_map/all_to_all | solution.py:458
  134.3 1.9 copy-done
  136.2 10.9 %shard_map.181 = bf16[4,512,256]{2,1,0:T(8,128)(2,1)S(1)} custom-call(bf16[4,512,256]{2,1,0:T(8,128)(2,1)} %all-to-all-done.2.rows_ref, bf16[12288,128]{1,0:T(8,128)(2,1)S(1)} %copy-done, bf16[12288,128]{1,0:T(8,128)(2,1)} %collective-permute-done.2.refs_1_, bf16[12288,128]{1,0:T(8,128)(2,1)} %collective-permute-done.refs_2_, ...), custom_call_target="tpu_custom_call" | custom-call | tf_op jit(solution)/shard_map/pallas_call | solution.py:527
  147.1 16.6 %all_to_all.35.terms_ref = bf16[4,512,256]{2,1,0:T(8,128)(2,1)S(1)} all-to-all(bf16[4,512,256]{2,1,0:T(8,128)(2,1)S(1)} %shard_map.181), channel_id=1, replica_groups={{0,128,256,384},{32,160,288,416},{64,192,320,448},{96,224,352,480},{1,1..., dimensions={0} | all-to-all | bytes 2097152 | tf_op jit(solution)/shard_map/all_to_all | solution.py:458
  163.7 1.3 shard_map.182
  165.7 16.9 %all-to-all-start.4 = ((bf16[32,16,256]{2,1,0:T(8,128)(2,1)}), bf16[32,16,256]{2,1,0:T(8,128)(2,1)}, u32[]{:S(2)}, u32[]{:S(2)}) async-start(bf16[32,16,256]{2,1,0:T(8,128)(2,1)} %bitcast.23), calls=%async_computation.4 | async-start | bytes 524288 | tf_op jit(solution)/shard_map/all_to_all | solution.py:458
  182.7 18.0 %all-to-all-done.4 = bf16[32,16,256]{2,1,0:T(8,128)(2,1)} async-done(((bf16[32,16,256]{2,1,0:T(8,128)(2,1)}), bf16[32,16,256]{2,1,0:T(8,128)(2,1)}, u32[]{:S(2)}, u32[]{:S(2)}) %all-to-all-start.4) | async-done | bytes 262176 | tf_op jit(solution)/shard_map/all_to_all | solution.py:458
  202.3 0.9 copy-done.8
  204.0 2.2 shard_map.183
  206.2 13.4 %all_to_all.36 = bf16[8,192,256]{2,1,0:T(8,128)(2,1)S(1)} all-to-all(bf16[8,192,256]{2,1,0:T(8,128)(2,1)S(1)} %broadcast_in_dim.13), channel_id=1, replica_groups={{0,64,128,192,256,320,384,448},{32,96,160,224,288,352,416,480},{1,65,12..., dimensions={0} | all-to-all | bytes 1572864 | tf_op jit(solution)/shard_map/all_to_all | solution.py:458
  219.6 8.6 %collective-permute-start.4 = (bf16[1536,256]{1,0:T(8,128)(2,1)S(1)}, bf16[1536,256]{1,0:T(8,128)(2,1)S(1)}, u32[]{:S(2)}, u32[]{:S(2)}) collective-permute-start(bf16[1536,256]{1,0:T(8,128)(2,1)S(1)} %bitcast.21), channel_id=1, source_target_pairs={{0,32},{32,0},{64,96},{96,64},{128,160},{160,128},{192,224},{224,1... | collective-permute-start | bytes 2359304 | tf_op jit(solution)/shard_map/ppermute | solution.py:485
  228.2 1.9 collective-permute-done.4.grad_cross_ref
  230.1 10.1 %shard_map.184 = (bf16[192,128]{1,0:T(8,128)(2,1)}, bf16[192,64]{1,0:T(8,128)(2,1)S(1)}, bf16[192,128]{1,0:T(8,128)(2,1)}, bf16[192,128]{1,0:T(8,128)(2,1)}, bf16[48,128]{1,0:T(8,128)(2,1)S(1)}) custom-call(s32[1]{0:T(128)} %bitcast.5.place_ref, bf16[1536,512]{1,0:T(8,128)(2,1)S(1)} %bitcast.20, bf16[1536,512]{1,0:T(8,128)(2,1)S(1)} %collective-permute-done.1.cross_ref, ...), custom_call_target="tpu_custom_call" | custom-call | tf_op jit(solution)/shard_map/pallas_call | solution.py:542
  241.0 3.9 %all-to-all-start.6 = ((bf16[32,48,128]{2,1,0:T(8,128)(2,1)}), bf16[32,48,128]{2,1,0:T(8,128)(2,1)S(1)}, u32[]{:S(2)}, u32[]{:S(2)}) async-start(bf16[32,48,128]{2,1,0:T(8,128)(2,1)} %broadcast_in_dim.14), calls=%async_computation.6 | async-start | bytes 786432 | tf_op jit(solution)/shard_map/all_to_all | solution.py:458
  245.6 25.0 %all-to-all-done.6.terms_ref = bf16[32,48,128]{2,1,0:T(8,128)(2,1)S(1)} async-done(((bf16[32,48,128]{2,1,0:T(8,128)(2,1)}), bf16[32,48,128]{2,1,0:T(8,128)(2,1)S(1)}, u32[]{:S(2)}, u32[]{:S(2)}) %all-to-all-start.6) | async-done | bytes 393248 | tf_op jit(solution)/shard_map/all_to_all | solution.py:458
  (43 shorter events, 9.0 us)
Async XLA Ops:
  4.6 28.3 %all-to-all-start = ((bf16[8,192,512]{2,1,0:T(8,128)(2,1)}), bf16[8,192,512]{2,1,0:T(8,128)(2,1)S(1)}, u32[]{:S(2)}, u32[]{:S(2)}) async-start(bf16[8,192,512]{2,1,0:T(8,128)(2,1)} %broadcast_in_dim.11), calls=%async_computation | async-start | bytes 3145728 | tf_op jit(solution)/shard_map/all_to_all | solution.py:458
  12.1 2.0 copy-start.13
  12.1 2.0 copy-start.14
  14.2 26.7 %copy-start.15 = (f32[192,8]{0,1:T(8,128)S(1)}, f32[192,8]{0,1:T(8,128)}, u32[]{:S(2)}) copy-start(f32[192,8]{0,1:T(8,128)} %param.21) | copy-start | bytes 18436
  14.2 29.7 %copy-start.3 = (bf16[192,128]{1,0:T(8,128)(2,1)S(1)}, bf16[192,128]{1,0:T(8,128)(2,1)}, u32[]{:S(2)}) copy-start(bf16[192,128]{1,0:T(8,128)(2,1)} %hidden_ref.3) | copy-start | bytes 147460
  14.2 29.7 %copy-start.5 = (bf16[192,128]{1,0:T(8,128)(2,1)S(1)}, bf16[192,128]{1,0:T(8,128)(2,1)}, u32[]{:S(2)}) copy-start(bf16[192,128]{1,0:T(8,128)(2,1)} %cotangent_ref.3) | copy-start | bytes 147460
  14.2 29.7 %copy-start.11 = (s32[192]{0:T(256)S(1)}, s32[192]{0:T(256)}, u32[]{:S(2)}) copy-start(s32[192]{0:T(256)} %param.20) | copy-start | bytes 2308
  14.2 29.7 %copy-start.12 = (f32[128]{0:T(128)S(1)}, f32[128]{0:T(128)}, u32[]{:S(2)}) copy-start(f32[128]{0:T(128)} %param.19) | copy-start | bytes 1540
  32.9 75.0 %collective-permute-start = (bf16[12288,128]{1,0:T(8,128)(2,1)}, bf16[12288,128]{1,0:T(8,128)(2,1)}, u32[]{:S(2)}, u32[]{:S(2)}) collective-permute-start(bf16[12288,128]{1,0:T(8,128)(2,1)} %pad_maximum_fusion.refs_0_), channel_id=1, source_target_pairs={{0,64},{32,96},{64,0},{96,32},{128,192},{160,224},{192,128},{224,1... | collective-permute-start | bytes 9437192 | tf_op jit(solution)/shard_map/ppermute | solution.py:485
  35.5 8.4 %collective-permute-start.1 = (bf16[1536,512]{1,0:T(8,128)(2,1)S(1)}, bf16[1536,512]{1,0:T(8,128)(2,1)S(1)}, u32[]{:S(2)}, u32[]{:S(2)}) collective-permute-start(bf16[1536,512]{1,0:T(8,128)(2,1)S(1)} %bitcast.18), channel_id=1, source_target_pairs={{0,32},{32,0},{64,96},{96,64},{128,160},{160,128},{192,224},{224,1... | collective-permute-start | bytes 4718600 | tf_op jit(solution)/shard_map/ppermute | solution.py:485
  45.2 0.7 copy-start.2
  45.9 0.6 copy-start.7
  46.6 0.6 copy-start.9
  47.2 60.7 %all-to-all-start.1 = ((bf16[32,16,256]{2,1,0:T(8,128)(2,1)}), bf16[32,16,256]{2,1,0:T(8,128)(2,1)}, u32[]{:S(2)}, u32[]{:S(2)}) async-start(bf16[32,16,256]{2,1,0:T(8,128)(2,1)} %bitcast.24), calls=%async_computation.1 | async-start | bytes 524288 | tf_op jit(solution)/shard_map/all_to_all | solution.py:458
  63.8 55.1 %collective-permute-start.2 = (bf16[12288,128]{1,0:T(8,128)(2,1)}, bf16[12288,128]{1,0:T(8,128)(2,1)}, u32[]{:S(2)}, u32[]{:S(2)}) collective-permute-start(bf16[12288,128]{1,0:T(8,128)(2,1)} %pad_maximum_fusion.refs_0_), channel_id=1, source_target_pairs={{0,32},{32,0},{64,96},{96,64},{128,160},{160,128},{192,224},{224,1... | collective-permute-start | bytes 9437192 | tf_op jit(solution)/shard_map/ppermute | solution.py:485
  107.9 26.4 %collective-permute-start.3 = (bf16[12288,128]{1,0:T(8,128)(2,1)}, bf16[12288,128]{1,0:T(8,128)(2,1)}, u32[]{:S(2)}, u32[]{:S(2)}) collective-permute-start(bf16[12288,128]{1,0:T(8,128)(2,1)} %collective-permute-done.refs_2_), channel_id=1, source_target_pairs={{0,32},{32,0},{64,96},{96,64},{128,160},{160,128},{192,224},{224,1... | collective-permute-start | bytes 9437192 | tf_op jit(solution)/shard_map/ppermute | solution.py:485
  114.7 19.6 %all-to-all-start.2 = ((bf16[4,512,256]{2,1,0:T(8,128)(2,1)}), bf16[4,512,256]{2,1,0:T(8,128)(2,1)}, u32[]{:S(2)}, u32[]{:S(2)}) async-start(bf16[4,512,256]{2,1,0:T(8,128)(2,1)} %broadcast_in_dim.12), calls=%async_computation.2 | async-start | bytes 2097152 | tf_op jit(solution)/shard_map/all_to_all | solution.py:458
  134.3 1.9 copy-start
  165.0 0.7 copy-start.1
  165.7 35.1 %all-to-all-start.4 = ((bf16[32,16,256]{2,1,0:T(8,128)(2,1)}), bf16[32,16,256]{2,1,0:T(8,128)(2,1)}, u32[]{:S(2)}, u32[]{:S(2)}) async-start(bf16[32,16,256]{2,1,0:T(8,128)(2,1)} %bitcast.23), calls=%async_computation.4 | async-start | bytes 524288 | tf_op jit(solution)/shard_map/all_to_all | solution.py:458
  200.7 0.8 copy-start.4
  201.5 0.8 copy-start.6
  202.3 0.9 copy-start.8
  203.2 0.8 copy-start.10
  219.6 10.5 %collective-permute-start.4 = (bf16[1536,256]{1,0:T(8,128)(2,1)S(1)}, bf16[1536,256]{1,0:T(8,128)(2,1)S(1)}, u32[]{:S(2)}, u32[]{:S(2)}) collective-permute-start(bf16[1536,256]{1,0:T(8,128)(2,1)S(1)} %bitcast.21), channel_id=1, source_target_pairs={{0,32},{32,0},{64,96},{96,64},{128,160},{160,128},{192,224},{224,1... | collective-permute-start | bytes 2359304 | tf_op jit(solution)/shard_map/ppermute | solution.py:485
  241.0 29.6 %all-to-all-start.6 = ((bf16[32,48,128]{2,1,0:T(8,128)(2,1)}), bf16[32,48,128]{2,1,0:T(8,128)(2,1)S(1)}, u32[]{:S(2)}, u32[]{:S(2)}) async-start(bf16[32,48,128]{2,1,0:T(8,128)(2,1)} %broadcast_in_dim.14), calls=%async_computation.6 | async-start | bytes 786432 | tf_op jit(solution)/shard_map/all_to_all | solution.py:458

commit v3 on v2

--- a/solution.py
+++ b/solution.py
@@ -87,7 +87,21 @@
     return route_row * SLOT + rank.astype(jnp.int32)
 
 
-def slots_along_columns(route_column, experts):
+def column_of(row):
+    count = row.shape[1]
+    shape = (count, count)
+    match = lax.broadcasted_iota(jnp.int32, shape, 0) == lanes_of(shape)
+    return jnp.sum(jnp.where(match, row, jnp.zeros_like(row)), 1, keepdims=True)
+
+
+def unit_matrix(rows, columns, offset=0):
+    shape = (rows, columns)
+    match = lax.broadcasted_iota(jnp.int32, shape, 0) + offset == lanes_of(shape)
+    return match.astype(f32).astype(bf16)
+
+
+def slots_along_columns(route_row, experts):
+    route_column = column_of(route_row)
     count = route_column.shape[0]
     hits = (lanes_of((count, experts)) == route_column).astype(f32)
     before = lanes_of((count, count)) < lax.broadcasted_iota(jnp.int32, (count, count), 0)
@@ -97,7 +111,22 @@
 
 
 def gate_share_of(affinity):
-    return route_scale * affinity[:, 0:1] / jnp.sum(affinity, 1, keepdims=True)
+    return column_of(route_scale * affinity[0:1] / jnp.sum(affinity, 0, keepdims=True))
+
+
+def pack_kernel(key_nope_ref, key_rope_ref, query_rope_ref, query_nope_ref, values_ref, *outs):
+    block_ref, copies_ref = outs
+    rows = key_nope_ref.shape[0]
+    rots = jnp.concatenate(
+        [key_rope_ref[...], query_rope_ref[...], jnp.zeros((ROPE, rows), bf16)], 0
+    )
+    block_ref[:, 0:128] = key_nope_ref[...]
+    block_ref[:, 128:256] = nt_dot(unit_matrix(rows, rows), rots).astype(bf16)
+    block_ref[:, 256:384] = query_nope_ref[...]
+    block_ref[:, 384:512] = values_ref[...]
+    block = block_ref[...]
+    for index in range(copies_ref.shape[0]):
+        copies_ref[index] = block
 
 
 def forward_kernel(
@@ -196,51 +225,39 @@
 
 
 def expert_kernel(rows_ref, *refs):
-    weight_refs, out_ref = refs[:-1], refs[-1]
+    gates, ups, downs, out_ref = refs[0:2], refs[2:4], refs[4:6], refs[6]
     count, depth, _ = rows_ref.shape
     slices = depth // SLOT
     wide = 2 * LANES
     raised = gathered_rows(rows_ref, count, slices, 0)
     grad = gathered_rows(rows_ref, count, slices, LANES)
     inverse = inverse_of(raised, gain_of(raised[0:SLOT]))
-    pairs = [weight_refs[at : at + 2] for at in range(0, len(weight_refs), 2)]
-
-    def side_by_side(pair, base, index):
-        at = slice(base + index * wide, base + (index + 1) * wide)
-        return jnp.concatenate([pair[0][at, :], pair[1][at, :]], 1)
-
-    def down_block(pair, index):
-        at = 2 * D + index * wide
-        halves = [
-            jnp.concatenate([ref[at : at + LANES, :], ref[at + LANES : at + wide, :]], 1)
-            for ref in pair
-        ]
-        return jnp.concatenate(halves, 0)
-
-    made = []
-    for pair in pairs:
-        zero = jnp.zeros((count * SLOT, wide), f32)
-        gate_val, up_val, grad_active = zero, zero, zero
-        for index in range(slices // 2):
-            at = slice(index * wide, (index + 1) * wide)
-            gate_val = gate_val + nn_dot(raised[:, at], side_by_side(pair, 0, index))
-            up_val = up_val + nn_dot(raised[:, at], side_by_side(pair, D, index))
-            grad_active = grad_active + nt_dot(grad[:, at], down_block(pair, index))
-        gate_val, up_val = inverse * gate_val, inverse * up_val
-        sig = 1.0 / (1.0 + jnp.exp(-gate_val))
-        silu = gate_val * sig
-        active = (silu * up_val).astype(bf16)
-        grad_gate = (grad_active * up_val * (sig * (1.0 + gate_val * (1.0 - sig)))).astype(bf16)
-        grad_up = (grad_active * silu).astype(bf16)
-        made.append((active, grad_gate, grad_up))
+
+    def columns_of(refs, index):
+        at = slice(index * wide, (index + 1) * wide)
+        return jnp.concatenate([ref[at, :] for ref in refs], 1)
+
+    def rows_of(refs, index):
+        at = slice(index * wide, (index + 1) * wide)
+        return jnp.concatenate([ref[:, at] for ref in refs], 0)
+
+    zero = jnp.zeros((count * SLOT, wide), f32)
+    gate_val, up_val, grad_active = zero, zero, zero
     for index in range(slices // 2):
-        out = jnp.zeros((count * SLOT, wide), f32)
-        back = jnp.zeros((count * SLOT, wide), f32)
-        for pair, (active, grad_gate, grad_up) in zip(pairs, made):
-            out = out + nn_dot(active, down_block(pair, index))
-            back = back + nt_dot(grad_gate, side_by_side(pair, 0, index))
-            back = back + nt_dot(grad_up, side_by_side(pair, D, index))
-        out, back = out.astype(bf16), back.astype(bf16)
+        at = slice(index * wide, (index + 1) * wide)
+        gate_val = gate_val + nn_dot(raised[:, at], columns_of(gates, index))
+        up_val = up_val + nn_dot(raised[:, at], columns_of(ups, index))
+        grad_active = grad_active + nt_dot(grad[:, at], rows_of(downs, index))
+    gate_val, up_val = inverse * gate_val, inverse * up_val
+    sig = 1.0 / (1.0 + jnp.exp(-gate_val))
+    silu = gate_val * sig
+    active = (silu * up_val).astype(bf16)
+    grad_gate = (grad_active * up_val * (sig * (1.0 + gate_val * (1.0 - sig)))).astype(bf16)
+    grad_up = (grad_active * silu).astype(bf16)
+    for index in range(slices // 2):
+        out = nn_dot(active, rows_of(downs, index)).astype(bf16)
+        back = nt_dot(grad_gate, columns_of(gates, index))
+        back = (back + nt_dot(grad_up, columns_of(ups, index))).astype(bf16)
         for part in range(2):
             at = slice(part * LANES, (part + 1) * LANES)
             span = slice((2 * index + part) * SLOT, (2 * index + part + 1) * SLOT)
@@ -301,8 +318,10 @@
     stats = jnp.zeros((rows, LANES), f32)
     for index, column in enumerate(columns):
         stats = jnp.where(lane == index, column, stats)
-    stats_ref[:, 0:LANES] = grad
-    stats_ref[:, LANES:] = stats.astype(bf16)
+    stats = stats.astype(bf16)
+    for index in range(stats_ref.shape[0]):
+        stats_ref[index, :, 0:LANES] = grad
+        stats_ref[index, :, LANES:] = stats
 
 
 def backward_kernel(
@@ -341,8 +360,8 @@
         of_log = jnp.where((lane >= base + 3) & (lane < base + 6), one, 0.0).astype(bf16)
         ones_log.append(of_log)
         mine = lane // VDIM == head
-        stats = stats_ref[:, LANES:].astype(f32)
-        own = jnp.where(mine, stats_ref[:, 0:LANES], zero)
+        stats = stats_ref[0, :, LANES:].astype(f32)
+        own = jnp.where(mine, stats_ref[0, :, 0:LANES], zero)
         value = jnp.where(mine, block_ref[:, VALUE], zero)
         grads_ref[head] = own
         vals_ref[head] = jnp.concatenate([value, minus], 1)
@@ -409,7 +428,8 @@
     rot = jnp.where(
         lane < ROPE, dq_ref[0, :, LANES:], pltpu.roll(dq_ref[1, :, LANES:], ROPE, 1)
     )
-    query_rope_ref[...] = (score_scale * rot).astype(bf16)[:, 0 : 2 * ROPE]
+    rot = (score_scale * rot).astype(bf16)
+    query_rope_ref[...] = nt_dot(unit_matrix(2 * ROPE, LANES), rot).astype(bf16)
     key_nope_ref[...] = (
         score_scale * jnp.where(first, dk_ref[0, :, LANES:], dk_ref[1, :, LANES:])
     ).astype(bf16)
@@ -425,17 +445,22 @@
         if index:
             part = pltpu.roll(part, index * ROPE, 1)
         packed = jnp.where(small // ROPE == index, part, packed)
-    rope_ref[...] = (score_scale * packed).astype(bf16)
+    packed = (score_scale * packed).astype(bf16)
+    for index in range(rope_ref.shape[0]):
+        rope_ref[index] = packed
 
 
 def rope_kernel(terms_ref, out_ref):
     total = terms_ref[0].astype(f32)
     for index in range(1, terms_ref.shape[0]):
         total = total + terms_ref[index].astype(f32)
+    total = total.astype(bf16)
     quarter = total.shape[0]
+    out = jnp.zeros((ROPE, 4 * quarter), f32)
     for index in range(4):
-        part = total if index == 0 else pltpu.roll(total, LANES - index * ROPE, 1)
-        out_ref[index * quarter : (index + 1) * quarter, :] = part[:, 0:ROPE].astype(bf16)
+        part = nt_dot(unit_matrix(ROPE, LANES, index * ROPE), total).astype(bf16)
+        out = out + nn_dot(part, unit_matrix(quarter, 4 * quarter, index * quarter))
+    out_ref[...] = out.astype(bf16)
 
 
 def call(body, limit, outs, scratch=(), scalars=0, count=0):
@@ -475,32 +500,28 @@
 ):
     rows, width = hidden_in.shape
     ctx_count, experts = lax.axis_size("ctx"), lax.axis_size("exp")
-    half, quarter_ctx = ctx_count // 2, ctx_count // 4
+    half = ctx_count // 2
     by_core = [[core + 2 * index for index in range(half)] for core in range(2)]
-    by_four = [[part + 4 * index for index in range(quarter_ctx)] for part in range(4)]
+    across = [(index, index ^ 1) for index in range(ctx_count)]
     depth = experts * SLOT
-
-    def swap(value, distance=1):
-        route = [(index, index ^ distance) for index in range(ctx_count)]
-        return lax.ppermute(value, "ctx", route)
-
-    def spread(block, groups):
-        count = len(groups[0])
-        copies = jnp.broadcast_to(block[None], (count,) + block.shape)
-        return exchange(copies, "ctx", groups)
+    quarter = rows // 4
+
+    def swap(value):
+        return lax.ppermute(value, "ctx", across)
 
     place = lax.axis_index("ctx").astype(jnp.int32).reshape(1)
-    down = down_weight[0].reshape(-1, D // LANES, LANES).transpose(1, 0, 2).reshape(-1, LANES)
-    weights = [jnp.concatenate([gate_weight[0], up_weight[0], down], 0)]
-    weights.append(swap(weights[0]))
-    block = jnp.concatenate(
-        [key_nope, key_rope, query_rope, jnp.zeros((rows, ROPE), bf16), query_nope, values], 1
-    )
-    same = spread(block, by_core).reshape(half * rows, -1)
+    route = expert_route.reshape(1, rows)
+    affinity = affinity.T
+    weights = []
+    for weight in (gate_weight[0], up_weight[0], down_weight[0]):
+        weights += [weight, swap(weight)]
+    block, copies = call(
+        pack_kernel, 8, (shape_of(rows, 512), shape_of(half, rows, 512)), count=5
+    )(key_nope, key_rope.T, query_rope.T, query_nope, values)
+    same = exchange(copies, "ctx", by_core)
+    same, weights = lax.optimization_barrier((same, weights))
+    same = same.reshape(half * rows, -1)
     cross = swap(same)
-    far, same = lax.optimization_barrier((weights[0], same))
-    weights.append(swap(far, 2))
-    gain_row = norm_gain.reshape(1, width)
 
     attended, logs, send = call(
         functools.partial(forward_kernel, experts),
@@ -515,39 +536,37 @@
         cross,
         block,
         hidden_in,
-        gain_row,
-        expert_route.reshape(1, rows),
+        norm_gain.reshape(1, width),
+        route,
         affinity,
         cotangent,
     )
     received = exchange(send.reshape(experts, SLOT, 2 * width), "exp").reshape(depth, 2 * width)
-    far, received = lax.optimization_barrier((weights[2], received))
-    weights.append(swap(far))
-    rows_all = spread(received, by_four)
-    partial = call(expert_kernel, 32, shape_of(quarter_ctx, depth, 2 * width), count=5)(
+    copies = jnp.broadcast_to(received[None], (half, depth, 2 * width))
+    rows_all = exchange(copies, "ctx", by_core)
+    partial = call(expert_kernel, 28, shape_of(half, depth, 2 * width), count=7)(
         rows_all, *weights
     )
-    terms = exchange(partial, "ctx", by_four)
+    terms = exchange(partial, "ctx", by_core)
     back = call(reduce_kernel, 10, shape_of(depth, 2 * width), count=2)(terms, received)
     home = exchange(back.reshape(experts, SLOT, 2 * width), "exp").reshape(depth, 2 * width)
     layer_out, grad_hidden, stats = call(
         functools.partial(combine_kernel, experts),
-        6,
-        (shape_of(rows, width), shape_of(rows, width), shape_of(rows, 2 * width)),
+        8,
+        (shape_of(rows, width), shape_of(rows, width), shape_of(half, rows, 2 * width)),
         count=7,
-    )(home, hidden_in, attended, logs, expert_route.reshape(rows, 1), affinity, cotangent)
-    grad_same = spread(stats, by_core).reshape(half * rows, -1)
+    )(home, hidden_in, attended, logs, route, affinity, cotangent)
+    grad_same = exchange(stats, "ctx", by_core).reshape(half * rows, -1)
     grad_cross = swap(grad_same)
-    quarter = rows // 4
-    gq_nope, gq_rope, gk_nope, g_values, rope_part = call(
+    *grads, rope_part = call(
         backward_kernel,
         20,
         (
             shape_of(rows, width),
-            shape_of(rows, 2 * ROPE),
+            shape_of(2 * ROPE, rows),
             shape_of(rows, width),
             shape_of(rows, width),
-            shape_of(quarter, LANES),
+            shape_of(experts, quarter, LANES),
         ),
         [
             pltpu.VMEM((2, rows, 2 * width), bf16),
@@ -561,9 +580,16 @@
         1,
         6,
     )(place, same, cross, grad_same, grad_cross, block, stats)
-    rope_terms = exchange(jnp.broadcast_to(rope_part[None], (experts, quarter, LANES)), "exp")
-    gk_rope = call(rope_kernel, 4, shape_of(rows, ROPE), count=1)(rope_terms)
-    return (layer_out, grad_hidden, gq_nope, gq_rope, gk_nope, gk_rope, g_values)
+    grads, layer_out, grad_hidden, rope_part = lax.optimization_barrier(
+        (grads, layer_out, grad_hidden, rope_part)
+    )
+    rope_terms = exchange(rope_part, "exp")
+    grads, layer_out, grad_hidden, rope_terms = lax.optimization_barrier(
+        (grads, layer_out, grad_hidden, rope_terms)
+    )
+    gk_rope = call(rope_kernel, 4, shape_of(ROPE, rows), count=1)(rope_terms)
+    gq_nope, gq_rope, gk_nope, g_values = grads
+    return (layer_out, grad_hidden, gq_nope, gq_rope.T, gk_nope, gk_rope.T, g_values)
 
 
 def solution(mesh):

time: 273 us -> 237 us (0.87)
  blocking collectives: 29.9 us -> 165 us
  waiting for transfers between devices: 107 us -> 13.5 us
  starting transfers between devices: 73.2 us -> 30.4 us
  other arithmetic: 16.4 us -> 0 us
  local copies, waits for them, and re-layouts: 18.3 us -> 7.08 us
  Pallas kernels: 25.9 us -> 19.7 us
    all_to_all x2 -> x6, blocking collectives: 29.9 us -> 165 us  [exchange(): lax.all_to_all(blocks, axis, 0, 0, tiled=True, axis_index_groups=groups)]
    all_to_all x5 -> x1, waiting for transfers between devices: 102 us -> 8.08 us  [exchange(): lax.all_to_all(blocks, axis, 0, 0, tiled=True, axis_index_groups=groups)]
    all_to_all x5 -> x1, starting transfers between devices: 49.2 us -> 7.48 us  [exchange(): lax.all_to_all(blocks, axis, 0, 0, tiled=True, axis_index_groups=groups)]
    concatenate x1 -> x0, other arithmetic: 16.4 us -> none  [per_device(): weights = [jnp.concatenate([gate_weight[0], up_weight[0], down], 0)]]
    unnamed x38 -> x40, local copies, waits for them, and re-layouts: 12.7 us -> 6.94 us
    pallas_call x4 -> x5, Pallas kernels: 23.3 us -> 17.9 us  [the longest x1 10.2 us: per_device(): call(backward_kernel, 20, (shape_of(rows, width), shape_of(2 * ROPE, rows...]
    broadcast_in_dim x5 -> x1, local copies, waits for them, and re-layouts: 4.16 us -> 0.14 us  [per_device(): copies = jnp.broadcast_to(received[None], (half, depth, 2 * width))]
  transfers between devices with their start and end apart: 10 -> 6, of which waited for: 7 -> 4; matrix products, arithmetic and copies ran while one was open for 8% -> 0% of each run, Pallas kernels for 0% -> 0%
where the time goes in v3:
time: 237 us; the launch traced here: 236 us
  blocking collectives  165 us (70%)
  starting transfers between devices  30.4 us (13%)
  Pallas kernels  19.7 us (8%)
  waiting for transfers between devices  13.5 us (6%)
  local copies, waits for them, and re-layouts  7.08 us (3%)
    all_to_all x6, blocking collectives, exchange(): lax.all_to_all(blocks, axis, 0, 0, tiled=True, axis_index_groups=groups)  165 us
    ppermute x5, starting transfers between devices, swap(): return lax.ppermute(value, 'ctx', across)  23 us
    pallas_call x1, Pallas kernels, per_device(): call(backward_kernel, 20, (shape_of(rows, width), shape_of(2 * ROPE, rows...  10.2 us
    all_to_all x1, waiting for transfers between devices, exchange(): lax.all_to_all(blocks, axis, 0, 0, tiled=True, axis_index_groups=groups)  8.08 us
    all_to_all x1, starting transfers between devices, exchange(): lax.all_to_all(blocks, axis, 0, 0, tiled=True, axis_index_groups=groups)  7.48 us
    unnamed x40, local copies, waits for them, and re-layouts  6.94 us
    ppermute x5, waiting for transfers between devices, swap(): return lax.ppermute(value, 'ctx', across)  5.4 us
  transfers between devices with their start and end apart: 6, of which 4 were waited for; matrix products, arithmetic and copies ran while one was open for 0% of the time, Pallas kernels for 0%

profile of v3, /device:TPU:1, one launch (start us, length us, event | category | flops | bytes accessed | tf_op | source)
XLA Modules:
  0.0 236.3 jit_solution(12856402359643731649)
XLA Ops:
  0.7 0.9 copy-done.12
  1.6 0.8 copy-done.13
  2.4 0.8 copy-done.14
  3.2 0.8 copy-done.16
  3.9 0.7 copy-done.17
  4.6 1.4 shard_map.180
  6.1 7.5 %all-to-all-start = ((bf16[8,192,512]{2,1,0:T(8,128)(2,1)}), bf16[8,192,512]{2,1,0:T(8,128)(2,1)S(1)}, u32[]{:S(2)}, u32[]{:S(2)}) async-start(bf16[8,192,512]{2,1,0:T(8,128)(2,1)} %get-tuple-element.41), calls=%async_computation | async-start | bytes 3145728 | tf_op jit(solution)/shard_map/all_to_all | solution.py:483
  13.6 4.9 %collective-permute-start = (bf16[4096,128]{1,0:T(8,128)(2,1)S(1)}, bf16[4096,128]{1,0:T(8,128)(2,1)S(1)}, u32[]{:S(2)}, u32[]{:S(2)}) collective-permute-start(bf16[4096,128]{1,0:T(8,128)(2,1)S(1)} %bitcast.24), channel_id=1, source_target_pairs={{0,32},{32,0},{64,96},{96,64},{128,160},{160,128},{192,224},{224,1... | collective-permute-start | bytes 3145736 | tf_op jit(solution)/shard_map/ppermute | solution.py:510
  18.5 1.9 collective-permute-start.1
  20.4 2.4 %collective-permute-start.2 = (bf16[128,4096]{1,0:T(8,128)(2,1)}, bf16[128,4096]{1,0:T(8,128)(2,1)S(1)}, u32[]{:S(2)}, u32[]{:S(2)}) collective-permute-start(bf16[128,4096]{1,0:T(8,128)(2,1)} %bitcast.28), channel_id=1, source_target_pairs={{0,32},{32,0},{64,96},{96,64},{128,160},{160,128},{192,224},{224,1... | collective-permute-start | bytes 3145736 | tf_op jit(solution)/shard_map/ppermute | solution.py:510
  22.8 1.0 copy-done.4
  23.8 1.0 copy-done.6
  24.8 0.5 collective-permute-done.2.refs_5_
  25.3 1.0 copy-done.8
  26.3 8.1 %all-to-all-done = bf16[8,192,512]{2,1,0:T(8,128)(2,1)S(1)} async-done(((bf16[8,192,512]{2,1,0:T(8,128)(2,1)}), bf16[8,192,512]{2,1,0:T(8,128)(2,1)S(1)}, u32[]{:S(2)}, u32[]{:S(2)}) %all-to-all-start) | async-done | bytes 1572896 | tf_op jit(solution)/shard_map/all_to_all | solution.py:483
  34.4 4.4 %collective-permute-start.3 = (bf16[1536,512]{1,0:T(8,128)(2,1)S(1)}, bf16[1536,512]{1,0:T(8,128)(2,1)S(1)}, u32[]{:S(2)}, u32[]{:S(2)}) collective-permute-start(bf16[1536,512]{1,0:T(8,128)(2,1)S(1)} %bitcast.17), channel_id=1, source_target_pairs={{0,32},{32,0},{64,96},{96,64},{128,160},{160,128},{192,224},{224,1... | collective-permute-start | bytes 4718600 | tf_op jit(solution)/shard_map/ppermute | solution.py:510
  38.8 3.0 %collective-permute-done.3.cross_ref = bf16[1536,512]{1,0:T(8,128)(2,1)S(1)} collective-permute-done((bf16[1536,512]{1,0:T(8,128)(2,1)S(1)}, bf16[1536,512]{1,0:T(8,128)(2,1)S(1)}, u32[]{:S(2)}, u32[]{:S(2)}) %collective-permute-start.3) | collective-permute-done | bytes 1572896 | tf_op jit(solution)/shard_map/ppermute | solution.py:510
  41.8 1.3 shard_map.181
  43.1 36.8 %all_to_all.35 = bf16[32,16,256]{2,1,0:T(8,128)(2,1)S(1)} all-to-all(bf16[32,16,256]{2,1,0:T(8,128)(2,1)S(1)} %bitcast.32), channel_id=1, replica_groups=mesh['ctx'=16,'exp'=32] {'exp'}, dimensions={0} | all-to-all | bytes 524288 | tf_op jit(solution)/shard_map/all_to_all | solution.py:483
  79.9 0.1 broadcast_in_dim.8
  80.1 33.8 %all_to_all.36.rows_ref = bf16[8,512,256]{2,1,0:T(8,128)(2,1)S(1)} all-to-all(bf16[8,512,256]{2,1,0:T(8,128)(2,1)S(1)} %broadcast_in_dim.8), channel_id=1, replica_groups={{0,64,128,192,256,320,384,448},{32,96,160,224,288,352,416,480},{1,65,12..., dimensions={0} | all-to-all | bytes 4194304 | tf_op jit(solution)/shard_map/all_to_all | solution.py:483
  114.0 4.0 %shard_map.182 = bf16[8,512,256]{2,1,0:T(8,128)(2,1)S(1)} custom-call(bf16[8,512,256]{2,1,0:T(8,128)(2,1)S(1)} %all_to_all.36.rows_ref, bf16[4096,128]{1,0:T(8,128)(2,1)S(1)} %bitcast.25, bf16[4096,128]{1,0:T(8,128)(2,1)S(1)} %copy-done.5, bf16[4096,128]{1,0:T(8,128)(2,1)S(1)} %bitcast.27, bf16[4096,128]{1,0:T(8,128)(2,1)S(1)} %copy-done.7, ...), custom_call_target="tpu_custom_call" | custom-call | tf_op jit(solution)/shard_map/pallas_call | solution.py:547
  118.0 26.2 %all_to_all.37.terms_ref = bf16[8,512,256]{2,1,0:T(8,128)(2,1)S(1)} all-to-all(bf16[8,512,256]{2,1,0:T(8,128)(2,1)S(1)} %shard_map.182), channel_id=1, replica_groups={{0,64,128,192,256,320,384,448},{32,96,160,224,288,352,416,480},{1,65,12..., dimensions={0} | all-to-all | bytes 4194304 | tf_op jit(solution)/shard_map/all_to_all | solution.py:483
  144.2 0.6 shard_map.183
  144.8 24.9 %all_to_all.38 = bf16[32,16,256]{2,1,0:T(8,128)(2,1)S(1)} all-to-all(bf16[32,16,256]{2,1,0:T(8,128)(2,1)S(1)} %bitcast.30), channel_id=1, replica_groups=mesh['ctx'=16,'exp'=32] {'exp'}, dimensions={0} | all-to-all | bytes 524288 | tf_op jit(solution)/shard_map/all_to_all | solution.py:483
  169.7 1.2 shard_map.184
  170.9 14.1 %all_to_all.39 = bf16[8,192,256]{2,1,0:T(8,128)(2,1)S(1)} all-to-all(bf16[8,192,256]{2,1,0:T(8,128)(2,1)S(1)} %get-tuple-element.53.stats_ref), channel_id=1, replica_groups={{0,64,128,192,256,320,384,448},{32,96,160,224,288,352,416,480},{1,65,12..., dimensions={0} | all-to-all | bytes 1572864 | tf_op jit(solution)/shard_map/all_to_all | solution.py:483
  185.0 9.3 %collective-permute-start.4 = (bf16[1536,256]{1,0:T(8,128)(2,1)S(1)}, bf16[1536,256]{1,0:T(8,128)(2,1)S(1)}, u32[]{:S(2)}, u32[]{:S(2)}) collective-permute-start(bf16[1536,256]{1,0:T(8,128)(2,1)S(1)} %bitcast.20), channel_id=1, source_target_pairs={{0,32},{32,0},{64,96},{96,64},{128,160},{160,128},{192,224},{224,1... | collective-permute-start | bytes 2359304 | tf_op jit(solution)/shard_map/ppermute | solution.py:510
  194.3 1.9 collective-permute-done.4.grad_cross_ref
  196.2 10.2 %shard_map.185 = (bf16[192,128]{1,0:T(8,128)(2,1)}, bf16[64,192]{1,0:T(8,128)(2,1)}, bf16[192,128]{1,0:T(8,128)(2,1)}, bf16[192,128]{1,0:T(8,128)(2,1)}, bf16[32,48,128]{2,1,0:T(8,128)(2,1)S(1)}) custom-call(s32[1]{0:T(128)} %bitcast.place_ref, bf16[1536,512]{1,0:T(8,128)(2,1)S(1)} %bitcast.19, bf16[1536,512]{1,0:T(8,128)(2,1)S(1)} %collective-permute-done.3.cross_ref, ...), custom_call_target="tpu_custom_call" | custom-call | tf_op jit(solution)/shard_map/pallas_call | solution.py:561
  206.4 28.9 %all_to_all.40.terms_ref = bf16[32,48,128]{2,1,0:T(8,128)(2,1)S(1)} all-to-all(bf16[32,48,128]{2,1,0:T(8,128)(2,1)S(1)} %get-tuple-element.67), channel_id=1, replica_groups=mesh['ctx'=16,'exp'=32] {'exp'}, dimensions={0} | all-to-all | bytes 786432 | tf_op jit(solution)/shard_map/all_to_all | solution.py:483
  235.3 0.9 shard_map.186
  (34 shorter events, 0.1 us)
Async XLA Ops:
  0.6 12.9 %copy-start = (bf16[1,4096,128]{2,1,0:T(8,128)(2,1)S(1)}, bf16[1,4096,128]{2,1,0:T(8,128)(2,1)}, u32[]{:S(2)}) copy-start(bf16[1,4096,128]{2,1,0:T(8,128)(2,1)} %param.22) | copy-start | bytes 3145732
  0.6 41.2 %copy-start.11 = (bf16[192,128]{1,0:T(8,128)(2,1)S(1)}, bf16[192,128]{1,0:T(8,128)(2,1)}, u32[]{:S(2)}) copy-start(bf16[192,128]{1,0:T(8,128)(2,1)} %cotangent_ref.3) | copy-start | bytes 147460
  0.7 41.1 %copy-start.10 = (bf16[192,128]{1,0:T(8,128)(2,1)S(1)}, bf16[192,128]{1,0:T(8,128)(2,1)}, u32[]{:S(2)}) copy-start(bf16[192,128]{1,0:T(8,128)(2,1)} %hidden_ref.3) | copy-start | bytes 147460
  0.7 0.9 copy-start.12
  1.6 0.8 copy-start.13
  2.4 0.8 copy-start.14
  3.1 0.8 copy-start.16
  3.9 0.7 copy-start.17
  4.6 37.2 %copy-start.15 = (f32[192,8]{0,1:T(8,128)S(1)}, f32[192,8]{0,1:T(8,128)}, u32[]{:S(2)}) copy-start(f32[192,8]{0,1:T(8,128)} %param.21) | copy-start | bytes 18436
  4.6 37.2 %copy-start.18 = (s32[192]{0:T(256)S(1)}, s32[192]{0:T(256)}, u32[]{:S(2)}) copy-start(s32[192]{0:T(256)} %param.20) | copy-start | bytes 2308
  4.6 37.2 %copy-start.19 = (f32[128]{0:T(128)S(1)}, f32[128]{0:T(128)}, u32[]{:S(2)}) copy-start(f32[128]{0:T(128)} %param.19) | copy-start | bytes 1540
  6.1 28.3 %all-to-all-start = ((bf16[8,192,512]{2,1,0:T(8,128)(2,1)}), bf16[8,192,512]{2,1,0:T(8,128)(2,1)S(1)}, u32[]{:S(2)}, u32[]{:S(2)}) async-start(bf16[8,192,512]{2,1,0:T(8,128)(2,1)} %get-tuple-element.41), calls=%async_computation | async-start | bytes 3145728 | tf_op jit(solution)/shard_map/all_to_all | solution.py:483
  13.6 9.3 %collective-permute-start = (bf16[4096,128]{1,0:T(8,128)(2,1)S(1)}, bf16[4096,128]{1,0:T(8,128)(2,1)S(1)}, u32[]{:S(2)}, u32[]{:S(2)}) collective-permute-start(bf16[4096,128]{1,0:T(8,128)(2,1)S(1)} %bitcast.24), channel_id=1, source_target_pairs={{0,32},{32,0},{64,96},{96,64},{128,160},{160,128},{192,224},{224,1... | collective-permute-start | bytes 3145736 | tf_op jit(solution)/shard_map/ppermute | solution.py:510
  18.5 5.3 %collective-permute-start.1 = (bf16[4096,128]{1,0:T(8,128)(2,1)}, bf16[4096,128]{1,0:T(8,128)(2,1)S(1)}, u32[]{:S(2)}, u32[]{:S(2)}) collective-permute-start(bf16[4096,128]{1,0:T(8,128)(2,1)} %bitcast.26), channel_id=1, source_target_pairs={{0,32},{32,0},{64,96},{96,64},{128,160},{160,128},{192,224},{224,1... | collective-permute-start | bytes 3145736 | tf_op jit(solution)/shard_map/ppermute | solution.py:510
  20.4 4.9 %collective-permute-start.2 = (bf16[128,4096]{1,0:T(8,128)(2,1)}, bf16[128,4096]{1,0:T(8,128)(2,1)S(1)}, u32[]{:S(2)}, u32[]{:S(2)}) collective-permute-start(bf16[128,4096]{1,0:T(8,128)(2,1)} %bitcast.28), channel_id=1, source_target_pairs={{0,32},{32,0},{64,96},{96,64},{128,160},{160,128},{192,224},{224,1... | collective-permute-start | bytes 3145736 | tf_op jit(solution)/shard_map/ppermute | solution.py:510
  22.8 1.0 copy-start.4
  23.8 1.0 copy-start.6
  25.3 1.0 copy-start.8
  34.4 7.4 %collective-permute-start.3 = (bf16[1536,512]{1,0:T(8,128)(2,1)S(1)}, bf16[1536,512]{1,0:T(8,128)(2,1)S(1)}, u32[]{:S(2)}, u32[]{:S(2)}) collective-permute-start(bf16[1536,512]{1,0:T(8,128)(2,1)S(1)} %bitcast.17), channel_id=1, source_target_pairs={{0,32},{32,0},{64,96},{96,64},{128,160},{160,128},{192,224},{224,1... | collective-permute-start | bytes 4718600 | tf_op jit(solution)/shard_map/ppermute | solution.py:510
  79.9 34.0 %copy-start.7 = (bf16[4096,128]{1,0:T(8,128)(2,1)S(1)}, bf16[4096,128]{1,0:T(8,128)(2,1)}, u32[]{:S(2)}) copy-start(bf16[4096,128]{1,0:T(8,128)(2,1)} %copy-done.6) | copy-start | bytes 3145732
  79.9 34.0 %copy-start.9 = (bf16[128,4096]{1,0:T(8,128)(2,1)S(1)}, bf16[128,4096]{1,0:T(8,128)(2,1)}, u32[]{:S(2)}) copy-start(bf16[128,4096]{1,0:T(8,128)(2,1)} %copy-done.8) | copy-start | bytes 3145732
  80.1 33.9 %copy-start.1 = (bf16[1,4096,128]{2,1,0:T(8,128)(2,1)S(1)}, bf16[1,4096,128]{2,1,0:T(8,128)(2,1)}, u32[]{:S(2)}) copy-start(bf16[1,4096,128]{2,1,0:T(8,128)(2,1)} %param.22) | copy-start | bytes 3145732
  80.1 33.9 %copy-start.2 = (bf16[1,4096,128]{2,1,0:T(8,128)(2,1)S(1)}, bf16[1,4096,128]{2,1,0:T(8,128)(2,1)}, u32[]{:S(2)}) copy-start(bf16[1,4096,128]{2,1,0:T(8,128)(2,1)} %param.23) | copy-start | bytes 3145732
  80.1 33.9 %copy-start.3 = (bf16[1,128,4096]{2,1,0:T(8,128)(2,1)S(1)}, bf16[1,128,4096]{2,1,0:T(8,128)(2,1)}, u32[]{:S(2)}) copy-start(bf16[1,128,4096]{2,1,0:T(8,128)(2,1)} %param.24) | copy-start | bytes 3145732
  80.1 33.9 %copy-start.5 = (bf16[4096,128]{1,0:T(8,128)(2,1)S(1)}, bf16[4096,128]{1,0:T(8,128)(2,1)}, u32[]{:S(2)}) copy-start(bf16[4096,128]{1,0:T(8,128)(2,1)} %copy-done.4) | copy-start | bytes 3145732
  185.0 11.2 %collective-permute-start.4 = (bf16[1536,256]{1,0:T(8,128)(2,1)S(1)}, bf16[1536,256]{1,0:T(8,128)(2,1)S(1)}, u32[]{:S(2)}, u32[]{:S(2)}) collective-permute-start(bf16[1536,256]{1,0:T(8,128)(2,1)S(1)} %bitcast.20), channel_id=1, source_target_pairs={{0,32},{32,0},{64,96},{96,64},{128,160},{160,128},{192,224},{224,1... | collective-permute-start | bytes 2359304 | tf_op jit(solution)/shard_map/ppermute | solution.py:510

commit v4 on v2

v4 whole, which is shorter than its diff:
```python
import functools
import math

import jax
import jax.numpy as jnp
from jax import lax
from jax.experimental import pallas as pl
from jax.experimental.pallas import tpu as pltpu
from jax.sharding import PartitionSpec as P

NOPE = 64
ROPE = 32
VDIM = 64
D = 4096
CAP = 12
SLOT = 16
LANES = 128

norm_eps = 1e-06
route_scale = 2.5
masked_low = -1e30
score_scale = 1.0 / math.sqrt(NOPE + ROPE)

bf16 = jnp.bfloat16
f32 = jnp.float32
MIB = 1024 * 1024

LEFT = slice(0, LANES)
RIGHT = slice(LANES, 2 * LANES)


def nt_dot(a, b):
    return lax.dot_general(a, b, (((1,), (1,)), ((), ())), preferred_element_type=f32)


def nn_dot(a, b):
    return jnp.dot(a, b, preferred_element_type=f32)


def lanes_of(shape):
    return lax.broadcasted_iota(jnp.int32, shape, len(shape) - 1)


def pieces_of(value, count):
    pieces = []
    for _ in range(count):
        piece = value.astype(bf16).astype(f32)
        pieces.append(piece)
        value = value - piece
    return pieces


def own_query(queries, head):
    rows = queries.shape[0]
    lane = lanes_of((rows, LANES))
    nope = jnp.where(lane // NOPE == head, queries[:, LEFT], jnp.zeros((rows, LANES), bf16))
    rot = queries[:, RIGHT].astype(f32)
    if head:
        rot = pltpu.roll(rot, LANES - head * ROPE, 1)
    rot = jnp.where(lane < ROPE, rot, 0.0).astype(bf16)
    return jnp.concatenate([nope, rot], 1)


def own_key(keys, head):
    rows = keys.shape[0]
    lane = lanes_of((rows, LANES))
    nope = jnp.where(lane // NOPE == head, keys[:, LEFT], jnp.zeros((rows, LANES), bf16))
    rot = keys[:, RIGHT].astype(f32)
    if head:
        rot = pltpu.roll(rot, head * ROPE, 1)
    return jnp.concatenate([nope, rot.astype(bf16)], 1)


def upright(narrow):
    count, rows = narrow.shape
    full = jnp.concatenate([narrow, jnp.zeros((LANES - count, rows), bf16)], 0)
    return nt_dot(unit_matrix(rows, rows), full).astype(bf16)


def keys_of(message, rows):
    rot = upright(message[rows : rows + ROPE, :][:, 0:rows])
    return jnp.concatenate([message[0:rows, LEFT], rot], 1)


def pair_places(rows, core):
    lane = lanes_of((rows, 2 * rows))
    return lane - jnp.where(lane >= rows, 2 * rows, 0) * core


def slots_along_rows(route_row, experts):
    count = route_row.shape[1]
    hits = (lax.broadcasted_iota(jnp.int32, (experts, count), 0) == route_row).astype(f32)
    before = lax.broadcasted_iota(jnp.int32, (count, count), 0) < lanes_of((count, count))
    ranks = nn_dot(hits.astype(bf16), before.astype(f32).astype(bf16))
    rank = jnp.sum(ranks * hits, 0, keepdims=True)
    return route_row * SLOT + rank.astype(jnp.int32)


def column_of(row):
    count = row.shape[1]
    shape = (count, count)
    match = lax.broadcasted_iota(jnp.int32, shape, 0) == lanes_of(shape)
    return jnp.sum(jnp.where(match, row, jnp.zeros_like(row)), 1, keepdims=True)


def unit_matrix(rows, columns, offset=0):
    shape = (rows, columns)
    match = lax.broadcasted_iota(jnp.int32, shape, 0) + offset == lanes_of(shape)
    return match.astype(f32).astype(bf16)


def slots_along_columns(route_row, experts):
    route_column = column_of(route_row)
    count = route_column.shape[0]
    hits = (lanes_of((count, experts)) == route_column).astype(f32)
    before = lanes_of((count, count)) < lax.broadcasted_iota(jnp.int32, (count, count), 0)
    ranks = nn_dot(before.astype(f32).astype(bf16), hits.astype(bf16))
    rank = jnp.sum(ranks * hits, 1, keepdims=True)
    return route_column * SLOT + rank.astype(jnp.int32)


def gate_share_of(affinity):
    return column_of(route_scale * affinity[0:1] / jnp.sum(affinity, 0, keepdims=True))


def pack_kernel(
    place_ref,
    key_nope_hbm,
    key_rope_hbm,
    query_rope_hbm,
    query_nope_hbm,
    values_hbm,
    gate_hbm,
    up_hbm,
    down_hbm,
    own_key_ref,
    own_query_ref,
    message_ref,
    weights_ref,
    key_nope_ref,
    key_rope_ref,
    query_rope_ref,
    query_nope_ref,
    values_ref,
    sems,
):
    pairs = (
        (key_rope_hbm, key_rope_ref),
        (query_rope_hbm, query_rope_ref),
        (key_nope_hbm, key_nope_ref),
        (values_hbm, values_ref),
        (query_nope_hbm, query_nope_ref),
    )
    copies = [
        pltpu.make_async_copy(source, target, sems.at[index])
        for index, (source, target) in enumerate(pairs)
    ]
    moves = [(gate_hbm, weights_ref.at[0:D, :]), (up_hbm, weights_ref.at[D : 2 * D, :])]
    for index in range(D // LANES):
        start = 2 * D + index * LANES
        source = down_hbm.at[:, index * LANES : (index + 1) * LANES]
        moves.append((source, weights_ref.at[start : start + LANES, :]))
    moves = [
        pltpu.make_async_copy(source, target, sems.at[len(pairs) + index])
        for index, (source, target) in enumerate(moves)
    ]
    for copy in copies + moves:
        copy.start()
    for copy in copies:
        copy.wait()
    rows = key_nope_ref.shape[0]
    place = place_ref[0]
    pair, core = place // 2, place % 2
    own_key_ref[:, LEFT] = key_nope_ref[...]
    own_key_ref[:, RIGHT] = upright(key_rope_ref[...])
    own_query_ref[:, LEFT] = query_nope_ref[...]
    own_query_ref[:, RIGHT] = upright(query_rope_ref[...])
    rot = jnp.concatenate([key_rope_ref[...], jnp.zeros((ROPE, 2 * LANES - rows), bf16)], 1)
    empty = jnp.zeros((ROPE, 2 * LANES), bf16)
    for index in range(message_ref.shape[0]):
        to_later = (index > pair) | ((index == pair) & (core == 0))

        @pl.when(to_later)
        def _():
            message_ref[index, 0:rows, LEFT] = key_nope_ref[...]
            message_ref[index, 0:rows, RIGHT] = values_ref[...]
            message_ref[index, rows:, :] = rot

        @pl.when(jnp.logical_not(to_later))
        def _():
            message_ref[index, 0:rows, :] = own_query_ref[...]
            message_ref[index, rows:, :] = empty

    for copy in moves:
        copy.wait()


def forward_kernel(
    experts,
    place_ref,
    same_ref,
    cross_ref,
    own_key_ref,
    own_query_ref,
    values_ref,
    hidden_ref,
    gain_ref,
    route_ref,
    affinity_ref,
    cotangent_ref,
    attended_ref,
    log_ref,
    send_ref,
    query_ref,
):
    rows = own_key_ref.shape[0]
    place = place_ref[0]
    pair, core = place // 2, place % 2
    for head in range(2):
        query_ref[head] = own_query(own_query_ref[...], head)

    cross = cross_ref[pair]
    keys = jnp.concatenate([own_key_ref[...], keys_of(cross, rows)], 0)
    vals = jnp.concatenate([values_ref[...], cross[0:rows, RIGHT]], 0)
    visible = pair_places(rows, core) <= lax.broadcasted_iota(jnp.int32, (rows, 2 * rows), 0)
    state = []
    for head in range(2):
        scores = jnp.where(visible, nt_dot(query_ref[head], keys) * score_scale, masked_low)
        top = jnp.max(scores, 1, keepdims=True)
        weights = jnp.where(visible, jnp.exp(scores - top), 0.0)
        total = jnp.sum(weights, 1, keepdims=True)
        state.extend([top, total, nn_dot(weights.astype(bf16), vals)])

    def step(index, state):
        same, cross = same_ref[index], cross_ref[index]
        keys = jnp.concatenate([keys_of(same, rows), keys_of(cross, rows)], 0)
        vals = jnp.concatenate([same[0:rows, RIGHT], cross[0:rows, RIGHT]], 0)
        after = []
        for head in range(2):
            top, total, mixed = state[3 * head : 3 * head + 3]
            scores = nt_dot(query_ref[head], keys) * score_scale
            new_top = jnp.maximum(top, jnp.max(scores, 1, keepdims=True))
            weights = jnp.exp(scores - new_top)
            factor = jnp.exp(top - new_top)
            total = total * factor + jnp.sum(weights, 1, keepdims=True)
            mixed = mixed * factor + nn_dot(weights.astype(bf16), vals)
            after.extend([new_top, total, mixed])
        return tuple(after)

    state = lax.fori_loop(0, pair, step, tuple(state))
    first = lanes_of((rows, LANES)) < VDIM
    attended = jnp.where(first, state[2] / state[1], state[5] / state[4]).astype(bf16)
    attended_ref[...] = attended
    log_ref[...] = jnp.where(
        first, state[0] + jnp.log(state[1]), state[3] + jnp.log(state[4])
    )
    hidden = hidden_ref[...].astype(f32) + attended.astype(f32)
    raised = (hidden * gain_ref[...]).astype(bf16)
    share = gate_share_of(affinity_ref[...])
    grad = (share * cotangent_ref[...].astype(f32)).astype(bf16)
    slots = slots_along_rows(route_ref[...], experts)
    table = lax.broadcasted_iota(jnp.int32, (experts * SLOT, rows), 0) == slots
    table = table.astype(f32).astype(bf16)
    row = lax.broadcasted_iota(jnp.int32, (SLOT, LANES), 0)
    gains = jnp.zeros((SLOT, LANES), f32)
    for index, piece in enumerate(pieces_of(gain_ref[...], 3)):
        gains = jnp.where(row == CAP + index, piece, gains)
    gains = jnp.broadcast_to(gains[None], (experts, SLOT, LANES)).reshape(-1, LANES)
    send_ref[:, 0:LANES] = (nn_dot(table, raised) + gains).astype(bf16)
    send_ref[:, LANES:] = nn_dot(table, grad).astype(bf16)


def gathered_rows(ref, count, slices, column):
    parts = []
    for index in range(slices):
        part = ref[:, index * SLOT : (index + 1) * SLOT, column : column + LANES]
        parts.append(part.reshape(count * SLOT, LANES))
    return jnp.concatenate(parts, 1)


def gain_of(raised):
    pieces = raised[CAP : CAP + 3].astype(f32)
    return pieces[0:1] + pieces[1:2] + pieces[2:3]


def inverse_of(raised, gain):
    hidden = raised.astype(f32) / gain
    return lax.rsqrt(jnp.sum(hidden * hidden, 1, keepdims=True) / D + norm_eps)


def expert_kernel(rows_ref, *refs):
    weight_refs, out_ref = refs[:-1], refs[-1]
    count, depth, _ = rows_ref.shape
    slices = depth // SLOT
    wide = 2 * LANES
    raised = gathered_rows(rows_ref, count, slices, 0)
    grad = gathered_rows(rows_ref, count, slices, LANES)
    inverse = inverse_of(raised, gain_of(raised[0:SLOT]))
    pairs = [weight_refs[at : at + 2] for at in range(0, len(weight_refs), 2)]

    def side_by_side(pair, base, index):
        at = slice(base + index * wide, base + (index + 1) * wide)
        return jnp.concatenate([pair[0][at, :], pair[1][at, :]], 1)

    def down_block(pair, index):
        at = 2 * D + index * wide
        halves = [
            jnp.concatenate([ref[at : at + LANES, :], ref[at + LANES : at + wide, :]], 1)
            for ref in pair
        ]
        return jnp.concatenate(halves, 0)

    made = []
    for pair in pairs:
        zero = jnp.zeros((count * SLOT, wide), f32)
        gate_val, up_val, grad_active = zero, zero, zero
        for index in range(slices // 2):
            at = slice(index * wide, (index + 1) * wide)
            gate_val = gate_val + nn_dot(raised[:, at], side_by_side(pair, 0, index))
            up_val = up_val + nn_dot(raised[:, at], side_by_side(pair, D, index))
            grad_active = grad_active + nt_dot(grad[:, at], down_block(pair, index))
        gate_val, up_val = inverse * gate_val, inverse * up_val
        sig = 1.0 / (1.0 + jnp.exp(-gate_val))
        silu = gate_val * sig
        active = (silu * up_val).astype(bf16)
        grad_gate = (grad_active * up_val * (sig * (1.0 + gate_val * (1.0 - sig)))).astype(bf16)
        grad_up = (grad_active * silu).astype(bf16)
        made.append((active, grad_gate, grad_up))
    for index in range(slices // 2):
        out = jnp.zeros((count * SLOT, wide), f32)
        back = jnp.zeros((count * SLOT, wide), f32)
        for pair, (active, grad_gate, grad_up) in zip(pairs, made):
            out = out + nn_dot(active, down_block(pair, index))
            back = back + nt_dot(grad_gate, side_by_side(pair, 0, index))
            back = back + nt_dot(grad_up, side_by_side(pair, D, index))
        out, back = out.astype(bf16), back.astype(bf16)
        for part in range(2):
            at = slice(part * LANES, (part + 1) * LANES)
            span = slice((2 * index + part) * SLOT, (2 * index + part + 1) * SLOT)
            out_ref[:, span, 0:LANES] = out[:, at].reshape(count, SLOT, LANES)
            out_ref[:, span, LANES:] = back[:, at].reshape(count, SLOT, LANES)


def reduce_kernel(terms_ref, rows_ref, out_ref):
    count, depth, _ = terms_ref.shape
    slices = depth // SLOT
    total = terms_ref[0].astype(f32)
    for index in range(1, count):
        total = total + terms_ref[index].astype(f32)
    raised = rows_ref[:, 0:LANES].astype(f32).reshape(slices, SLOT, LANES)
    back = total[:, LANES:].reshape(slices, SLOT, LANES)
    gain = jnp.sum(raised[:, CAP : CAP + 3, :], 1, keepdims=True)
    hidden = raised / gain
    squares = jnp.sum(jnp.sum(hidden * hidden, 0), 1, keepdims=True)
    inverse = lax.rsqrt(squares / D + norm_eps)
    cross = jnp.sum(jnp.sum(back * raised, 0), 1, keepdims=True) / D
    grad = inverse[None] * (back * gain - hidden * (inverse * inverse * cross)[None])
    row = lax.broadcasted_iota(jnp.int32, (slices, SLOT, LANES), 1)
    grad = jnp.where(row < CAP, grad, 0.0)
    out_ref[:, 0:LANES] = total[:, 0:LANES].astype(bf16)
    out_ref[:, LANES:] = grad.astype(bf16).reshape(depth, LANES)


def combine_kernel(
    experts,
    home_ref,
    hidden_ref,
    attended_ref,
    log_ref,
    route_ref,
    affinity_ref,
    cotangent_ref,
    layer_ref,
    grad_ref,
    stats_ref,
    message_ref,
):
    rows = hidden_ref.shape[0]
    slots = slots_along_columns(route_ref[...], experts)
    table = (lanes_of((rows, experts * SLOT)) == slots).astype(f32).astype(bf16)
    token = nn_dot(table, home_ref[...])
    attended = attended_ref[...].astype(f32)
    hidden = hidden_ref[...].astype(f32) + attended
    share = gate_share_of(affinity_ref[...])
    layer_ref[...] = (hidden + share * token[:, 0:LANES]).astype(bf16)
    grad = (cotangent_ref[...].astype(f32) + token[:, LANES:]).astype(bf16)
    grad_ref[...] = grad
    product = grad.astype(f32) * attended
    lane = lanes_of((rows, LANES))
    stats, pieces = jnp.zeros((rows, LANES), f32), jnp.zeros((rows, LANES), f32)
    for head in range(2):
        dot = jnp.sum(jnp.where(lane // VDIM == head, product, 0.0), 1, keepdims=True)
        log = log_ref[:, head * VDIM : head * VDIM + 1]
        stats = jnp.where(lane == 2 * head, dot, jnp.where(lane == 2 * head + 1, log, stats))
        for index, piece in enumerate(pieces_of(dot, 3) + pieces_of(log, 3)):
            pieces = jnp.where(lane == 6 * head + index, piece, pieces)
    stats_ref[...] = stats
    pieces = jnp.concatenate(
        [pieces.astype(bf16), jnp.zeros((2 * LANES - rows, LANES), bf16)], 0
    )
    lines = nt_dot(unit_matrix(SLOT, LANES), pieces).astype(bf16)
    for index in range(message_ref.shape[0]):
        message_ref[index, 0:rows, :] = grad
        message_ref[index, rows : rows + SLOT, :] = lines[:, LEFT]
        message_ref[index, rows + SLOT :, :] = lines[:, RIGHT]


def query_kernel(
    place_ref,
    same_ref,
    cross_ref,
    own_key_ref,
    own_query_ref,
    values_ref,
    grad_ref,
    stats_ref,
    query_nope_ref,
    query_rope_ref,
    query_ref,
    grads_ref,
    dq_ref,
):
    rows = own_key_ref.shape[0]
    place = place_ref[0]
    pair, core = place // 2, place % 2
    lane = lanes_of((rows, LANES))
    for head in range(2):
        query_ref[head] = own_query(own_query_ref[...], head)
        grads_ref[head] = jnp.where(
            lane // VDIM == head, grad_ref[...], jnp.zeros((rows, LANES), bf16)
        )

    def part(head, keys, vals, visible):
        dot = stats_ref[:, 2 * head : 2 * head + 1]
        log = stats_ref[:, 2 * head + 1 : 2 * head + 2]
        prob = jnp.exp(nt_dot(query_ref[head], keys) * score_scale - log)
        if visible is not None:
            prob = jnp.where(visible, prob, 0.0)
        grad_prob = nt_dot(grads_ref[head], vals)
        grad_score = (prob * (grad_prob - dot)).astype(bf16)
        return nn_dot(grad_score, keys)

    cross = cross_ref[pair]
    keys = jnp.concatenate([own_key_ref[...], keys_of(cross, rows)], 0)
    vals = jnp.concatenate([values_ref[...], cross[0:rows, RIGHT]], 0)
    visible = pair_places(rows, core) <= lax.broadcasted_iota(jnp.int32, (rows, 2 * rows), 0)
    for head in range(2):
        dq_ref[head] = part(head, keys, vals, visible)

    def step(index, carry):
        same, cross = same_ref[index], cross_ref[index]
        keys = jnp.concatenate([keys_of(same, rows), keys_of(cross, rows)], 0)
        vals = jnp.concatenate([same[0:rows, RIGHT], cross[0:rows, RIGHT]], 0)
        for head in range(2):
            dq_ref[head] += part(head, keys, vals, None)
        return carry

    lax.fori_loop(0, pair, step, 0)
    query_nope_ref[...] = (
        score_scale * jnp.where(lane < NOPE, dq_ref[0, :, LEFT], dq_ref[1, :, LEFT])
    ).astype(bf16)
    rot = jnp.where(lane < ROPE, dq_ref[0, :, RIGHT], pltpu.roll(dq_ref[1, :, RIGHT], ROPE, 1))
    rot = (score_scale * rot).astype(bf16)
    query_rope_ref[...] = nt_dot(unit_matrix(2 * ROPE, LANES), rot).astype(bf16)


def key_kernel(
    place_ref,
    same_ref,
    cross_ref,
    grad_same_ref,
    grad_cross_ref,
    own_key_ref,
    own_query_ref,
    values_ref,
    own_grad_ref,
    key_nope_ref,
    grad_values_ref,
    rope_ref,
    key_ref,
    vals_ref,
    dk_ref,
    dv_ref,
):
    rows = own_key_ref.shape[0]
    place = place_ref[0]
    pair, core = place // 2, place % 2
    lane = lanes_of((rows, LANES))
    for head in range(2):
        key_ref[head] = own_key(own_key_ref[...], head)
        vals_ref[head] = jnp.where(
            lane // VDIM == head, values_ref[...], jnp.zeros((rows, LANES), bf16)
        )

    def lines_of(first, second):
        zero = jnp.zeros((SLOT, LANES), f32)
        parts = []
        for message in (first, second):
            low = message[rows : rows + SLOT].astype(f32)
            high = message[rows + SLOT :].astype(f32)
            parts.append(jnp.concatenate([low, high, zero], 1))
        moved = pltpu.roll(parts[1], rows, 1)
        return jnp.where(lanes_of(moved.shape) < rows, parts[0], moved)

    def part(head, queries, grads, lines, visible):
        at = 6 * head
        dot = lines[at : at + 1] + lines[at + 1 : at + 2] + lines[at + 2 : at + 3]
        log = lines[at + 3 : at + 4] + lines[at + 4 : at + 5] + lines[at + 5 : at + 6]
        prob = jnp.exp(nt_dot(key_ref[head], queries) * score_scale - log)
        if visible is not None:
            prob = jnp.where(visible, prob, 0.0)
        grad_prob = nt_dot(vals_ref[head], grads)
        grad_score = (prob * (grad_prob - dot)).astype(bf16)
        return nn_dot(grad_score, queries), nn_dot(prob.astype(bf16), grads)

    def both(first, second, first_grad, second_grad, visible):
        queries = jnp.concatenate([first, second], 0)
        grads = jnp.concatenate([first_grad[0:rows], second_grad[0:rows]], 0)
        lines = lines_of(first_grad, second_grad)
        return [part(head, queries, grads, lines, visible) for head in range(2)]

    visible = pair_places(rows, core) >= lax.broadcasted_iota(jnp.int32, (rows, 2 * rows), 0)
    made = both(
        own_query_ref[...],
        cross_ref[pair][0:rows],
        own_grad_ref[0],
        grad_cross_ref[pair],
        visible,
    )
    for head in range(2):
        dk_ref[head], dv_ref[head] = made[head]

    def step(index, carry):
        made = both(
            same_ref[index][0:rows],
            cross_ref[index][0:rows],
            grad_same_ref[index],
            grad_cross_ref[index],
            None,
        )
        for head in range(2):
            dk_ref[head] += made[head][0]
            dv_ref[head] += made[head][1]
        return carry

    lax.fori_loop(pair + 1, same_ref.shape[0], step, 0)
    key_nope_ref[...] = (
        score_scale * jnp.where(lane < NOPE, dk_ref[0, :, LEFT], dk_ref[1, :, LEFT])
    ).astype(bf16)
    grad_values_ref[...] = jnp.where(lane < VDIM, dv_ref[0], dv_ref[1]).astype(bf16)
    shared = dk_ref[0, :, RIGHT] + pltpu.roll(dk_ref[1, :, RIGHT], LANES - ROPE, 1)
    quarter = rows // 4
    packed = jnp.zeros((quarter, LANES), f32)
    small = lanes_of((quarter, LANES))
    for index in range(4):
        piece = shared[index * quarter : (index + 1) * quarter]
        if index:
            piece = pltpu.roll(piece, index * ROPE, 1)
        packed = jnp.where(small // ROPE == index, piece, packed)
    packed = (score_scale * packed).astype(bf16)
    for index in range(rope_ref.shape[0]):
        rope_ref[index] = packed


def rope_kernel(terms_ref, out_ref):
    total = terms_ref[0].astype(f32)
    for index in range(1, terms_ref.shape[0]):
        total = total + terms_ref[index].astype(f32)
    total = total.astype(bf16)
    quarter = total.shape[0]
    out = jnp.zeros((ROPE, 4 * quarter), f32)
    for index in range(4):
        part = nt_dot(unit_matrix(ROPE, LANES, index * ROPE), total).astype(bf16)
        out = out + nn_dot(part, unit_matrix(quarter, 4 * quarter, index * quarter))
    out_ref[...] = out.astype(bf16)


def call(body, limit, outs, scratch=(), scalars=0, count=0, space=pltpu.VMEM):
    place = [pl.BlockSpec(memory_space=pltpu.SMEM)] * scalars
    return pl.pallas_call(
        body,
        out_shape=outs,
        in_specs=place + [pl.BlockSpec(memory_space=space)] * count,
        out_specs=jax.tree.map(lambda _: pl.BlockSpec(memory_space=pltpu.VMEM), outs),
        scratch_shapes=list(scratch),
        compiler_params=pltpu.CompilerParams(vmem_limit_bytes=limit * MIB),
    )


def shape_of(*dims, dtype=bf16):
    return jax.ShapeDtypeStruct(dims, dtype)


def held(value):
    return pltpu.with_memory_space_constraint(value, pltpu.HBM)


def exchange(blocks, axis, groups=None):
    return lax.all_to_all(blocks, axis, 0, 0, tiled=True, axis_index_groups=groups)


def per_device(
    hidden_in,
    query_nope,
    query_rope,
    key_nope,
    key_rope,
    values,
    norm_gain,
    expert_route,
    affinity,
    gate_weight,
    up_weight,
    down_weight,
    cotangent,
):
    rows, width = hidden_in.shape
    ctx_count, experts = lax.axis_size("ctx"), lax.axis_size("exp")
    half = ctx_count // 2
    by_core = [[core + 2 * index for index in range(half)] for core in range(2)]
    across = [(index, index ^ 1) for index in range(ctx_count)]
    depth = experts * SLOT
    quarter = rows // 4

    def swap(value):
        return lax.ppermute(value, "ctx", across)

    place = lax.axis_index("ctx").astype(jnp.int32).reshape(1)
    route = expert_route.reshape(1, rows)
    affinity = affinity.T
    tall = rows + ROPE
    own_key_rows, own_query_rows, messages, weights = call(
        pack_kernel,
        12,
        (
            shape_of(rows, 2 * width),
            shape_of(rows, 2 * width),
            shape_of(half, tall, 2 * width),
            shape_of(3 * D, LANES),
        ),
        [
            pltpu.VMEM((rows, width), bf16),
            pltpu.VMEM((ROPE, rows), bf16),
            pltpu.VMEM((2 * ROPE, rows), bf16),
            pltpu.VMEM((rows, width), bf16),
            pltpu.VMEM((rows, width), bf16),
            pltpu.SemaphoreType.DMA((7 + D // LANES,)),
        ],
        1,
        8,
        pltpu.HBM,
    )(
        place,
        *(held(value) for value in (key_nope, key_rope.T, query_rope.T, query_nope, values)),
        *(held(value[0]) for value in (gate_weight, up_weight, down_weight)),
    )
    own = (own_key_rows, own_query_rows, held(values))
    same = exchange(messages, "ctx", by_core)
    weights = (weights, swap(weights))
    same, weights = lax.optimization_barrier((same, weights))
    cross = swap(same)

    attended, logs, send = call(
        functools.partial(forward_kernel, experts),
        14,
        (shape_of(rows, width), shape_of(rows, width, dtype=f32), shape_of(depth, 2 * width)),
        [pltpu.VMEM((2, rows, 2 * width), bf16)],
        1,
        10,
    )(
        place,
        same,
        cross,
        *own,
        *(held(value) for value in (hidden_in, norm_gain.reshape(1, width))),
        *(held(value) for value in (route, affinity, cotangent)),
    )
    received = exchange(send.reshape(experts, SLOT, 2 * width), "exp").reshape(depth, 2 * width)
    copies = jnp.broadcast_to(received[None], (half, depth, 2 * width))
    rows_all = exchange(copies, "ctx", by_core)
    partial = call(expert_kernel, 28, shape_of(half, depth, 2 * width), count=3)(
        rows_all, *weights
    )
    terms = exchange(partial, "ctx", by_core)
    back = call(reduce_kernel, 10, shape_of(depth, 2 * width), count=2)(terms, received)
    home = exchange(back.reshape(experts, SLOT, 2 * width), "exp").reshape(depth, 2 * width)
    layer_out, grad_hidden, stats, messages = call(
        functools.partial(combine_kernel, experts),
        8,
        (
            shape_of(rows, width),
            shape_of(rows, width),
            shape_of(rows, width, dtype=f32),
            shape_of(half, tall, width),
        ),
        count=7,
    )(home, hidden_in, attended, logs, route, affinity, cotangent)
    grad_same = exchange(messages, "ctx", by_core)
    grad_cross = swap(grad_same)
    gk_nope, g_values, rope_part = call(
        key_kernel,
        14,
        (shape_of(rows, width), shape_of(rows, width), shape_of(experts, quarter, LANES)),
        [
            pltpu.VMEM((2, rows, 2 * width), bf16),
            pltpu.VMEM((2, rows, width), bf16),
            pltpu.VMEM((2, rows, 2 * width), f32),
            pltpu.VMEM((2, rows, width), f32),
        ],
        1,
        8,
    )(place, same, cross, grad_same, grad_cross, *own, messages)
    rope_terms = exchange(rope_part, "exp")
    gq_nope, gq_rope = call(
        query_kernel,
        14,
        (shape_of(rows, width), shape_of(2 * ROPE, rows)),
        [
            pltpu.VMEM((2, rows, 2 * width), bf16),
            pltpu.VMEM((2, rows, width), bf16),
            pltpu.VMEM((2, rows, 2 * width), f32),
        ],
        1,
        7,
    )(place, same, cross, *own, grad_hidden, stats)
    gk_rope = call(rope_kernel, 4, shape_of(ROPE, rows), count=1)(rope_terms)
    return (layer_out, grad_hidden, gq_nope, gq_rope.T, gk_nope, gk_rope.T, g_values)


def solution(mesh):
    placed = (
        P("ctx", "exp"),
        P("ctx", "exp"),
        P("ctx", "exp"),
        P("ctx", "exp"),
        P("ctx", None),
        P("ctx", "exp"),
        P("exp"),
        P("ctx"),
        P("ctx", None),
        P("exp", None, "ctx"),
        P("exp", None, "ctx"),
        P("exp", "ctx", None),
        P("ctx", "exp"),
    )
    return jax.shard_map(
        per_device,
        mesh=mesh,
        in_specs=placed,
        out_specs=(
            P("ctx", "exp"),
            P("ctx", "exp"),
            P("ctx", "exp"),
            P("ctx", "exp"),
            P("ctx", "exp"),
            P("ctx", None),
            P("ctx", "exp"),
        ),
        check_vma=False,
    )
```

time: 273 us -> 225 us (0.82)
  blocking collectives: 29.9 us -> 150 us
  waiting for transfers between devices: 107 us -> 26.9 us
  starting transfers between devices: 73.2 us -> 25.3 us
  local copies, waits for them, and re-layouts: 18.3 us -> 0.15 us
  other arithmetic: 16.4 us -> 0 us
  Pallas kernels: 25.9 us -> 21.3 us
    all_to_all x2 -> x6, blocking collectives: 29.9 us -> 150 us  [exchange(): lax.all_to_all(blocks, axis, 0, 0, tiled=True, axis_index_groups=groups)]
    all_to_all x5 -> x1, waiting for transfers between devices: 102 us -> 23.4 us  [exchange(): lax.all_to_all(blocks, axis, 0, 0, tiled=True, axis_index_groups=groups)]
    all_to_all x5 -> x1, starting transfers between devices: 49.2 us -> 3.88 us  [exchange(): lax.all_to_all(blocks, axis, 0, 0, tiled=True, axis_index_groups=groups)]
    concatenate x1 -> x0, other arithmetic: 16.4 us -> none  [per_device(): weights = [jnp.concatenate([gate_weight[0], up_weight[0], down], 0)]]
    unnamed x38 -> x10, local copies, waits for them, and re-layouts: 12.7 us -> 0.02 us
    pallas_call x4 -> x6, Pallas kernels: 23.3 us -> 18.5 us  [the longest x1 7.57 us: per_device(): call(key_kernel, 14, (shape_of(rows, width), shape_of(rows, width), shape...]
    broadcast_in_dim x5 -> x1, local copies, waits for them, and re-layouts: 4.16 us -> 0.14 us  [per_device(): copies = jnp.broadcast_to(received[None], (half, depth, 2 * width))]
    ppermute x5 -> x3, starting transfers between devices: 24 us -> 21.4 us  [swap(): return lax.ppermute(value, 'ctx', across)]
  transfers between devices with their start and end apart: 10 -> 4, of which waited for: 7 -> 3; matrix products, arithmetic and copies ran while one was open for 8% -> 0% of each run, Pallas kernels for 0% -> 1%
where the time goes in v4:
time: 225 us
  blocking collectives  150 us (67%)
  waiting for transfers between devices  26.9 us (12%)
  starting transfers between devices  25.3 us (11%)
  Pallas kernels  21.3 us (9%)
    all_to_all x6, blocking collectives, exchange(): lax.all_to_all(blocks, axis, 0, 0, tiled=True, axis_index_groups=groups)  150 us
    all_to_all x1, waiting for transfers between devices, exchange(): lax.all_to_all(blocks, axis, 0, 0, tiled=True, axis_index_groups=groups)  23.4 us
    ppermute x3, starting transfers between devices, swap(): return lax.ppermute(value, 'ctx', across)  21.4 us
    pallas_call x1, Pallas kernels, per_device(): call(key_kernel, 14, (shape_of(rows, width), shape_of(rows, width), shape...  7.57 us
  transfers between devices with their start and end apart: 4, of which 3 were waited for; matrix products, arithmetic and copies ran while one was open for 0% of the time, Pallas kernels for 1%

profile of v4, /device:TPU:1, one launch (start us, length us, event | category | flops | bytes accessed | tf_op | source)
XLA Modules:
  0.0 224.6 jit_solution(14242222179911038818)
XLA Ops:
  0.6 2.2 shard_map.180
  2.8 8.8 %collective-permute-start = (bf16[12288,128]{1,0:T(8,128)(2,1)S(1)}, bf16[12288,128]{1,0:T(8,128)(2,1)S(1)}, u32[]{:S(2)}, u32[]{:S(2)}) collective-permute-start(bf16[12288,128]{1,0:T(8,128)(2,1)S(1)} %get-tuple-element.32.refs_0_), channel_id=1, source_target_pairs={{0,32},{32,0},{64,96},{96,64},{128,160},{160,128},{192,224},{224,1... | collective-permute-start | bytes 9437192 | tf_op jit(solution)/shard_map/ppermute | solution.py:626
  11.6 17.6 %all_to_all.35.same_ref = bf16[8,224,256]{2,1,0:T(8,128)(2,1)S(1)} all-to-all(bf16[8,224,256]{2,1,0:T(8,128)(2,1)S(1)} %get-tuple-element.26), channel_id=1, replica_groups={{0,64,128,192,256,320,384,448},{32,96,160,224,288,352,416,480},{1,65,12..., dimensions={0} | all-to-all | bytes 1835008 | tf_op jit(solution)/shard_map/all_to_all | solution.py:599
  29.3 0.0 collective-permute-done.refs_1_
  29.3 3.2 %collective-permute-start.1 = (bf16[8,224,256]{2,1,0:T(8,128)(2,1)S(1)}, bf16[8,224,256]{2,1,0:T(8,128)(2,1)S(1)}, u32[]{:S(2)}, u32[]{:S(2)}) collective-permute-start(bf16[8,224,256]{2,1,0:T(8,128)(2,1)S(1)} %all_to_all.35.same_ref), channel_id=1, source_target_pairs={{0,32},{32,0},{64,96},{96,64},{128,160},{160,128},{192,224},{224,1... | collective-permute-start | bytes 2752520 | tf_op jit(solution)/shard_map/ppermute | solution.py:626
  32.4 2.1 collective-permute-done.1.cross_ref
  34.5 2.3 %shard_map.181 = (bf16[192,128]{1,0:T(8,128)(2,1)S(1)}, f32[192,128]{1,0:T(8,128)S(1)}, bf16[512,256]{1,0:T(8,128)(2,1)S(1)}) custom-call(s32[1]{0:T(128)} %bitcast.place_ref, bf16[8,224,256]{2,1,0:T(8,128)(2,1)S(1)} %all_to_all.35.same_ref, bf16[8,224,256]{2,1,0:T(8,128)(2,1)S(1)} %collective-permute-done.1.cross_ref, ...), custom_call_target="tpu_custom_call" | custom-call | tf_op jit(solution)/shard_map/pallas_call | solution.py:663
  36.8 34.2 %all_to_all.36 = bf16[32,16,256]{2,1,0:T(8,128)(2,1)S(1)} all-to-all(bf16[32,16,256]{2,1,0:T(8,128)(2,1)S(1)} %bitcast.19), channel_id=1, replica_groups=mesh['ctx'=16,'exp'=32] {'exp'}, dimensions={0} | all-to-all | bytes 524288 | tf_op jit(solution)/shard_map/all_to_all | solution.py:599
  71.0 0.1 broadcast_in_dim.8
  71.2 34.8 %all_to_all.37.rows_ref = bf16[8,512,256]{2,1,0:T(8,128)(2,1)S(1)} all-to-all(bf16[8,512,256]{2,1,0:T(8,128)(2,1)S(1)} %broadcast_in_dim.8), channel_id=1, replica_groups={{0,64,128,192,256,320,384,448},{32,96,160,224,288,352,416,480},{1,65,12..., dimensions={0} | all-to-all | bytes 4194304 | tf_op jit(solution)/shard_map/all_to_all | solution.py:599
  106.0 4.0 %shard_map.182 = bf16[8,512,256]{2,1,0:T(8,128)(2,1)S(1)} custom-call(bf16[8,512,256]{2,1,0:T(8,128)(2,1)S(1)} %all_to_all.37.rows_ref, bf16[12288,128]{1,0:T(8,128)(2,1)S(1)} %get-tuple-element.32.refs_0_, bf16[12288,128]{1,0:T(8,128)(2,1)S(1)} %collective-permute-done.refs_1_), custom_call_target="tpu_custom_call" | custom-call | tf_op jit(solution)/shard_map/pallas_call | solution.py:681
  110.0 26.2 %all_to_all.38.terms_ref = bf16[8,512,256]{2,1,0:T(8,128)(2,1)S(1)} all-to-all(bf16[8,512,256]{2,1,0:T(8,128)(2,1)S(1)} %shard_map.182), channel_id=1, replica_groups={{0,64,128,192,256,320,384,448},{32,96,160,224,288,352,416,480},{1,65,12..., dimensions={0} | all-to-all | bytes 4194304 | tf_op jit(solution)/shard_map/all_to_all | solution.py:599
  136.2 0.0 copy-start
  136.2 0.0 copy-start.1
  136.2 0.0 copy-start.3
  136.2 0.0 copy-start.4
  136.2 0.6 shard_map.183
  136.8 24.9 %all_to_all.39 = bf16[32,16,256]{2,1,0:T(8,128)(2,1)S(1)} all-to-all(bf16[32,16,256]{2,1,0:T(8,128)(2,1)S(1)} %bitcast.17), channel_id=1, replica_groups=mesh['ctx'=16,'exp'=32] {'exp'}, dimensions={0} | all-to-all | bytes 524288 | tf_op jit(solution)/shard_map/all_to_all | solution.py:599
  161.7 0.0 copy-done
  161.7 0.0 copy-done.1
  161.7 0.0 copy-done.3
  161.7 0.0 copy-done.4
  161.7 1.3 shard_map.184
  163.0 12.4 %all_to_all.40.grad_same_ref = bf16[8,224,128]{2,1,0:T(8,128)(2,1)S(1)} all-to-all(bf16[8,224,128]{2,1,0:T(8,128)(2,1)S(1)} %get-tuple-element.41.own_grad_ref), channel_id=1, replica_groups={{0,64,128,192,256,320,384,448},{32,96,160,224,288,352,416,480},{1,65,12..., dimensions={0} | all-to-all | bytes 917504 | tf_op jit(solution)/shard_map/all_to_all | solution.py:599
  175.4 9.4 %collective-permute-start.2 = (bf16[8,224,128]{2,1,0:T(8,128)(2,1)S(1)}, bf16[8,224,128]{2,1,0:T(8,128)(2,1)S(1)}, u32[]{:S(2)}, u32[]{:S(2)}) collective-permute-start(bf16[8,224,128]{2,1,0:T(8,128)(2,1)S(1)} %all_to_all.40.grad_same_ref), channel_id=1, source_target_pairs={{0,32},{32,0},{64,96},{96,64},{128,160},{160,128},{192,224},{224,1... | collective-permute-start | bytes 1376264 | tf_op jit(solution)/shard_map/ppermute | solution.py:626
  184.9 1.4 collective-permute-done.2.grad_cross_ref
  186.3 7.6 %shard_map.186 = (bf16[192,128]{1,0:T(8,128)(2,1)}, bf16[192,128]{1,0:T(8,128)(2,1)}, bf16[32,48,128]{2,1,0:T(8,128)(2,1)}) custom-call(s32[1]{0:T(128)} %bitcast.place_ref, bf16[8,224,256]{2,1,0:T(8,128)(2,1)S(1)} %all_to_all.35.same_ref, bf16[8,224,256]{2,1,0:T(8,128)(2,1)S(1)} %collective-permute-done.1.cross_ref, ...), custom_call_target="tpu_custom_call" | custom-call | tf_op jit(solution)/shard_map/pallas_call | solution.py:700
  193.9 3.9 %all-to-all-start.6 = ((bf16[32,48,128]{2,1,0:T(8,128)(2,1)}), bf16[32,48,128]{2,1,0:T(8,128)(2,1)S(1)}, u32[]{:S(2)}, u32[]{:S(2)}) async-start(bf16[32,48,128]{2,1,0:T(8,128)(2,1)} %get-tuple-element.43), calls=%async_computation.6 | async-start | bytes 786432 | tf_op jit(solution)/shard_map/all_to_all | solution.py:599
  197.7 0.0 copy-done.2
  197.8 2.5 %shard_map.185 = (bf16[192,128]{1,0:T(8,128)(2,1)}, bf16[64,192]{1,0:T(8,128)(2,1)}) custom-call(s32[1]{0:T(128)} %bitcast.place_ref, bf16[8,224,256]{2,1,0:T(8,128)(2,1)S(1)} %all_to_all.35.same_ref, bf16[8,224,256]{2,1,0:T(8,128)(2,1)S(1)} %collective-permute-done.1.cross_ref, bf16[192,256]{1,0:T(8,128)(2,1)S(1)} %get-tuple-element.29.own_key_ref, ...), custom_call_target="tpu_custom_call" | custom-call | tf_op jit(solution)/shard_map/pallas_call | solution.py:714
  200.3 23.4 %all-to-all-done.6.terms_ref = bf16[32,48,128]{2,1,0:T(8,128)(2,1)S(1)} async-done(((bf16[32,48,128]{2,1,0:T(8,128)(2,1)}), bf16[32,48,128]{2,1,0:T(8,128)(2,1)S(1)}, u32[]{:S(2)}, u32[]{:S(2)}) %all-to-all-start.6) | async-done | bytes 393248 | tf_op jit(solution)/shard_map/all_to_all | solution.py:599
  223.7 0.9 shard_map.187
  (1 shorter events, 0.0 us)
Async XLA Ops:
  2.8 26.4 %collective-permute-start = (bf16[12288,128]{1,0:T(8,128)(2,1)S(1)}, bf16[12288,128]{1,0:T(8,128)(2,1)S(1)}, u32[]{:S(2)}, u32[]{:S(2)}) collective-permute-start(bf16[12288,128]{1,0:T(8,128)(2,1)S(1)} %get-tuple-element.32.refs_0_), channel_id=1, source_target_pairs={{0,32},{32,0},{64,96},{96,64},{128,160},{160,128},{192,224},{224,1... | collective-permute-start | bytes 9437192 | tf_op jit(solution)/shard_map/ppermute | solution.py:626
  29.3 5.3 %collective-permute-start.1 = (bf16[8,224,256]{2,1,0:T(8,128)(2,1)S(1)}, bf16[8,224,256]{2,1,0:T(8,128)(2,1)S(1)}, u32[]{:S(2)}, u32[]{:S(2)}) collective-permute-start(bf16[8,224,256]{2,1,0:T(8,128)(2,1)S(1)} %all_to_all.35.same_ref), channel_id=1, source_target_pairs={{0,32},{32,0},{64,96},{96,64},{128,160},{160,128},{192,224},{224,1... | collective-permute-start | bytes 2752520 | tf_op jit(solution)/shard_map/ppermute | solution.py:626
  136.2 25.5 %copy-start = (bf16[192,128]{1,0:T(8,128)(2,1)S(1)}, bf16[192,128]{1,0:T(8,128)(2,1)}, u32[]{:S(2)}) copy-start(bf16[192,128]{1,0:T(8,128)(2,1)} %hidden_ref.3) | copy-start | bytes 147460
  136.2 25.5 %copy-start.1 = (bf16[192,128]{1,0:T(8,128)(2,1)S(1)}, bf16[192,128]{1,0:T(8,128)(2,1)}, u32[]{:S(2)}) copy-start(bf16[192,128]{1,0:T(8,128)(2,1)} %cotangent_ref.3) | copy-start | bytes 147460
  136.2 25.5 %copy-start.3 = (f32[192,8]{0,1:T(8,128)S(1)}, f32[192,8]{0,1:T(8,128)}, u32[]{:S(2)}) copy-start(f32[192,8]{0,1:T(8,128)} %param.21) | copy-start | bytes 18436
  136.2 25.5 %copy-start.4 = (s32[192]{0:T(256)S(1)}, s32[192]{0:T(256)}, u32[]{:S(2)}) copy-start(s32[192]{0:T(256)} %param.20) | copy-start | bytes 2308
  175.4 22.3 %copy-start.2 = (bf16[192,128]{1,0:T(8,128)(2,1)S(1)}, bf16[192,128]{1,0:T(8,128)(2,1)}, u32[]{:S(2)}) copy-start(bf16[192,128]{1,0:T(8,128)(2,1)} %get-tuple-element.20.grad_ref) | copy-start | bytes 147460
  175.4 10.9 %collective-permute-start.2 = (bf16[8,224,128]{2,1,0:T(8,128)(2,1)S(1)}, bf16[8,224,128]{2,1,0:T(8,128)(2,1)S(1)}, u32[]{:S(2)}, u32[]{:S(2)}) collective-permute-start(bf16[8,224,128]{2,1,0:T(8,128)(2,1)S(1)} %all_to_all.40.grad_same_ref), channel_id=1, source_target_pairs={{0,32},{32,0},{64,96},{96,64},{128,160},{160,128},{192,224},{224,1... | collective-permute-start | bytes 1376264 | tf_op jit(solution)/shard_map/ppermute | solution.py:626
  193.9 29.8 %all-to-all-start.6 = ((bf16[32,48,128]{2,1,0:T(8,128)(2,1)}), bf16[32,48,128]{2,1,0:T(8,128)(2,1)S(1)}, u32[]{:S(2)}, u32[]{:S(2)}) async-start(bf16[32,48,128]{2,1,0:T(8,128)(2,1)} %get-tuple-element.43), calls=%async_computation.6 | async-start | bytes 786432 | tf_op jit(solution)/shard_map/all_to_all | solution.py:599

commit v5 on v4

--- a/solution.py
+++ b/solution.py
@@ -13,7 +13,9 @@
 VDIM = 64
 D = 4096
 CAP = 12
-SLOT = 16
+PAIR = 2 * CAP
+TALL = 32
+LINES = 16
 LANES = 128
 
 norm_eps = 1e-06
@@ -93,7 +95,7 @@
     before = lax.broadcasted_iota(jnp.int32, (count, count), 0) < lanes_of((count, count))
     ranks = nn_dot(hits.astype(bf16), before.astype(f32).astype(bf16))
     rank = jnp.sum(ranks * hits, 0, keepdims=True)
-    return route_row * SLOT + rank.astype(jnp.int32)
+    return route_row * TALL + rank.astype(jnp.int32)
 
 
 def column_of(row):
@@ -116,7 +118,7 @@
     before = lanes_of((count, count)) < lax.broadcasted_iota(jnp.int32, (count, count), 0)
     ranks = nn_dot(before.astype(f32).astype(bf16), hits.astype(bf16))
     rank = jnp.sum(ranks * hits, 1, keepdims=True)
-    return route_column * SLOT + rank.astype(jnp.int32)
+    return route_column * PAIR + rank.astype(jnp.int32)
 
 
 def gate_share_of(affinity):
@@ -211,43 +213,43 @@
     attended_ref,
     log_ref,
     send_ref,
-    query_ref,
+    all_keys_ref,
+    all_vals_ref,
+    scores_ref,
 ):
     rows = own_key_ref.shape[0]
     place = place_ref[0]
     pair, core = place // 2, place % 2
-    for head in range(2):
-        query_ref[head] = own_query(own_query_ref[...], head)
-
-    cross = cross_ref[pair]
-    keys = jnp.concatenate([own_key_ref[...], keys_of(cross, rows)], 0)
-    vals = jnp.concatenate([values_ref[...], cross[0:rows, RIGHT]], 0)
-    visible = pair_places(rows, core) <= lax.broadcasted_iota(jnp.int32, (rows, 2 * rows), 0)
+    count = same_ref.shape[0]
+    for index in range(count):
+        for part, ref in enumerate((same_ref, cross_ref)):
+            at = slice(part * rows, (part + 1) * rows)
+            rot = ref[index, rows : rows + ROPE, :][:, 0:rows]
+            all_keys_ref[index, at, LEFT] = ref[index, 0:rows, LEFT]
+            all_keys_ref[index, at, RIGHT] = upright(rot)
+            all_vals_ref[index, at, :] = ref[index, 0:rows, RIGHT]
+    all_keys_ref[pair, 0:rows, :] = own_key_ref[...]
+    all_vals_ref[pair, 0:rows, :] = values_ref[...]
+    queries = [own_query(own_query_ref[...], head) for head in range(2)]
+    ahead = pair_places(rows, core) - lax.broadcasted_iota(jnp.int32, (rows, 2 * rows), 0)
+    tops = [None, None]
+    for index in range(count):
+        visible = ahead <= (pair - index) * (2 * rows)
+        for head in range(2):
+            scores = nt_dot(queries[head], all_keys_ref[index]) * score_scale
+            scores = jnp.where(visible, scores, masked_low)
+            scores_ref[head, index] = scores
+            tops[head] = scores if index == 0 else jnp.maximum(tops[head], scores)
     state = []
     for head in range(2):
-        scores = jnp.where(visible, nt_dot(query_ref[head], keys) * score_scale, masked_low)
-        top = jnp.max(scores, 1, keepdims=True)
-        weights = jnp.where(visible, jnp.exp(scores - top), 0.0)
-        total = jnp.sum(weights, 1, keepdims=True)
-        state.extend([top, total, nn_dot(weights.astype(bf16), vals)])
-
-    def step(index, state):
-        same, cross = same_ref[index], cross_ref[index]
-        keys = jnp.concatenate([keys_of(same, rows), keys_of(cross, rows)], 0)
-        vals = jnp.concatenate([same[0:rows, RIGHT], cross[0:rows, RIGHT]], 0)
-        after = []
-        for head in range(2):
-            top, total, mixed = state[3 * head : 3 * head + 3]
-            scores = nt_dot(query_ref[head], keys) * score_scale
-            new_top = jnp.maximum(top, jnp.max(scores, 1, keepdims=True))
-            weights = jnp.exp(scores - new_top)
-            factor = jnp.exp(top - new_top)
-            total = total * factor + jnp.sum(weights, 1, keepdims=True)
-            mixed = mixed * factor + nn_dot(weights.astype(bf16), vals)
-            after.extend([new_top, total, mixed])
-        return tuple(after)
-
-    state = lax.fori_loop(0, pair, step, tuple(state))
+        top = jnp.max(tops[head], 1, keepdims=True)
+        total = jnp.zeros((rows, 2 * rows), f32)
+        mixed = jnp.zeros((rows, LANES), f32)
+        for index in range(count):
+            weights = jnp.exp(scores_ref[head, index] - top)
+            total = total + weights
+            mixed = mixed + nn_dot(weights.astype(bf16), all_vals_ref[index])
+        state.extend([top, jnp.sum(total, 1, keepdims=True), mixed])
     first = lanes_of((rows, LANES)) < VDIM
     attended = jnp.where(first, state[2] / state[1], state[5] / state[4]).astype(bf16)
     attended_ref[...] = attended
@@ -259,106 +261,88 @@
     share = gate_share_of(affinity_ref[...])
     grad = (share * cotangent_ref[...].astype(f32)).astype(bf16)
     slots = slots_along_rows(route_ref[...], experts)
-    table = lax.broadcasted_iota(jnp.int32, (experts * SLOT, rows), 0) == slots
-    table = table.astype(f32).astype(bf16)
-    row = lax.broadcasted_iota(jnp.int32, (SLOT, LANES), 0)
-    gains = jnp.zeros((SLOT, LANES), f32)
+    line = lax.broadcasted_iota(jnp.int32, (experts * TALL, rows), 0)
+    raised_table = (line == slots).astype(f32).astype(bf16)
+    grad_table = (line == slots + CAP).astype(f32).astype(bf16)
+    row = lax.broadcasted_iota(jnp.int32, (TALL, LANES), 0)
+    gains = jnp.zeros((TALL, LANES), f32)
     for index, piece in enumerate(pieces_of(gain_ref[...], 3)):
-        gains = jnp.where(row == CAP + index, piece, gains)
-    gains = jnp.broadcast_to(gains[None], (experts, SLOT, LANES)).reshape(-1, LANES)
-    send_ref[:, 0:LANES] = (nn_dot(table, raised) + gains).astype(bf16)
-    send_ref[:, LANES:] = nn_dot(table, grad).astype(bf16)
-
-
-def gathered_rows(ref, count, slices, column):
-    parts = []
-    for index in range(slices):
-        part = ref[:, index * SLOT : (index + 1) * SLOT, column : column + LANES]
-        parts.append(part.reshape(count * SLOT, LANES))
-    return jnp.concatenate(parts, 1)
-
-
-def gain_of(raised):
-    pieces = raised[CAP : CAP + 3].astype(f32)
-    return pieces[0:1] + pieces[1:2] + pieces[2:3]
-
-
-def inverse_of(raised, gain):
-    hidden = raised.astype(f32) / gain
-    return lax.rsqrt(jnp.sum(hidden * hidden, 1, keepdims=True) / D + norm_eps)
-
-
-def expert_kernel(rows_ref, *refs):
-    weight_refs, out_ref = refs[:-1], refs[-1]
-    count, depth, _ = rows_ref.shape
-    slices = depth // SLOT
+        gains = jnp.where(row == PAIR + index, piece, gains)
+    gains = jnp.broadcast_to(gains[None], (experts, TALL, LANES)).reshape(-1, LANES)
+    sent = nn_dot(raised_table, raised) + nn_dot(grad_table, grad) + gains
+    send_ref[...] = sent.astype(bf16)
+
+
+def unfold_kernel(received_ref, rows_ref, own_ref, gain_ref):
+    for index in range(received_ref.shape[0] // TALL):
+        at = slice(index * LANES, (index + 1) * LANES)
+        start = index * TALL
+        tile = received_ref[start : start + PAIR, :]
+        own_ref[:, at] = tile
+        for copy in range(rows_ref.shape[0]):
+            rows_ref[copy, :, at] = tile
+        pieces = received_ref[start : start + TALL, :].astype(f32)[PAIR : PAIR + 3]
+        gain_ref[:, at] = pieces[0:1] + pieces[1:2] + pieces[2:3]
+
+
+def expert_kernel(rows_ref, gain_ref, own_ref, other_ref, out_ref):
+    count = rows_ref.shape[0]
     wide = 2 * LANES
-    raised = gathered_rows(rows_ref, count, slices, 0)
-    grad = gathered_rows(rows_ref, count, slices, LANES)
-    inverse = inverse_of(raised, gain_of(raised[0:SLOT]))
-    pairs = [weight_refs[at : at + 2] for at in range(0, len(weight_refs), 2)]
-
-    def side_by_side(pair, base, index):
+    refs = (own_ref, other_ref)
+
+    def side_by_side(base, index):
         at = slice(base + index * wide, base + (index + 1) * wide)
-        return jnp.concatenate([pair[0][at, :], pair[1][at, :]], 1)
-
-    def down_block(pair, index):
+        return jnp.concatenate([ref[at, :] for ref in refs], 1)
+
+    def down_block(index):
         at = 2 * D + index * wide
         halves = [
             jnp.concatenate([ref[at : at + LANES, :], ref[at + LANES : at + wide, :]], 1)
-            for ref in pair
+            for ref in refs
         ]
         return jnp.concatenate(halves, 0)
 
-    made = []
-    for pair in pairs:
-        zero = jnp.zeros((count * SLOT, wide), f32)
-        gate_val, up_val, grad_active = zero, zero, zero
-        for index in range(slices // 2):
-            at = slice(index * wide, (index + 1) * wide)
-            gate_val = gate_val + nn_dot(raised[:, at], side_by_side(pair, 0, index))
-            up_val = up_val + nn_dot(raised[:, at], side_by_side(pair, D, index))
-            grad_active = grad_active + nt_dot(grad[:, at], down_block(pair, index))
-        gate_val, up_val = inverse * gate_val, inverse * up_val
-        sig = 1.0 / (1.0 + jnp.exp(-gate_val))
-        silu = gate_val * sig
-        active = (silu * up_val).astype(bf16)
-        grad_gate = (grad_active * up_val * (sig * (1.0 + gate_val * (1.0 - sig)))).astype(bf16)
-        grad_up = (grad_active * silu).astype(bf16)
-        made.append((active, grad_gate, grad_up))
-    for index in range(slices // 2):
-        out = jnp.zeros((count * SLOT, wide), f32)
-        back = jnp.zeros((count * SLOT, wide), f32)
-        for pair, (active, grad_gate, grad_up) in zip(pairs, made):
-            out = out + nn_dot(active, down_block(pair, index))
-            back = back + nt_dot(grad_gate, side_by_side(pair, 0, index))
-            back = back + nt_dot(grad_up, side_by_side(pair, D, index))
-        out, back = out.astype(bf16), back.astype(bf16)
-        for part in range(2):
-            at = slice(part * LANES, (part + 1) * LANES)
-            span = slice((2 * index + part) * SLOT, (2 * index + part + 1) * SLOT)
-            out_ref[:, span, 0:LANES] = out[:, at].reshape(count, SLOT, LANES)
-            out_ref[:, span, LANES:] = back[:, at].reshape(count, SLOT, LANES)
-
-
-def reduce_kernel(terms_ref, rows_ref, out_ref):
-    count, depth, _ = terms_ref.shape
-    slices = depth // SLOT
+    zero = jnp.zeros((count, wide), f32)
+    gate_val, up_val, grad_active, squares = zero, zero, zero, zero
+    for index in range(D // wide):
+        at = slice(index * wide, (index + 1) * wide)
+        rows = rows_ref[:, at]
+        hidden = rows.astype(f32) / gain_ref[:, at]
+        squares = squares + hidden * hidden
+        gate_val = gate_val + nn_dot(rows, side_by_side(0, index))
+        up_val = up_val + nn_dot(rows, side_by_side(D, index))
+        grad_active = grad_active + nt_dot(rows, down_block(index))
+    inverse = lax.rsqrt(jnp.sum(squares, 1, keepdims=True) / D + norm_eps)
+    gate_val, up_val = inverse * gate_val, inverse * up_val
+    grad_active = pltpu.roll(grad_active, count - CAP, 0)
+    upper = lax.rem(lax.broadcasted_iota(jnp.int32, (count, wide), 0), PAIR) < CAP
+    sig = 1.0 / (1.0 + jnp.exp(-gate_val))
+    silu = gate_val * sig
+    active = jnp.where(upper, silu * up_val, 0.0).astype(bf16)
+    grad_gate = grad_active * up_val * (sig * (1.0 + gate_val * (1.0 - sig)))
+    grad_gate = pltpu.roll(jnp.where(upper, grad_gate, 0.0), CAP, 0).astype(bf16)
+    grad_up = pltpu.roll(jnp.where(upper, grad_active * silu, 0.0), CAP, 0).astype(bf16)
+    for index in range(D // wide):
+        out = nn_dot(active, down_block(index))
+        out = out + nt_dot(grad_gate, side_by_side(0, index))
+        out = out + nt_dot(grad_up, side_by_side(D, index))
+        out_ref[:, index * wide : (index + 1) * wide] = out.astype(bf16)
+
+
+def reduce_kernel(terms_ref, own_ref, gain_ref, out_ref):
     total = terms_ref[0].astype(f32)
-    for index in range(1, count):
+    for index in range(1, terms_ref.shape[0]):
         total = total + terms_ref[index].astype(f32)
-    raised = rows_ref[:, 0:LANES].astype(f32).reshape(slices, SLOT, LANES)
-    back = total[:, LANES:].reshape(slices, SLOT, LANES)
-    gain = jnp.sum(raised[:, CAP : CAP + 3, :], 1, keepdims=True)
+    raised = own_ref[...].astype(f32)
+    gain = gain_ref[...]
+    back = jnp.concatenate([total[CAP:], total[:CAP]], 0)
     hidden = raised / gain
-    squares = jnp.sum(jnp.sum(hidden * hidden, 0), 1, keepdims=True)
-    inverse = lax.rsqrt(squares / D + norm_eps)
-    cross = jnp.sum(jnp.sum(back * raised, 0), 1, keepdims=True) / D
-    grad = inverse[None] * (back * gain - hidden * (inverse * inverse * cross)[None])
-    row = lax.broadcasted_iota(jnp.int32, (slices, SLOT, LANES), 1)
-    grad = jnp.where(row < CAP, grad, 0.0)
-    out_ref[:, 0:LANES] = total[:, 0:LANES].astype(bf16)
-    out_ref[:, LANES:] = grad.astype(bf16).reshape(depth, LANES)
+    inverse = lax.rsqrt(jnp.sum(hidden * hidden, 1, keepdims=True) / D + norm_eps)
+    cross = jnp.sum(back * raised, 1, keepdims=True) / D
+    grad = inverse * (back * gain - hidden * (inverse * inverse * cross))
+    out = jnp.concatenate([total[:CAP], grad[:CAP]], 0).astype(bf16)
+    for index in range(out_ref.shape[0]):
+        out_ref[index] = out[:, index * LANES : (index + 1) * LANES]
 
 
 def combine_kernel(
@@ -377,13 +361,15 @@
 ):
     rows = hidden_ref.shape[0]
     slots = slots_along_columns(route_ref[...], experts)
-    table = (lanes_of((rows, experts * SLOT)) == slots).astype(f32).astype(bf16)
-    token = nn_dot(table, home_ref[...])
+    column = lanes_of((rows, experts * PAIR))
+    home = home_ref[...]
+    token_out = nn_dot((column == slots).astype(f32).astype(bf16), home)
+    token_grad = nn_dot((column == slots + CAP).astype(f32).astype(bf16), home)
     attended = attended_ref[...].astype(f32)
     hidden = hidden_ref[...].astype(f32) + attended
     share = gate_share_of(affinity_ref[...])
-    layer_ref[...] = (hidden + share * token[:, 0:LANES]).astype(bf16)
-    grad = (cotangent_ref[...].astype(f32) + token[:, LANES:]).astype(bf16)
+    layer_ref[...] = (hidden + share * token_out).astype(bf16)
+    grad = (cotangent_ref[...].astype(f32) + token_grad).astype(bf16)
     grad_ref[...] = grad
     product = grad.astype(f32) * attended
     lane = lanes_of((rows, LANES))
@@ -398,20 +384,18 @@
     pieces = jnp.concatenate(
         [pieces.astype(bf16), jnp.zeros((2 * LANES - rows, LANES), bf16)], 0
     )
-    lines = nt_dot(unit_matrix(SLOT, LANES), pieces).astype(bf16)
+    lines = nt_dot(unit_matrix(LINES, LANES), pieces).astype(bf16)
     for index in range(message_ref.shape[0]):
         message_ref[index, 0:rows, :] = grad
-        message_ref[index, rows : rows + SLOT, :] = lines[:, LEFT]
-        message_ref[index, rows + SLOT :, :] = lines[:, RIGHT]
+        message_ref[index, rows : rows + LINES, :] = lines[:, LEFT]
+        message_ref[index, rows + LINES :, :] = lines[:, RIGHT]
 
 
 def query_kernel(
     place_ref,
-    same_ref,
-    cross_ref,
-    own_key_ref,
+    keys_ref,
+    vals_ref,
     own_query_ref,
-    values_ref,
     grad_ref,
     stats_ref,
     query_nope_ref,
@@ -420,7 +404,7 @@
     grads_ref,
     dq_ref,
 ):
-    rows = own_key_ref.shape[0]
+    rows = own_query_ref.shape[0]
     place = place_ref[0]
     pair, core = place // 2, place % 2
     lane = lanes_of((rows, LANES))
@@ -430,29 +414,24 @@
             lane // VDIM == head, grad_ref[...], jnp.zeros((rows, LANES), bf16)
         )
 
-    def part(head, keys, vals, visible):
+    def part(head, index, visible):
         dot = stats_ref[:, 2 * head : 2 * head + 1]
         log = stats_ref[:, 2 * head + 1 : 2 * head + 2]
+        keys = keys_ref[index]
         prob = jnp.exp(nt_dot(query_ref[head], keys) * score_scale - log)
         if visible is not None:
             prob = jnp.where(visible, prob, 0.0)
-        grad_prob = nt_dot(grads_ref[head], vals)
+        grad_prob = nt_dot(grads_ref[head], vals_ref[index])
         grad_score = (prob * (grad_prob - dot)).astype(bf16)
         return nn_dot(grad_score, keys)
 
-    cross = cross_ref[pair]
-    keys = jnp.concatenate([own_key_ref[...], keys_of(cross, rows)], 0)
-    vals = jnp.concatenate([values_ref[...], cross[0:rows, RIGHT]], 0)
     visible = pair_places(rows, core) <= lax.broadcasted_iota(jnp.int32, (rows, 2 * rows), 0)
     for head in range(2):
-        dq_ref[head] = part(head, keys, vals, visible)
+        dq_ref[head] = part(head, pair, visible)
 
     def step(index, carry):
-        same, cross = same_ref[index], cross_ref[index]
-        keys = jnp.concatenate([keys_of(same, rows), keys_of(cross, rows)], 0)
-        vals = jnp.concatenate([same[0:rows, RIGHT], cross[0:rows, RIGHT]], 0)
         for head in range(2):
-            dq_ref[head] += part(head, keys, vals, None)
+            dq_ref[head] += part(head, index, None)
         return carry
 
     lax.fori_loop(0, pair, step, 0)
@@ -473,31 +452,24 @@
     own_key_ref,
     own_query_ref,
     values_ref,
-    own_grad_ref,
     key_nope_ref,
     grad_values_ref,
     rope_ref,
-    key_ref,
-    vals_ref,
-    dk_ref,
-    dv_ref,
 ):
     rows = own_key_ref.shape[0]
     place = place_ref[0]
     pair, core = place // 2, place % 2
     lane = lanes_of((rows, LANES))
-    for head in range(2):
-        key_ref[head] = own_key(own_key_ref[...], head)
-        vals_ref[head] = jnp.where(
-            lane // VDIM == head, values_ref[...], jnp.zeros((rows, LANES), bf16)
-        )
+    zero = jnp.zeros((rows, LANES), bf16)
+    keys = [own_key(own_key_ref[...], head) for head in range(2)]
+    vals = [jnp.where(lane // VDIM == head, values_ref[...], zero) for head in range(2)]
 
     def lines_of(first, second):
-        zero = jnp.zeros((SLOT, LANES), f32)
+        zero = jnp.zeros((LINES, LANES), f32)
         parts = []
         for message in (first, second):
-            low = message[rows : rows + SLOT].astype(f32)
-            high = message[rows + SLOT :].astype(f32)
+            low = message[rows : rows + LINES].astype(f32)
+            high = message[rows + LINES :].astype(f32)
             parts.append(jnp.concatenate([low, high, zero], 1))
         moved = pltpu.roll(parts[1], rows, 1)
         return jnp.where(lanes_of(moved.shape) < rows, parts[0], moved)
@@ -506,49 +478,30 @@
         at = 6 * head
         dot = lines[at : at + 1] + lines[at + 1 : at + 2] + lines[at + 2 : at + 3]
         log = lines[at + 3 : at + 4] + lines[at + 4 : at + 5] + lines[at + 5 : at + 6]
-        prob = jnp.exp(nt_dot(key_ref[head], queries) * score_scale - log)
-        if visible is not None:
-            prob = jnp.where(visible, prob, 0.0)
-        grad_prob = nt_dot(vals_ref[head], grads)
+        prob = jnp.exp(nt_dot(keys[head], queries) * score_scale - log)
+        prob = jnp.where(visible, prob, 0.0)
+        grad_prob = nt_dot(vals[head], grads)
         grad_score = (prob * (grad_prob - dot)).astype(bf16)
         return nn_dot(grad_score, queries), nn_dot(prob.astype(bf16), grads)
 
-    def both(first, second, first_grad, second_grad, visible):
-        queries = jnp.concatenate([first, second], 0)
+    ahead = pair_places(rows, core) - lax.broadcasted_iota(jnp.int32, (rows, 2 * rows), 0)
+    dk, dv = [0.0, 0.0], [0.0, 0.0]
+    for index in range(same_ref.shape[0]):
+        first = jnp.where(index == pair, own_query_ref[...], same_ref[index, 0:rows, :])
+        queries = jnp.concatenate([first, cross_ref[index, 0:rows, :]], 0)
+        first_grad, second_grad = grad_same_ref[index], grad_cross_ref[index]
         grads = jnp.concatenate([first_grad[0:rows], second_grad[0:rows]], 0)
         lines = lines_of(first_grad, second_grad)
-        return [part(head, queries, grads, lines, visible) for head in range(2)]
-
-    visible = pair_places(rows, core) >= lax.broadcasted_iota(jnp.int32, (rows, 2 * rows), 0)
-    made = both(
-        own_query_ref[...],
-        cross_ref[pair][0:rows],
-        own_grad_ref[0],
-        grad_cross_ref[pair],
-        visible,
-    )
-    for head in range(2):
-        dk_ref[head], dv_ref[head] = made[head]
-
-    def step(index, carry):
-        made = both(
-            same_ref[index][0:rows],
-            cross_ref[index][0:rows],
-            grad_same_ref[index],
-            grad_cross_ref[index],
-            None,
-        )
+        visible = ahead >= (pair - index) * (2 * rows)
         for head in range(2):
-            dk_ref[head] += made[head][0]
-            dv_ref[head] += made[head][1]
-        return carry
-
-    lax.fori_loop(pair + 1, same_ref.shape[0], step, 0)
+            more_dk, more_dv = part(head, queries, grads, lines, visible)
+            dk[head] = dk[head] + more_dk
+            dv[head] = dv[head] + more_dv
     key_nope_ref[...] = (
-        score_scale * jnp.where(lane < NOPE, dk_ref[0, :, LEFT], dk_ref[1, :, LEFT])
+        score_scale * jnp.where(lane < NOPE, dk[0][:, LEFT], dk[1][:, LEFT])
     ).astype(bf16)
-    grad_values_ref[...] = jnp.where(lane < VDIM, dv_ref[0], dv_ref[1]).astype(bf16)
-    shared = dk_ref[0, :, RIGHT] + pltpu.roll(dk_ref[1, :, RIGHT], LANES - ROPE, 1)
+    grad_values_ref[...] = jnp.where(lane < VDIM, dv[0], dv[1]).astype(bf16)
+    shared = dk[0][:, RIGHT] + pltpu.roll(dk[1][:, RIGHT], LANES - ROPE, 1)
     quarter = rows // 4
     packed = jnp.zeros((quarter, LANES), f32)
     small = lanes_of((quarter, LANES))
@@ -619,7 +572,6 @@
     half = ctx_count // 2
     by_core = [[core + 2 * index for index in range(half)] for core in range(2)]
     across = [(index, index ^ 1) for index in range(ctx_count)]
-    depth = experts * SLOT
     quarter = rows // 4
 
     def swap(value):
@@ -660,11 +612,17 @@
     same, weights = lax.optimization_barrier((same, weights))
     cross = swap(same)
 
-    attended, logs, send = call(
+    attended, logs, send, all_keys, all_vals = call(
         functools.partial(forward_kernel, experts),
-        14,
-        (shape_of(rows, width), shape_of(rows, width, dtype=f32), shape_of(depth, 2 * width)),
-        [pltpu.VMEM((2, rows, 2 * width), bf16)],
+        24,
+        (
+            shape_of(rows, width),
+            shape_of(rows, width, dtype=f32),
+            shape_of(experts * TALL, width),
+            shape_of(half, 2 * rows, 2 * width),
+            shape_of(half, 2 * rows, width),
+        ),
+        [pltpu.VMEM((2, half, rows, 2 * rows), f32)],
         1,
         10,
     )(
@@ -675,15 +633,22 @@
         *(held(value) for value in (hidden_in, norm_gain.reshape(1, width))),
         *(held(value) for value in (route, affinity, cotangent)),
     )
-    received = exchange(send.reshape(experts, SLOT, 2 * width), "exp").reshape(depth, 2 * width)
-    copies = jnp.broadcast_to(received[None], (half, depth, 2 * width))
-    rows_all = exchange(copies, "ctx", by_core)
-    partial = call(expert_kernel, 28, shape_of(half, depth, 2 * width), count=3)(
-        rows_all, *weights
-    )
-    terms = exchange(partial, "ctx", by_core)
-    back = call(reduce_kernel, 10, shape_of(depth, 2 * width), count=2)(terms, received)
-    home = exchange(back.reshape(experts, SLOT, 2 * width), "exp").reshape(depth, 2 * width)
+    received = exchange(send.reshape(experts, TALL, width), "exp").reshape(-1, width)
+    rows_all, own_rows, gain = call(
+        unfold_kernel,
+        6,
+        (shape_of(half, PAIR, D), shape_of(PAIR, D), shape_of(1, D, dtype=f32)),
+        count=1,
+    )(received)
+    rows_all = exchange(rows_all, "ctx", by_core).reshape(half * PAIR, D)
+    partial = call(expert_kernel, 24, shape_of(half * PAIR, D), count=4)(
+        rows_all, gain, *weights
+    )
+    terms = exchange(partial.reshape(half, PAIR, D), "ctx", by_core)
+    back = call(reduce_kernel, 8, shape_of(experts, PAIR, width), count=3)(
+        terms, own_rows, gain
+    )
+    home = exchange(back, "exp").reshape(experts * PAIR, width)
     layer_out, grad_hidden, stats, messages = call(
         functools.partial(combine_kernel, experts),
         8,
@@ -701,15 +666,10 @@
         key_kernel,
         14,
         (shape_of(rows, width), shape_of(rows, width), shape_of(experts, quarter, LANES)),
-        [
-            pltpu.VMEM((2, rows, 2 * width), bf16),
-            pltpu.VMEM((2, rows, width), bf16),
-            pltpu.VMEM((2, rows, 2 * width), f32),
-            pltpu.VMEM((2, rows, width), f32),
-        ],
+        (),
         1,
-        8,
-    )(place, same, cross, grad_same, grad_cross, *own, messages)
+        7,
+    )(place, same, cross, grad_same, grad_cross, *own)
     rope_terms = exchange(rope_part, "exp")
     gq_nope, gq_rope = call(
         query_kernel,
@@ -721,8 +681,8 @@
             pltpu.VMEM((2, rows, 2 * width), f32),
         ],
         1,
-        7,
-    )(place, same, cross, *own, grad_hidden, stats)
+        5,
+    )(place, all_keys, all_vals, own_query_rows, grad_hidden, stats)
     gk_rope = call(rope_kernel, 4, shape_of(ROPE, rows), count=1)(rope_terms)
     return (layer_out, grad_hidden, gq_nope, gq_rope.T, gk_nope, gk_rope.T, g_values)
 

time: 225 us -> 206 us (0.916)
  blocking collectives: 150 us -> 130 us
    all_to_all x6, blocking collectives: 150 us -> 130 us  [exchange(): lax.all_to_all(blocks, axis, 0, 0, tiled=True, axis_index_groups=groups)]
    pallas_call x3 -> x4, Pallas kernels: 6.85 us -> 10.4 us  [the longest x1 5.02 us: per_device(): call(functools.partial(forward_kernel, experts), 24, (shape_of(rows, widt...]
where the time goes in v5:
time: 206 us
  blocking collectives  130 us (63%)
  waiting for transfers between devices  27.6 us (13%)
  starting transfers between devices  23.8 us (12%)
  Pallas kernels  22.9 us (11%)
    all_to_all x6, blocking collectives, exchange(): lax.all_to_all(blocks, axis, 0, 0, tiled=True, axis_index_groups=groups)  130 us
    all_to_all x1, waiting for transfers between devices, exchange(): lax.all_to_all(blocks, axis, 0, 0, tiled=True, axis_index_groups=groups)  24.3 us
    ppermute x3, starting transfers between devices, swap(): return lax.ppermute(value, 'ctx', across)  20 us
    pallas_call x1, Pallas kernels, per_device(): call(key_kernel, 14, (shape_of(rows, width), shape_of(rows, width), shape...  6.19 us
    pallas_call x1, Pallas kernels, per_device(): call(functools.partial(forward_kernel, experts), 24, (shape_of(rows, widt...  5.02 us
    pallas_call x1, Pallas kernels, per_device(): call(expert_kernel, 24, shape_of(half * PAIR, D), count=4)  4.55 us
  transfers between devices with their start and end apart: 4, of which 3 were waited for; matrix products, arithmetic and copies ran while one was open for 0% of the time, Pallas kernels for 1%

profile of v5, /device:TPU:1, one launch (start us, length us, event | category | flops | bytes accessed | tf_op | source)
XLA Modules:
  0.0 205.6 jit_solution(5822134423144291702)
XLA Ops:
  0.6 2.2 %shard_map.180 = (bf16[192,256]{1,0:T(8,128)(2,1)S(1)}, bf16[192,256]{1,0:T(8,128)(2,1)S(1)}, bf16[8,224,256]{2,1,0:T(8,128)(2,1)S(1)}, bf16[12288,128]{1,0:T(8,128)(2,1)S(1)}) custom-call(s32[1]{0:T(128)} %bitcast.place_ref, bf16[192,128]{1,0:T(8,128)(2,1)} %key_nope_hbm.1, bf16[32,192]{1,0:T(8,128)(2,1)} %bitcast.29, bf16[64,192]{1,0:T(8,128)(2,1)} %bitcast.28, ...), custom_call_target="tpu_custom_call" | custom-call | tf_op jit(solution)/shard_map/pallas_call | solution.py:584
  2.8 8.8 %collective-permute-start = (bf16[12288,128]{1,0:T(8,128)(2,1)S(1)}, bf16[12288,128]{1,0:T(8,128)(2,1)S(1)}, u32[]{:S(2)}, u32[]{:S(2)}) collective-permute-start(bf16[12288,128]{1,0:T(8,128)(2,1)S(1)} %get-tuple-element.39.own_ref), channel_id=1, source_target_pairs={{0,32},{32,0},{64,96},{96,64},{128,160},{160,128},{192,224},{224,1... | collective-permute-start | bytes 9437192 | tf_op jit(solution)/shard_map/ppermute | solution.py:578
  11.6 17.6 %all_to_all.35.same_ref = bf16[8,224,256]{2,1,0:T(8,128)(2,1)S(1)} all-to-all(bf16[8,224,256]{2,1,0:T(8,128)(2,1)S(1)} %get-tuple-element.31), channel_id=1, replica_groups={{0,64,128,192,256,320,384,448},{32,96,160,224,288,352,416,480},{1,65,12..., dimensions={0} | all-to-all | bytes 1835008 | tf_op jit(solution)/shard_map/all_to_all | solution.py:552
  29.3 0.0 collective-permute-done.other_ref
  29.3 3.2 %collective-permute-start.1 = (bf16[8,224,256]{2,1,0:T(8,128)(2,1)S(1)}, bf16[8,224,256]{2,1,0:T(8,128)(2,1)S(1)}, u32[]{:S(2)}, u32[]{:S(2)}) collective-permute-start(bf16[8,224,256]{2,1,0:T(8,128)(2,1)S(1)} %all_to_all.35.same_ref), channel_id=1, source_target_pairs={{0,32},{32,0},{64,96},{96,64},{128,160},{160,128},{192,224},{224,1... | collective-permute-start | bytes 2752520 | tf_op jit(solution)/shard_map/ppermute | solution.py:578
  32.4 2.1 %collective-permute-done.1.cross_ref = bf16[8,224,256]{2,1,0:T(8,128)(2,1)S(1)} collective-permute-done((bf16[8,224,256]{2,1,0:T(8,128)(2,1)S(1)}, bf16[8,224,256]{2,1,0:T(8,128)(2,1)S(1)}, u32[]{:S(2)}, u32[]{:S(2)}) %collective-permute-start.1) | collective-permute-done | bytes 917536 | tf_op jit(solution)/shard_map/ppermute | solution.py:578
  34.5 5.0 %shard_map.181 = (bf16[192,128]{1,0:T(8,128)(2,1)S(1)}, f32[192,128]{1,0:T(8,128)S(1)}, bf16[1024,128]{1,0:T(8,128)(2,1)S(1)}, bf16[8,384,256]{2,1,0:T(8,128)(2,1)S(1)}, bf16[8,384,128]{2,1,0:T(8,128)(2,1)S(1)}) custom-call(s32[1]{0:T(128)} %bitcast.place_ref, bf16[8,224,256]{2,1,0:T(8,128)(2,1)S(1)} %all_to_all.35.same_ref, ...), custom_call_target="tpu_custom_call" | custom-call | tf_op jit(solution)/shard_map/pallas_call | solution.py:615
  39.5 34.3 %all_to_all.36 = bf16[32,32,128]{2,1,0:T(8,128)(2,1)S(1)} all-to-all(bf16[32,32,128]{2,1,0:T(8,128)(2,1)S(1)} %bitcast.20), channel_id=1, replica_groups=mesh['ctx'=16,'exp'=32] {'exp'}, dimensions={0} | all-to-all | bytes 524288 | tf_op jit(solution)/shard_map/all_to_all | solution.py:552
  73.8 0.4 shard_map.182
  74.2 22.2 %all_to_all.37 = bf16[8,24,4096]{2,1,0:T(8,128)(2,1)S(1)} all-to-all(bf16[8,24,4096]{2,1,0:T(8,128)(2,1)S(1)} %get-tuple-element.37), channel_id=1, replica_groups={{0,64,128,192,256,320,384,448},{32,96,160,224,288,352,416,480},{1,65,12..., dimensions={0} | all-to-all | bytes 3145728 | tf_op jit(solution)/shard_map/all_to_all | solution.py:552
  96.4 4.5 %shard_map.183 = bf16[192,4096]{1,0:T(8,128)(2,1)S(1)} custom-call(bf16[192,4096]{1,0:T(8,128)(2,1)S(1)} %bitcast.16, f32[1,4096]{1,0:T(1,128)S(1)} %get-tuple-element.38.gain_ref, bf16[12288,128]{1,0:T(8,128)(2,1)S(1)} %get-tuple-element.39.own_ref, bf16[12288,128]{1,0:T(8,128)(2,1)S(1)} %collective-permute-done.other_ref), custom_call_target="tpu_custom_call" | custom-call | tf_op jit(solution)/shard_map/pallas_call | solution.py:644
  101.0 20.7 %all_to_all.38.terms_ref = bf16[8,24,4096]{2,1,0:T(8,128)(2,1)S(1)} all-to-all(bf16[8,24,4096]{2,1,0:T(8,128)(2,1)S(1)} %bitcast.17), channel_id=1, replica_groups={{0,64,128,192,256,320,384,448},{32,96,160,224,288,352,416,480},{1,65,12..., dimensions={0} | all-to-all | bytes 3145728 | tf_op jit(solution)/shard_map/all_to_all | solution.py:552
  121.7 0.0 copy-start
  121.7 0.0 copy-start.1
  121.7 0.0 copy-start.3
  121.7 0.0 copy-start.4
  121.7 0.5 shard_map.184
  122.1 23.7 %all_to_all.39 = bf16[32,24,128]{2,1,0:T(8,128)(2,1)S(1)} all-to-all(bf16[32,24,128]{2,1,0:T(8,128)(2,1)S(1)} %shard_map.184), channel_id=1, replica_groups=mesh['ctx'=16,'exp'=32] {'exp'}, dimensions={0} | all-to-all | bytes 393216 | tf_op jit(solution)/shard_map/all_to_all | solution.py:552
  145.8 0.0 copy-done
  145.8 0.0 copy-done.1
  145.8 0.0 copy-done.3
  145.8 0.0 copy-done.4
  145.8 1.6 shard_map.185
  147.4 12.0 %all_to_all.40.grad_same_ref = bf16[8,224,128]{2,1,0:T(8,128)(2,1)S(1)} all-to-all(bf16[8,224,128]{2,1,0:T(8,128)(2,1)S(1)} %get-tuple-element.51), channel_id=1, replica_groups={{0,64,128,192,256,320,384,448},{32,96,160,224,288,352,416,480},{1,65,12..., dimensions={0} | all-to-all | bytes 917504 | tf_op jit(solution)/shard_map/all_to_all | solution.py:552
  159.4 8.0 %collective-permute-start.2 = (bf16[8,224,128]{2,1,0:T(8,128)(2,1)S(1)}, bf16[8,224,128]{2,1,0:T(8,128)(2,1)S(1)}, u32[]{:S(2)}, u32[]{:S(2)}) collective-permute-start(bf16[8,224,128]{2,1,0:T(8,128)(2,1)S(1)} %all_to_all.40.grad_same_ref), channel_id=1, source_target_pairs={{0,32},{32,0},{64,96},{96,64},{128,160},{160,128},{192,224},{224,1... | collective-permute-start | bytes 1376264 | tf_op jit(solution)/shard_map/ppermute | solution.py:578
  167.4 1.2 collective-permute-done.2.grad_cross_ref
  168.6 6.2 %shard_map.187 = (bf16[192,128]{1,0:T(8,128)(2,1)}, bf16[192,128]{1,0:T(8,128)(2,1)}, bf16[32,48,128]{2,1,0:T(8,128)(2,1)}) custom-call(s32[1]{0:T(128)} %bitcast.place_ref, bf16[8,224,256]{2,1,0:T(8,128)(2,1)S(1)} %all_to_all.35.same_ref, bf16[8,224,256]{2,1,0:T(8,128)(2,1)S(1)} %collective-permute-done.1.cross_ref, ...), custom_call_target="tpu_custom_call" | custom-call | tf_op jit(solution)/shard_map/pallas_call | solution.py:665
  174.8 3.9 %all-to-all-start.6 = ((bf16[32,48,128]{2,1,0:T(8,128)(2,1)}), bf16[32,48,128]{2,1,0:T(8,128)(2,1)S(1)}, u32[]{:S(2)}, u32[]{:S(2)}) async-start(bf16[32,48,128]{2,1,0:T(8,128)(2,1)} %get-tuple-element.53), calls=%async_computation.6 | async-start | bytes 786432 | tf_op jit(solution)/shard_map/all_to_all | solution.py:552
  178.7 0.0 copy-done.2
  178.7 1.6 shard_map.186
  180.3 24.3 %all-to-all-done.6.terms_ref = bf16[32,48,128]{2,1,0:T(8,128)(2,1)S(1)} async-done(((bf16[32,48,128]{2,1,0:T(8,128)(2,1)}), bf16[32,48,128]{2,1,0:T(8,128)(2,1)S(1)}, u32[]{:S(2)}, u32[]{:S(2)}) %all-to-all-start.6) | async-done | bytes 393248 | tf_op jit(solution)/shard_map/all_to_all | solution.py:552
  204.6 0.9 shard_map.188
  (1 shorter events, 0.0 us)
Async XLA Ops:
  2.8 26.4 %collective-permute-start = (bf16[12288,128]{1,0:T(8,128)(2,1)S(1)}, bf16[12288,128]{1,0:T(8,128)(2,1)S(1)}, u32[]{:S(2)}, u32[]{:S(2)}) collective-permute-start(bf16[12288,128]{1,0:T(8,128)(2,1)S(1)} %get-tuple-element.39.own_ref), channel_id=1, source_target_pairs={{0,32},{32,0},{64,96},{96,64},{128,160},{160,128},{192,224},{224,1... | collective-permute-start | bytes 9437192 | tf_op jit(solution)/shard_map/ppermute | solution.py:578
  29.3 5.3 %collective-permute-start.1 = (bf16[8,224,256]{2,1,0:T(8,128)(2,1)S(1)}, bf16[8,224,256]{2,1,0:T(8,128)(2,1)S(1)}, u32[]{:S(2)}, u32[]{:S(2)}) collective-permute-start(bf16[8,224,256]{2,1,0:T(8,128)(2,1)S(1)} %all_to_all.35.same_ref), channel_id=1, source_target_pairs={{0,32},{32,0},{64,96},{96,64},{128,160},{160,128},{192,224},{224,1... | collective-permute-start | bytes 2752520 | tf_op jit(solution)/shard_map/ppermute | solution.py:578
  121.7 24.1 %copy-start = (bf16[192,128]{1,0:T(8,128)(2,1)S(1)}, bf16[192,128]{1,0:T(8,128)(2,1)}, u32[]{:S(2)}) copy-start(bf16[192,128]{1,0:T(8,128)(2,1)} %hidden_ref.3) | copy-start | bytes 147460
  121.7 24.1 %copy-start.1 = (bf16[192,128]{1,0:T(8,128)(2,1)S(1)}, bf16[192,128]{1,0:T(8,128)(2,1)}, u32[]{:S(2)}) copy-start(bf16[192,128]{1,0:T(8,128)(2,1)} %cotangent_ref.3) | copy-start | bytes 147460
  121.7 24.1 %copy-start.3 = (f32[192,8]{0,1:T(8,128)S(1)}, f32[192,8]{0,1:T(8,128)}, u32[]{:S(2)}) copy-start(f32[192,8]{0,1:T(8,128)} %param.21) | copy-start | bytes 18436
  121.7 24.1 %copy-start.4 = (s32[192]{0:T(256)S(1)}, s32[192]{0:T(256)}, u32[]{:S(2)}) copy-start(s32[192]{0:T(256)} %param.20) | copy-start | bytes 2308
  159.4 19.3 %copy-start.2 = (bf16[192,128]{1,0:T(8,128)(2,1)S(1)}, bf16[192,128]{1,0:T(8,128)(2,1)}, u32[]{:S(2)}) copy-start(bf16[192,128]{1,0:T(8,128)(2,1)} %get-tuple-element.25.grad_ref) | copy-start | bytes 147460
  159.4 9.3 %collective-permute-start.2 = (bf16[8,224,128]{2,1,0:T(8,128)(2,1)S(1)}, bf16[8,224,128]{2,1,0:T(8,128)(2,1)S(1)}, u32[]{:S(2)}, u32[]{:S(2)}) collective-permute-start(bf16[8,224,128]{2,1,0:T(8,128)(2,1)S(1)} %all_to_all.40.grad_same_ref), channel_id=1, source_target_pairs={{0,32},{32,0},{64,96},{96,64},{128,160},{160,128},{192,224},{224,1... | collective-permute-start | bytes 1376264 | tf_op jit(solution)/shard_map/ppermute | solution.py:578
  174.8 29.8 %all-to-all-start.6 = ((bf16[32,48,128]{2,1,0:T(8,128)(2,1)}), bf16[32,48,128]{2,1,0:T(8,128)(2,1)S(1)}, u32[]{:S(2)}, u32[]{:S(2)}) async-start(bf16[32,48,128]{2,1,0:T(8,128)(2,1)} %get-tuple-element.53), calls=%async_computation.6 | async-start | bytes 786432 | tf_op jit(solution)/shard_map/all_to_all | solution.py:552

commit v6 on v5

--- a/solution.py
+++ b/solution.py
@@ -84,9 +84,17 @@
     return jnp.concatenate([message[0:rows, LEFT], rot], 1)
 
 
-def pair_places(rows, core):
-    lane = lanes_of((rows, 2 * rows))
-    return lane - jnp.where(lane >= rows, 2 * rows, 0) * core
+def lead_of(rows):
+    shape = (rows, 2 * rows)
+    lane = lanes_of(shape)
+    return lane + jnp.where(lane >= rows, rows, 0) - lax.broadcasted_iota(jnp.int32, shape, 0)
+
+
+def chunk_start(place, rows, index, cross):
+    start = (place // 2 - 2 * index) * (2 * rows)
+    if cross:
+        start = start + (2 * (place % 2) - 1) * rows
+    return start
 
 
 def slots_along_rows(route_row, experts):
@@ -197,14 +205,61 @@
         copy.wait()
 
 
+def unpack_messages(messages_ref, keys_ref, vals_ref, rows):
+    for index in range(messages_ref.shape[0]):
+        chunk, part = index // 2, index % 2
+        at = slice(part * rows, (part + 1) * rows)
+        rot = messages_ref[index, rows : rows + ROPE, :][:, 0:rows]
+        keys_ref[chunk, at, LEFT] = messages_ref[index, 0:rows, LEFT]
+        keys_ref[chunk, at, RIGHT] = upright(rot)
+        vals_ref[chunk, at, :] = messages_ref[index, 0:rows, RIGHT]
+
+
+def score_chunks(place, queries, keys_ref, scores_ref, tops, cross):
+    rows = queries[0].shape[0]
+    lead = lead_of(rows)
+    for index in range(keys_ref.shape[0]):
+        visible = lead <= chunk_start(place, rows, index, cross)
+        for head in range(2):
+            scores = nt_dot(queries[head], keys_ref[index]) * score_scale
+            scores = jnp.where(visible, scores, masked_low)
+            scores_ref[head, index] = scores
+            tops[head] = scores if tops[head] is None else jnp.maximum(tops[head], scores)
+    return tops
+
+
+def same_scores_kernel(
+    place_ref,
+    same_ref,
+    own_key_ref,
+    own_query_ref,
+    values_ref,
+    keys_ref,
+    vals_ref,
+    scores_ref,
+    tops_ref,
+):
+    rows = own_key_ref.shape[0]
+    place = place_ref[0]
+    unpack_messages(same_ref, keys_ref, vals_ref, rows)
+    pair = place // 2
+    at = pl.ds(pl.multiple_of(lax.rem(pair, 2) * rows, rows), rows)
+    keys_ref[pair // 2, at, :] = own_key_ref[...]
+    vals_ref[pair // 2, at, :] = values_ref[...]
+    queries = [own_query(own_query_ref[...], head) for head in range(2)]
+    tops = score_chunks(place, queries, keys_ref, scores_ref, [None, None], False)
+    for head in range(2):
+        tops_ref[head] = tops[head]
+
+
 def forward_kernel(
     experts,
     place_ref,
-    same_ref,
     cross_ref,
-    own_key_ref,
+    same_vals_ref,
+    same_scores_ref,
+    tops_ref,
     own_query_ref,
-    values_ref,
     hidden_ref,
     gain_ref,
     route_ref,
@@ -213,42 +268,26 @@
     attended_ref,
     log_ref,
     send_ref,
-    all_keys_ref,
-    all_vals_ref,
+    keys_ref,
+    vals_ref,
     scores_ref,
 ):
-    rows = own_key_ref.shape[0]
+    rows = own_query_ref.shape[0]
     place = place_ref[0]
-    pair, core = place // 2, place % 2
-    count = same_ref.shape[0]
-    for index in range(count):
-        for part, ref in enumerate((same_ref, cross_ref)):
-            at = slice(part * rows, (part + 1) * rows)
-            rot = ref[index, rows : rows + ROPE, :][:, 0:rows]
-            all_keys_ref[index, at, LEFT] = ref[index, 0:rows, LEFT]
-            all_keys_ref[index, at, RIGHT] = upright(rot)
-            all_vals_ref[index, at, :] = ref[index, 0:rows, RIGHT]
-    all_keys_ref[pair, 0:rows, :] = own_key_ref[...]
-    all_vals_ref[pair, 0:rows, :] = values_ref[...]
+    unpack_messages(cross_ref, keys_ref, vals_ref, rows)
     queries = [own_query(own_query_ref[...], head) for head in range(2)]
-    ahead = pair_places(rows, core) - lax.broadcasted_iota(jnp.int32, (rows, 2 * rows), 0)
-    tops = [None, None]
-    for index in range(count):
-        visible = ahead <= (pair - index) * (2 * rows)
-        for head in range(2):
-            scores = nt_dot(queries[head], all_keys_ref[index]) * score_scale
-            scores = jnp.where(visible, scores, masked_low)
-            scores_ref[head, index] = scores
-            tops[head] = scores if index == 0 else jnp.maximum(tops[head], scores)
+    tops = [tops_ref[head] for head in range(2)]
+    tops = score_chunks(place, queries, keys_ref, scores_ref, tops, True)
     state = []
     for head in range(2):
         top = jnp.max(tops[head], 1, keepdims=True)
         total = jnp.zeros((rows, 2 * rows), f32)
         mixed = jnp.zeros((rows, LANES), f32)
-        for index in range(count):
-            weights = jnp.exp(scores_ref[head, index] - top)
-            total = total + weights
-            mixed = mixed + nn_dot(weights.astype(bf16), all_vals_ref[index])
+        for some_scores, some_vals in ((same_scores_ref, same_vals_ref), (scores_ref, vals_ref)):
+            for index in range(some_vals.shape[0]):
+                weights = jnp.exp(some_scores[head, index] - top)
+                total = total + weights
+                mixed = mixed + nn_dot(weights.astype(bf16), some_vals[index])
         state.extend([top, jnp.sum(total, 1, keepdims=True), mixed])
     first = lanes_of((rows, LANES)) < VDIM
     attended = jnp.where(first, state[2] / state[1], state[5] / state[4]).astype(bf16)
@@ -393,8 +432,10 @@
 
 def query_kernel(
     place_ref,
-    keys_ref,
-    vals_ref,
+    same_keys_ref,
+    same_vals_ref,
+    cross_keys_ref,
+    cross_vals_ref,
     own_query_ref,
     grad_ref,
     stats_ref,
@@ -406,35 +447,33 @@
 ):
     rows = own_query_ref.shape[0]
     place = place_ref[0]
-    pair, core = place // 2, place % 2
     lane = lanes_of((rows, LANES))
+    lead = lead_of(rows)
     for head in range(2):
         query_ref[head] = own_query(own_query_ref[...], head)
         grads_ref[head] = jnp.where(
             lane // VDIM == head, grad_ref[...], jnp.zeros((rows, LANES), bf16)
         )
-
-    def part(head, index, visible):
-        dot = stats_ref[:, 2 * head : 2 * head + 1]
-        log = stats_ref[:, 2 * head + 1 : 2 * head + 2]
-        keys = keys_ref[index]
-        prob = jnp.exp(nt_dot(query_ref[head], keys) * score_scale - log)
-        if visible is not None:
-            prob = jnp.where(visible, prob, 0.0)
-        grad_prob = nt_dot(grads_ref[head], vals_ref[index])
-        grad_score = (prob * (grad_prob - dot)).astype(bf16)
-        return nn_dot(grad_score, keys)
-
-    visible = pair_places(rows, core) <= lax.broadcasted_iota(jnp.int32, (rows, 2 * rows), 0)
-    for head in range(2):
-        dq_ref[head] = part(head, pair, visible)
+    dq_ref[...] = jnp.zeros_like(dq_ref)
 
     def step(index, carry):
-        for head in range(2):
-            dq_ref[head] += part(head, index, None)
+        for cross in range(2):
+            keys_ref, vals_ref = (
+                (cross_keys_ref, cross_vals_ref) if cross else (same_keys_ref, same_vals_ref)
+            )
+            visible = lead <= chunk_start(place, rows, index, cross)
+            keys, vals = keys_ref[index], vals_ref[index]
+            for head in range(2):
+                dot = stats_ref[:, 2 * head : 2 * head + 1]
+                log = stats_ref[:, 2 * head + 1 : 2 * head + 2]
+                prob = jnp.exp(nt_dot(query_ref[head], keys) * score_scale - log)
+                prob = jnp.where(visible, prob, 0.0)
+                grad_prob = nt_dot(grads_ref[head], vals)
+                grad_score = (prob * (grad_prob - dot)).astype(bf16)
+                dq_ref[head] += nn_dot(grad_score, keys)
         return carry
 
-    lax.fori_loop(0, pair, step, 0)
+    lax.fori_loop(0, place // 4 + 1, step, 0)
     query_nope_ref[...] = (
         score_scale * jnp.where(lane < NOPE, dq_ref[0, :, LEFT], dq_ref[1, :, LEFT])
     ).astype(bf16)
@@ -443,26 +482,14 @@
     query_rope_ref[...] = nt_dot(unit_matrix(2 * ROPE, LANES), rot).astype(bf16)
 
 
-def key_kernel(
-    place_ref,
-    same_ref,
-    cross_ref,
-    grad_same_ref,
-    grad_cross_ref,
-    own_key_ref,
-    own_query_ref,
-    values_ref,
-    key_nope_ref,
-    grad_values_ref,
-    rope_ref,
-):
+def key_chunks(place, messages_ref, grads_ref, own_key_ref, own_query_ref, values_ref, dk, dv):
     rows = own_key_ref.shape[0]
-    place = place_ref[0]
-    pair, core = place // 2, place % 2
+    cross = own_query_ref is None
     lane = lanes_of((rows, LANES))
+    keys = [own_key(own_key_ref[...], head) for head in range(2)]
     zero = jnp.zeros((rows, LANES), bf16)
-    keys = [own_key(own_key_ref[...], head) for head in range(2)]
     vals = [jnp.where(lane // VDIM == head, values_ref[...], zero) for head in range(2)]
+    lead = lead_of(rows)
 
     def lines_of(first, second):
         zero = jnp.zeros((LINES, LANES), f32)
@@ -474,29 +501,81 @@
         moved = pltpu.roll(parts[1], rows, 1)
         return jnp.where(lanes_of(moved.shape) < rows, parts[0], moved)
 
-    def part(head, queries, grads, lines, visible):
-        at = 6 * head
-        dot = lines[at : at + 1] + lines[at + 1 : at + 2] + lines[at + 2 : at + 3]
-        log = lines[at + 3 : at + 4] + lines[at + 4 : at + 5] + lines[at + 5 : at + 6]
-        prob = jnp.exp(nt_dot(keys[head], queries) * score_scale - log)
-        prob = jnp.where(visible, prob, 0.0)
-        grad_prob = nt_dot(vals[head], grads)
-        grad_score = (prob * (grad_prob - dot)).astype(bf16)
-        return nn_dot(grad_score, queries), nn_dot(prob.astype(bf16), grads)
-
-    ahead = pair_places(rows, core) - lax.broadcasted_iota(jnp.int32, (rows, 2 * rows), 0)
-    dk, dv = [0.0, 0.0], [0.0, 0.0]
-    for index in range(same_ref.shape[0]):
-        first = jnp.where(index == pair, own_query_ref[...], same_ref[index, 0:rows, :])
-        queries = jnp.concatenate([first, cross_ref[index, 0:rows, :]], 0)
-        first_grad, second_grad = grad_same_ref[index], grad_cross_ref[index]
-        grads = jnp.concatenate([first_grad[0:rows], second_grad[0:rows]], 0)
-        lines = lines_of(first_grad, second_grad)
-        visible = ahead >= (pair - index) * (2 * rows)
+    def queries_of(index):
+        queries = messages_ref[index, 0:rows, :]
+        if cross:
+            return queries
+        return jnp.where(index == place // 2, own_query_ref[...], queries)
+
+    for chunk in range(messages_ref.shape[0] // 2):
+        index = 2 * chunk
+        queries = jnp.concatenate([queries_of(index), queries_of(index + 1)], 0)
+        first, second = grads_ref[index], grads_ref[index + 1]
+        grads = jnp.concatenate([first[0:rows], second[0:rows]], 0)
+        lines = lines_of(first, second)
+        visible = lead >= chunk_start(place, rows, chunk, cross)
         for head in range(2):
-            more_dk, more_dv = part(head, queries, grads, lines, visible)
-            dk[head] = dk[head] + more_dk
-            dv[head] = dv[head] + more_dv
+            at = 6 * head
+            dot = lines[at : at + 1] + lines[at + 1 : at + 2] + lines[at + 2 : at + 3]
+            log = lines[at + 3 : at + 4] + lines[at + 4 : at + 5] + lines[at + 5 : at + 6]
+            prob = jnp.exp(nt_dot(keys[head], queries) * score_scale - log)
+            prob = jnp.where(visible, prob, 0.0)
+            grad_prob = nt_dot(vals[head], grads)
+            grad_score = (prob * (grad_prob - dot)).astype(bf16)
+            dk[head] = dk[head] + nn_dot(grad_score, queries)
+            dv[head] = dv[head] + nn_dot(prob.astype(bf16), grads)
+    return dk, dv
+
+
+def same_key_kernel(
+    place_ref,
+    same_ref,
+    grad_same_ref,
+    own_key_ref,
+    own_query_ref,
+    values_ref,
+    dk_ref,
+    dv_ref,
+):
+    dk, dv = key_chunks(
+        place_ref[0],
+        same_ref,
+        grad_same_ref,
+        own_key_ref,
+        own_query_ref,
+        values_ref,
+        [0.0, 0.0],
+        [0.0, 0.0],
+    )
+    for head in range(2):
+        dk_ref[head] = dk[head]
+        dv_ref[head] = dv[head]
+
+
+def key_kernel(
+    place_ref,
+    cross_ref,
+    grad_cross_ref,
+    own_key_ref,
+    values_ref,
+    dk_ref,
+    dv_ref,
+    key_nope_ref,
+    grad_values_ref,
+    rope_ref,
+):
+    rows = own_key_ref.shape[0]
+    lane = lanes_of((rows, LANES))
+    dk, dv = key_chunks(
+        place_ref[0],
+        cross_ref,
+        grad_cross_ref,
+        own_key_ref,
+        None,
+        values_ref,
+        [dk_ref[head] for head in range(2)],
+        [dv_ref[head] for head in range(2)],
+    )
     key_nope_ref[...] = (
         score_scale * jnp.where(lane < NOPE, dk[0][:, LEFT], dk[1][:, LEFT])
     ).astype(bf16)
@@ -510,9 +589,13 @@
         if index:
             piece = pltpu.roll(piece, index * ROPE, 1)
         packed = jnp.where(small // ROPE == index, piece, packed)
-    packed = (score_scale * packed).astype(bf16)
-    for index in range(rope_ref.shape[0]):
-        rope_ref[index] = packed
+    rope_ref[...] = (score_scale * packed).astype(bf16)
+
+
+def pair_sum_kernel(own_ref, other_ref, out_ref):
+    total = (own_ref[...].astype(f32) + other_ref[...].astype(f32)).astype(bf16)
+    for index in range(out_ref.shape[0]):
+        out_ref[index] = total
 
 
 def rope_kernel(terms_ref, out_ref):
@@ -612,24 +695,40 @@
     same, weights = lax.optimization_barrier((same, weights))
     cross = swap(same)
 
-    attended, logs, send, all_keys, all_vals = call(
+    chunks = half // 2
+    same_keys, same_vals, same_scores, tops = call(
+        same_scores_kernel,
+        20,
+        (
+            shape_of(chunks, 2 * rows, 2 * width),
+            shape_of(chunks, 2 * rows, width),
+            shape_of(2, chunks, rows, 2 * rows, dtype=f32),
+            shape_of(2, rows, 2 * rows, dtype=f32),
+        ),
+        (),
+        1,
+        4,
+    )(place, same, *own)
+    attended, logs, send, cross_keys, cross_vals = call(
         functools.partial(forward_kernel, experts),
-        24,
+        20,
         (
             shape_of(rows, width),
             shape_of(rows, width, dtype=f32),
             shape_of(experts * TALL, width),
-            shape_of(half, 2 * rows, 2 * width),
-            shape_of(half, 2 * rows, width),
+            shape_of(chunks, 2 * rows, 2 * width),
+            shape_of(chunks, 2 * rows, width),
         ),
-        [pltpu.VMEM((2, half, rows, 2 * rows), f32)],
+        [pltpu.VMEM((2, chunks, rows, 2 * rows), f32)],
         1,
         10,
     )(
         place,
-        same,
         cross,
-        *own,
+        same_vals,
+        same_scores,
+        tops,
+        own_query_rows,
         *(held(value) for value in (hidden_in, norm_gain.reshape(1, width))),
         *(held(value) for value in (route, affinity, cotangent)),
     )
@@ -662,15 +761,34 @@
     )(home, hidden_in, attended, logs, route, affinity, cotangent)
     grad_same = exchange(messages, "ctx", by_core)
     grad_cross = swap(grad_same)
+    dk, dv = call(
+        same_key_kernel,
+        14,
+        (
+            shape_of(2, rows, 2 * width, dtype=f32),
+            shape_of(2, rows, width, dtype=f32),
+        ),
+        (),
+        1,
+        5,
+    )(place, same, grad_same, *own)
     gk_nope, g_values, rope_part = call(
         key_kernel,
         14,
-        (shape_of(rows, width), shape_of(rows, width), shape_of(experts, quarter, LANES)),
+        (shape_of(rows, width), shape_of(rows, width), shape_of(quarter, LANES)),
         (),
         1,
-        7,
-    )(place, same, cross, grad_same, grad_cross, *own)
-    rope_terms = exchange(rope_part, "exp")
+        6,
+    )(place, cross, grad_cross, own_key_rows, own[2], dk, dv)
+    line = experts // 2
+    rope_other = lax.ppermute(
+        rope_part, "exp", [(index, (index + line) % experts) for index in range(experts)]
+    )
+    rope_pairs = call(pair_sum_kernel, 2, shape_of(line, quarter, LANES), count=2)(
+        rope_part, rope_other
+    )
+    by_line = [[part * line + index for index in range(line)] for part in range(2)]
+    rope_terms = exchange(rope_pairs, "exp", by_line)
     gq_nope, gq_rope = call(
         query_kernel,
         14,
@@ -681,8 +799,8 @@
             pltpu.VMEM((2, rows, 2 * width), f32),
         ],
         1,
-        5,
-    )(place, all_keys, all_vals, own_query_rows, grad_hidden, stats)
+        7,
+    )(place, same_keys, same_vals, cross_keys, cross_vals, own_query_rows, grad_hidden, stats)
     gk_rope = call(rope_kernel, 4, shape_of(ROPE, rows), count=1)(rope_terms)
     return (layer_out, grad_hidden, gq_nope, gq_rope.T, gk_nope, gk_rope.T, g_values)
 

time: 206 us -> 199 us (0.966); the launches traced: 206 us -> 195 us
  waiting for transfers between devices: 27.6 us -> 12.5 us
  Pallas kernels: 22.9 us -> 25.5 us
    all_to_all x1, waiting for transfers between devices: 24.3 us -> 10.3 us  [exchange(): lax.all_to_all(blocks, axis, 0, 0, tiled=True, axis_index_groups=groups)]
    pallas_call x1 -> x4, Pallas kernels: 5.02 us -> 9.55 us  [the longest x1 3.78 us: per_device(): call(functools.partial(forward_kernel, experts), 20, (shape_of(rows, widt...]
    ppermute x3, waiting for transfers between devices: 3.32 us -> 0.12 us  [swap(): return lax.ppermute(value, 'ctx', across)]
    pallas_call x1, Pallas kernels: 6.19 us -> 3.86 us  [per_device(): call(key_kernel, 14, (shape_of(rows, width), shape_of(rows, width), shape...]
    ppermute x0 -> x1, starting transfers between devices: none -> 2.29 us  [per_device(): lax.ppermute(rope_part, 'exp', [(index, (index + line) % experts) for ind...]
    ppermute x0 -> x1, waiting for transfers between devices: none -> 2.13 us  [per_device(): lax.ppermute(rope_part, 'exp', [(index, (index + line) % experts) for ind...]
  transfers between devices with their start and end apart: 4 -> 5, of which waited for: 3 -> 3; matrix products, arithmetic and copies ran while one was open for 0% -> 0% of each run, Pallas kernels for 1% -> 4%
where the time goes in v6:
time: 199 us; the launch traced here: 195 us
  blocking collectives  130 us (65%)
  starting transfers between devices  25.6 us (13%)
  Pallas kernels  25.5 us (13%)
  waiting for transfers between devices  12.5 us (6%)
    all_to_all x6, blocking collectives, exchange(): lax.all_to_all(blocks, axis, 0, 0, tiled=True, axis_index_groups=groups)  130 us
    ppermute x3, starting transfers between devices, swap(): return lax.ppermute(value, 'ctx', across)  19.8 us
    all_to_all x1, waiting for transfers between devices, exchange(): lax.all_to_all(blocks, axis, 0, 0, tiled=True, axis_index_groups=groups)  10.3 us
    pallas_call x1, Pallas kernels, per_device(): call(expert_kernel, 24, shape_of(half * PAIR, D), count=4)  4.55 us
  transfers between devices with their start and end apart: 5, of which 3 were waited for; matrix products, arithmetic and copies ran while one was open for 0% of the time, Pallas kernels for 4%

profile of v6, /device:TPU:1, one launch (start us, length us, event | category | flops | bytes accessed | tf_op | source)
XLA Modules:
  0.0 194.8 jit_solution(2152236141730112267)
XLA Ops:
  0.6 2.2 %shard_map.180 = (bf16[192,256]{1,0:T(8,128)(2,1)S(1)}, bf16[192,256]{1,0:T(8,128)(2,1)S(1)}, bf16[8,224,256]{2,1,0:T(8,128)(2,1)S(1)}, bf16[12288,128]{1,0:T(8,128)(2,1)S(1)}) custom-call(s32[1]{0:T(128)} %bitcast.place_ref, bf16[192,128]{1,0:T(8,128)(2,1)} %key_nope_hbm.1, bf16[32,192]{1,0:T(8,128)(2,1)} %bitcast.29, bf16[64,192]{1,0:T(8,128)(2,1)} %bitcast.28, ...), custom_call_target="tpu_custom_call" | custom-call | tf_op jit(solution)/shard_map/pallas_call | solution.py:667
  2.8 8.8 %collective-permute-start = (bf16[12288,128]{1,0:T(8,128)(2,1)S(1)}, bf16[12288,128]{1,0:T(8,128)(2,1)S(1)}, u32[]{:S(2)}, u32[]{:S(2)}) collective-permute-start(bf16[12288,128]{1,0:T(8,128)(2,1)S(1)} %get-tuple-element.48.own_ref), channel_id=1, source_target_pairs={{0,32},{32,0},{64,96},{96,64},{128,160},{160,128},{192,224},{224,1... | collective-permute-start | bytes 9437192 | tf_op jit(solution)/shard_map/ppermute | solution.py:661
  11.6 17.6 %all_to_all.35.same_ref = bf16[8,224,256]{2,1,0:T(8,128)(2,1)S(1)} all-to-all(bf16[8,224,256]{2,1,0:T(8,128)(2,1)S(1)} %get-tuple-element.37), channel_id=1, replica_groups={{0,64,128,192,256,320,384,448},{32,96,160,224,288,352,416,480},{1,65,12..., dimensions={0} | all-to-all | bytes 1835008 | tf_op jit(solution)/shard_map/all_to_all | solution.py:635
  29.3 0.0 collective-permute-done.other_ref
  29.3 3.2 %collective-permute-start.1 = (bf16[8,224,256]{2,1,0:T(8,128)(2,1)S(1)}, bf16[8,224,256]{2,1,0:T(8,128)(2,1)S(1)}, u32[]{:S(2)}, u32[]{:S(2)}) collective-permute-start(bf16[8,224,256]{2,1,0:T(8,128)(2,1)S(1)} %all_to_all.35.same_ref), channel_id=1, source_target_pairs={{0,32},{32,0},{64,96},{96,64},{128,160},{160,128},{192,224},{224,1... | collective-permute-start | bytes 2752520 | tf_op jit(solution)/shard_map/ppermute | solution.py:661
  32.4 2.0 %shard_map.181 = (bf16[4,384,256]{2,1,0:T(8,128)(2,1)S(1)}, bf16[4,384,128]{2,1,0:T(8,128)(2,1)S(1)}, f32[2,4,192,384]{3,2,1,0:T(8,128)S(1)}, f32[2,192,384]{2,1,0:T(8,128)S(1)}) custom-call(s32[1]{0:T(128)} %bitcast.place_ref, bf16[8,224,256]{2,1,0:T(8,128)(2,1)S(1)} %all_to_all.35.same_ref, bf16[192,256]{1,0:T(8,128)(2,1)S(1)} %get-tuple-element.40.own_key_ref, ...), custom_call_target="tpu_custom_call" | custom-call | tf_op jit(solution)/shard_map/pallas_call | solution.py:699
  34.4 0.1 collective-permute-done.1.cross_ref
  34.5 3.8 %shard_map.182 = (bf16[192,128]{1,0:T(8,128)(2,1)S(1)}, f32[192,128]{1,0:T(8,128)S(1)}, bf16[1024,128]{1,0:T(8,128)(2,1)S(1)}, bf16[4,384,256]{2,1,0:T(8,128)(2,1)S(1)}, bf16[4,384,128]{2,1,0:T(8,128)(2,1)S(1)}) custom-call(s32[1]{0:T(128)} %bitcast.place_ref, bf16[8,224,256]{2,1,0:T(8,128)(2,1)S(1)} %collective-permute-done.1.cross_ref, ...), custom_call_target="tpu_custom_call" | custom-call | tf_op jit(solution)/shard_map/pallas_call | solution.py:712
  38.3 34.2 %all_to_all.36 = bf16[32,32,128]{2,1,0:T(8,128)(2,1)S(1)} all-to-all(bf16[32,32,128]{2,1,0:T(8,128)(2,1)S(1)} %bitcast.20), channel_id=1, replica_groups=mesh['ctx'=16,'exp'=32] {'exp'}, dimensions={0} | all-to-all | bytes 524288 | tf_op jit(solution)/shard_map/all_to_all | solution.py:635
  72.5 0.4 shard_map.183
  72.9 22.5 %all_to_all.37 = bf16[8,24,4096]{2,1,0:T(8,128)(2,1)S(1)} all-to-all(bf16[8,24,4096]{2,1,0:T(8,128)(2,1)S(1)} %get-tuple-element.46), channel_id=1, replica_groups={{0,64,128,192,256,320,384,448},{32,96,160,224,288,352,416,480},{1,65,12..., dimensions={0} | all-to-all | bytes 3145728 | tf_op jit(solution)/shard_map/all_to_all | solution.py:635
  95.4 4.6 %shard_map.184 = bf16[192,4096]{1,0:T(8,128)(2,1)S(1)} custom-call(bf16[192,4096]{1,0:T(8,128)(2,1)S(1)} %bitcast.16, f32[1,4096]{1,0:T(1,128)S(1)} %get-tuple-element.47.gain_ref, bf16[12288,128]{1,0:T(8,128)(2,1)S(1)} %get-tuple-element.48.own_ref, bf16[12288,128]{1,0:T(8,128)(2,1)S(1)} %collective-permute-done.other_ref), custom_call_target="tpu_custom_call" | custom-call | tf_op jit(solution)/shard_map/pallas_call | solution.py:743
  100.0 20.5 %all_to_all.38.terms_ref = bf16[8,24,4096]{2,1,0:T(8,128)(2,1)S(1)} all-to-all(bf16[8,24,4096]{2,1,0:T(8,128)(2,1)S(1)} %bitcast.17), channel_id=1, replica_groups={{0,64,128,192,256,320,384,448},{32,96,160,224,288,352,416,480},{1,65,12..., dimensions={0} | all-to-all | bytes 3145728 | tf_op jit(solution)/shard_map/all_to_all | solution.py:635
  120.5 0.5 shard_map.185
  121.0 23.6 %all_to_all.39 = bf16[32,24,128]{2,1,0:T(8,128)(2,1)S(1)} all-to-all(bf16[32,24,128]{2,1,0:T(8,128)(2,1)S(1)} %shard_map.185), channel_id=1, replica_groups=mesh['ctx'=16,'exp'=32] {'exp'}, dimensions={0} | all-to-all | bytes 393216 | tf_op jit(solution)/shard_map/all_to_all | solution.py:635
  144.6 0.0 copy-done
  144.6 0.0 copy-done.1
  144.6 0.0 copy-done.3
  144.6 1.5 shard_map.186
  146.1 11.9 %all_to_all.40.grad_same_ref = bf16[8,224,128]{2,1,0:T(8,128)(2,1)S(1)} all-to-all(bf16[8,224,128]{2,1,0:T(8,128)(2,1)S(1)} %get-tuple-element.61), channel_id=1, replica_groups={{0,64,128,192,256,320,384,448},{32,96,160,224,288,352,416,480},{1,65,12..., dimensions={0} | all-to-all | bytes 917504 | tf_op jit(solution)/shard_map/all_to_all | solution.py:635
  158.0 7.9 %collective-permute-start.2 = (bf16[8,224,128]{2,1,0:T(8,128)(2,1)S(1)}, bf16[8,224,128]{2,1,0:T(8,128)(2,1)S(1)}, u32[]{:S(2)}, u32[]{:S(2)}) collective-permute-start(bf16[8,224,128]{2,1,0:T(8,128)(2,1)S(1)} %all_to_all.40.grad_same_ref), channel_id=1, source_target_pairs={{0,32},{32,0},{64,96},{96,64},{128,160},{160,128},{192,224},{224,1... | collective-permute-start | bytes 1376264 | tf_op jit(solution)/shard_map/ppermute | solution.py:661
  165.9 3.1 %shard_map.188 = (f32[2,192,256]{2,1,0:T(8,128)S(1)}, f32[2,192,128]{2,1,0:T(8,128)S(1)}) custom-call(s32[1]{0:T(128)} %bitcast.place_ref, bf16[8,224,256]{2,1,0:T(8,128)(2,1)S(1)} %all_to_all.35.same_ref, bf16[8,224,128]{2,1,0:T(8,128)(2,1)S(1)} %all_to_all.40.grad_same_ref, bf16[192,256]{1,0:T(8,128)(2,1)S(1)} %get-tuple-element.40.own_key_ref, ...), custom_call_target="tpu_custom_call" | custom-call | tf_op jit(solution)/shard_map/pallas_call | solution.py:764
  169.0 0.0 copy-start.2
  169.0 0.0 collective-permute-done.2.grad_cross_ref
  169.0 3.9 %shard_map.189 = (bf16[192,128]{1,0:T(8,128)(2,1)}, bf16[192,128]{1,0:T(8,128)(2,1)}, bf16[48,128]{1,0:T(8,128)(2,1)S(1)}) custom-call(s32[1]{0:T(128)} %bitcast.place_ref, bf16[8,224,256]{2,1,0:T(8,128)(2,1)S(1)} %collective-permute-done.1.cross_ref, bf16[8,224,128]{2,1,0:T(8,128)(2,1)S(1)} %collective-permute-done.2.grad_cross_ref, ...), custom_call_target="tpu_custom_call" | custom-call | tf_op jit(solution)/shard_map/pallas_call | solution.py:775
  172.9 2.3 %collective-permute-start.3 = (bf16[48,128]{1,0:T(8,128)(2,1)S(1)}, bf16[48,128]{1,0:T(8,128)(2,1)S(1)}, u32[]{:S(2)}, u32[]{:S(2)}) collective-permute-start(bf16[48,128]{1,0:T(8,128)(2,1)S(1)} %get-tuple-element.65.own_ref), channel_id=1, source_target_pairs={{0,16},{1,17},{2,18},{3,19},{4,20},{5,21},{6,22},{7,23},{8,24},{9,... | collective-permute-start | bytes 36872 | tf_op jit(solution)/shard_map/ppermute | solution.py:784
  175.2 2.1 %collective-permute-done.3.other_ref = bf16[48,128]{1,0:T(8,128)(2,1)S(1)} collective-permute-done((bf16[48,128]{1,0:T(8,128)(2,1)S(1)}, bf16[48,128]{1,0:T(8,128)(2,1)S(1)}, u32[]{:S(2)}, u32[]{:S(2)}) %collective-permute-start.3) | collective-permute-done | bytes 12320 | tf_op jit(solution)/shard_map/ppermute | solution.py:784
  177.3 0.7 shard_map.190
  178.0 3.5 %all-to-all-start.6 = ((bf16[16,48,128]{2,1,0:T(8,128)(2,1)}), bf16[16,48,128]{2,1,0:T(8,128)(2,1)S(1)}, u32[]{:S(2)}, u32[]{:S(2)}) async-start(bf16[16,48,128]{2,1,0:T(8,128)(2,1)} %shard_map.190), calls=%async_computation.6 | async-start | bytes 393216 | tf_op jit(solution)/shard_map/all_to_all | solution.py:635
  181.6 2.1 %shard_map.187 = (bf16[192,128]{1,0:T(8,128)(2,1)}, bf16[64,192]{1,0:T(8,128)(2,1)}) custom-call(s32[1]{0:T(128)} %bitcast.place_ref, bf16[4,384,256]{2,1,0:T(8,128)(2,1)S(1)} %get-tuple-element.55.same_keys_ref, bf16[4,384,128]{2,1,0:T(8,128)(2,1)S(1)} %get-tuple-element.42.same_vals_ref, bf16[4,384,256]{2,1,0:T(8,128)(2,1)S(1)} %get-tuple-element.56.cross_keys_ref, ...), custom_call_target="tpu_custom_call" | custom-call | tf_op jit(solution)/shard_map/pallas_call | solution.py:792
  183.6 10.3 %all-to-all-done.6.terms_ref = bf16[16,48,128]{2,1,0:T(8,128)(2,1)S(1)} async-done(((bf16[16,48,128]{2,1,0:T(8,128)(2,1)}), bf16[16,48,128]{2,1,0:T(8,128)(2,1)S(1)}, u32[]{:S(2)}, u32[]{:S(2)}) %all-to-all-start.6) | async-done | bytes 196640 | tf_op jit(solution)/shard_map/all_to_all | solution.py:635
  193.9 0.9 shard_map.191
  (6 shorter events, 0.0 us)
Async XLA Ops:
  2.8 26.4 %collective-permute-start = (bf16[12288,128]{1,0:T(8,128)(2,1)S(1)}, bf16[12288,128]{1,0:T(8,128)(2,1)S(1)}, u32[]{:S(2)}, u32[]{:S(2)}) collective-permute-start(bf16[12288,128]{1,0:T(8,128)(2,1)S(1)} %get-tuple-element.48.own_ref), channel_id=1, source_target_pairs={{0,32},{32,0},{64,96},{96,64},{128,160},{160,128},{192,224},{224,1... | collective-permute-start | bytes 9437192 | tf_op jit(solution)/shard_map/ppermute | solution.py:661
  29.3 5.3 %collective-permute-start.1 = (bf16[8,224,256]{2,1,0:T(8,128)(2,1)S(1)}, bf16[8,224,256]{2,1,0:T(8,128)(2,1)S(1)}, u32[]{:S(2)}, u32[]{:S(2)}) collective-permute-start(bf16[8,224,256]{2,1,0:T(8,128)(2,1)S(1)} %all_to_all.35.same_ref), channel_id=1, source_target_pairs={{0,32},{32,0},{64,96},{96,64},{128,160},{160,128},{192,224},{224,1... | collective-permute-start | bytes 2752520 | tf_op jit(solution)/shard_map/ppermute | solution.py:661
  120.5 24.1 %copy-start = (bf16[192,128]{1,0:T(8,128)(2,1)S(1)}, bf16[192,128]{1,0:T(8,128)(2,1)}, u32[]{:S(2)}) copy-start(bf16[192,128]{1,0:T(8,128)(2,1)} %hidden_ref.3) | copy-start | bytes 147460
  120.5 24.1 %copy-start.1 = (bf16[192,128]{1,0:T(8,128)(2,1)S(1)}, bf16[192,128]{1,0:T(8,128)(2,1)}, u32[]{:S(2)}) copy-start(bf16[192,128]{1,0:T(8,128)(2,1)} %cotangent_ref.3) | copy-start | bytes 147460
  120.5 24.1 %copy-start.3 = (f32[192,8]{0,1:T(8,128)S(1)}, f32[192,8]{0,1:T(8,128)}, u32[]{:S(2)}) copy-start(f32[192,8]{0,1:T(8,128)} %param.21) | copy-start | bytes 18436
  120.5 24.1 %copy-start.4 = (s32[192]{0:T(256)S(1)}, s32[192]{0:T(256)}, u32[]{:S(2)}) copy-start(s32[192]{0:T(256)} %param.20) | copy-start | bytes 2308
  158.0 11.0 %collective-permute-start.2 = (bf16[8,224,128]{2,1,0:T(8,128)(2,1)S(1)}, bf16[8,224,128]{2,1,0:T(8,128)(2,1)S(1)}, u32[]{:S(2)}, u32[]{:S(2)}) collective-permute-start(bf16[8,224,128]{2,1,0:T(8,128)(2,1)S(1)} %all_to_all.40.grad_same_ref), channel_id=1, source_target_pairs={{0,32},{32,0},{64,96},{96,64},{128,160},{160,128},{192,224},{224,1... | collective-permute-start | bytes 1376264 | tf_op jit(solution)/shard_map/ppermute | solution.py:661
  169.0 12.5 %copy-start.2 = (bf16[192,128]{1,0:T(8,128)(2,1)S(1)}, bf16[192,128]{1,0:T(8,128)(2,1)}, u32[]{:S(2)}) copy-start(bf16[192,128]{1,0:T(8,128)(2,1)} %get-tuple-element.31.grad_ref) | copy-start | bytes 147460
  172.9 4.4 %collective-permute-start.3 = (bf16[48,128]{1,0:T(8,128)(2,1)S(1)}, bf16[48,128]{1,0:T(8,128)(2,1)S(1)}, u32[]{:S(2)}, u32[]{:S(2)}) collective-permute-start(bf16[48,128]{1,0:T(8,128)(2,1)S(1)} %get-tuple-element.65.own_ref), channel_id=1, source_target_pairs={{0,16},{1,17},{2,18},{3,19},{4,20},{5,21},{6,22},{7,23},{8,24},{9,... | collective-permute-start | bytes 36872 | tf_op jit(solution)/shard_map/ppermute | solution.py:784
  178.0 15.9 %all-to-all-start.6 = ((bf16[16,48,128]{2,1,0:T(8,128)(2,1)}), bf16[16,48,128]{2,1,0:T(8,128)(2,1)S(1)}, u32[]{:S(2)}, u32[]{:S(2)}) async-start(bf16[16,48,128]{2,1,0:T(8,128)(2,1)} %shard_map.190), calls=%async_computation.6 | async-start | bytes 393216 | tf_op jit(solution)/shard_map/all_to_all | solution.py:635

commit v7 on v6

--- a/solution.py
+++ b/solution.py
@@ -205,6 +205,37 @@
         copy.wait()
 
 
+def prepare_kernel(
+    experts,
+    route_ref,
+    affinity_ref,
+    cotangent_ref,
+    gain_ref,
+    table_ref,
+    base_ref,
+    home_ref,
+    share_ref,
+):
+    rows = cotangent_ref.shape[0]
+    share = gate_share_of(affinity_ref[...])
+    share_ref[...] = jnp.broadcast_to(share, (rows, LANES))
+    grad = (share * cotangent_ref[...].astype(f32)).astype(bf16)
+    slots = slots_along_rows(route_ref[...], experts)
+    line = lax.broadcasted_iota(jnp.int32, (experts * TALL, rows), 0)
+    table_ref[...] = (line == slots).astype(f32).astype(bf16)
+    grad_table = (line == slots + CAP).astype(f32).astype(bf16)
+    row = lax.broadcasted_iota(jnp.int32, (TALL, LANES), 0)
+    gains = jnp.zeros((TALL, LANES), f32)
+    for index, piece in enumerate(pieces_of(gain_ref[...], 3)):
+        gains = jnp.where(row == PAIR + index, piece, gains)
+    gains = jnp.broadcast_to(gains[None], (experts, TALL, LANES)).reshape(-1, LANES)
+    base_ref[...] = nn_dot(grad_table, grad) + gains
+    slots = slots_along_columns(route_ref[...], experts)
+    column = lanes_of((rows, experts * PAIR))
+    for index in range(2):
+        home_ref[index] = (column == slots + index * CAP).astype(f32).astype(bf16)
+
+
 def unpack_messages(messages_ref, keys_ref, vals_ref, rows):
     for index in range(messages_ref.shape[0]):
         chunk, part = index // 2, index % 2
@@ -253,18 +284,16 @@
 
 
 def forward_kernel(
-    experts,
     place_ref,
     cross_ref,
     same_vals_ref,
     same_scores_ref,
     tops_ref,
     own_query_ref,
+    table_ref,
+    base_ref,
     hidden_ref,
     gain_ref,
-    route_ref,
-    affinity_ref,
-    cotangent_ref,
     attended_ref,
     log_ref,
     send_ref,
@@ -297,19 +326,7 @@
     )
     hidden = hidden_ref[...].astype(f32) + attended.astype(f32)
     raised = (hidden * gain_ref[...]).astype(bf16)
-    share = gate_share_of(affinity_ref[...])
-    grad = (share * cotangent_ref[...].astype(f32)).astype(bf16)
-    slots = slots_along_rows(route_ref[...], experts)
-    line = lax.broadcasted_iota(jnp.int32, (experts * TALL, rows), 0)
-    raised_table = (line == slots).astype(f32).astype(bf16)
-    grad_table = (line == slots + CAP).astype(f32).astype(bf16)
-    row = lax.broadcasted_iota(jnp.int32, (TALL, LANES), 0)
-    gains = jnp.zeros((TALL, LANES), f32)
-    for index, piece in enumerate(pieces_of(gain_ref[...], 3)):
-        gains = jnp.where(row == PAIR + index, piece, gains)
-    gains = jnp.broadcast_to(gains[None], (experts, TALL, LANES)).reshape(-1, LANES)
-    sent = nn_dot(raised_table, raised) + nn_dot(grad_table, grad) + gains
-    send_ref[...] = sent.astype(bf16)
+    send_ref[...] = (nn_dot(table_ref[...], raised) + base_ref[...]).astype(bf16)
 
 
 def unfold_kernel(received_ref, rows_ref, own_ref, gain_ref):
@@ -385,13 +402,12 @@
 
 
 def combine_kernel(
-    experts,
     home_ref,
+    table_ref,
+    share_ref,
     hidden_ref,
     attended_ref,
     log_ref,
-    route_ref,
-    affinity_ref,
     cotangent_ref,
     layer_ref,
     grad_ref,
@@ -399,14 +415,12 @@
     message_ref,
 ):
     rows = hidden_ref.shape[0]
-    slots = slots_along_columns(route_ref[...], experts)
-    column = lanes_of((rows, experts * PAIR))
     home = home_ref[...]
-    token_out = nn_dot((column == slots).astype(f32).astype(bf16), home)
-    token_grad = nn_dot((column == slots + CAP).astype(f32).astype(bf16), home)
+    token_out = nn_dot(table_ref[0], home)
+    token_grad = nn_dot(table_ref[1], home)
     attended = attended_ref[...].astype(f32)
     hidden = hidden_ref[...].astype(f32) + attended
-    share = gate_share_of(affinity_ref[...])
+    share = share_ref[...]
     layer_ref[...] = (hidden + share * token_out).astype(bf16)
     grad = (cotangent_ref[...].astype(f32) + token_grad).astype(bf16)
     grad_ref[...] = grad
@@ -690,9 +704,23 @@
         *(held(value[0]) for value in (gate_weight, up_weight, down_weight)),
     )
     own = (own_key_rows, own_query_rows, held(values))
+    gain_row = held(norm_gain.reshape(1, width))
+    table, base, home_tables, share = call(
+        functools.partial(prepare_kernel, experts),
+        8,
+        (
+            shape_of(experts * TALL, rows),
+            shape_of(experts * TALL, width, dtype=f32),
+            shape_of(2, rows, experts * PAIR),
+            shape_of(rows, width, dtype=f32),
+        ),
+        count=4,
+    )(held(route), held(affinity), held(cotangent), gain_row)
     same = exchange(messages, "ctx", by_core)
     weights = (weights, swap(weights))
-    same, weights = lax.optimization_barrier((same, weights))
+    prepared = (table, base, home_tables, share)
+    same, weights, prepared = lax.optimization_barrier((same, weights, prepared))
+    table, base, home_tables, share = prepared
     cross = swap(same)
 
     chunks = half // 2
@@ -710,7 +738,7 @@
         4,
     )(place, same, *own)
     attended, logs, send, cross_keys, cross_vals = call(
-        functools.partial(forward_kernel, experts),
+        forward_kernel,
         20,
         (
             shape_of(rows, width),
@@ -721,7 +749,7 @@
         ),
         [pltpu.VMEM((2, chunks, rows, 2 * rows), f32)],
         1,
-        10,
+        9,
     )(
         place,
         cross,
@@ -729,8 +757,10 @@
         same_scores,
         tops,
         own_query_rows,
-        *(held(value) for value in (hidden_in, norm_gain.reshape(1, width))),
-        *(held(value) for value in (route, affinity, cotangent)),
+        held(table),
+        held(base),
+        held(hidden_in),
+        gain_row,
     )
     received = exchange(send.reshape(experts, TALL, width), "exp").reshape(-1, width)
     rows_all, own_rows, gain = call(
@@ -749,7 +779,7 @@
     )
     home = exchange(back, "exp").reshape(experts * PAIR, width)
     layer_out, grad_hidden, stats, messages = call(
-        functools.partial(combine_kernel, experts),
+        combine_kernel,
         8,
         (
             shape_of(rows, width),
@@ -758,7 +788,7 @@
             shape_of(half, tall, width),
         ),
         count=7,
-    )(home, hidden_in, attended, logs, route, affinity, cotangent)
+    )(home, home_tables, share, hidden_in, attended, logs, cotangent)
     grad_same = exchange(messages, "ctx", by_core)
     grad_cross = swap(grad_same)
     dk, dv = call(

time: 199 us -> 203 us (1.020)
  blocking collectives: 130 us -> 112 us
  waiting for transfers between devices: 12.5 us -> 23.2 us
  Pallas kernels: 25.5 us -> 31.3 us
  local copies, waits for them, and re-layouts: 0.02 us -> 3.16 us
  starting transfers between devices: 25.6 us -> 28.7 us
    all_to_all x6 -> x5, blocking collectives: 130 us -> 112 us  [exchange(): lax.all_to_all(blocks, axis, 0, 0, tiled=True, axis_index_groups=groups)]
    all_to_all x1 -> x2, waiting for transfers between devices: 10.3 us -> 20.9 us  [exchange(): lax.all_to_all(blocks, axis, 0, 0, tiled=True, axis_index_groups=groups)]
    all_to_all x1 -> x2, starting transfers between devices: 3.52 us -> 7.08 us  [exchange(): lax.all_to_all(blocks, axis, 0, 0, tiled=True, axis_index_groups=groups)]
    unnamed x10 -> x22, local copies, waits for them, and re-layouts: 0.02 us -> 3.16 us
    pallas_call x1, Pallas kernels: 4.55 us -> 7.39 us  [per_device(): call(expert_kernel, 24, shape_of(half * PAIR, D), count=4)]
    pallas_call x2 -> x3, Pallas kernels: 5.33 us -> 6.34 us  [the longest x1 3.92 us: per_device(): call(forward_kernel, 20, (shape_of(rows, width), shape_of(rows, width, dt...]
  transfers between devices with their start and end apart: 5 -> 6, of which waited for: 3 -> 4; matrix products, arithmetic and copies ran while one was open for 0% -> 0% of each run, Pallas kernels for 4% -> 4%
where the time goes in v7:
time: 203 us; the launch traced here: 199 us
  blocking collectives  112 us (55%)
  Pallas kernels  31.3 us (15%)
  starting transfers between devices  28.7 us (14%)
  waiting for transfers between devices  23.2 us (11%)
  local copies, waits for them, and re-layouts  3.16 us (2%)
    all_to_all x5, blocking collectives, exchange(): lax.all_to_all(blocks, axis, 0, 0, tiled=True, axis_index_groups=groups)  112 us
    all_to_all x2, waiting for transfers between devices, exchange(): lax.all_to_all(blocks, axis, 0, 0, tiled=True, axis_index_groups=groups)  20.9 us
    ppermute x3, starting transfers between devices, swap(): return lax.ppermute(value, 'ctx', across)  19.3 us
    pallas_call x1, Pallas kernels, per_device(): call(expert_kernel, 24, shape_of(half * PAIR, D), count=4)  7.39 us
    all_to_all x2, starting transfers between devices, exchange(): lax.all_to_all(blocks, axis, 0, 0, tiled=True, axis_index_groups=groups)  7.08 us
    pallas_call x1, Pallas kernels, per_device(): call(pack_kernel, 12, (shape_of(rows, 2 * width), shape_of(rows, 2 * widt...  4.12 us
  transfers between devices with their start and end apart: 6, of which 4 were waited for; matrix products, arithmetic and copies ran while one was open for 0% of the time, Pallas kernels for 4%

profile of v7, /device:TPU:1, one launch (start us, length us, event | category | flops | bytes accessed | tf_op | source)
XLA Modules:
  0.0 199.4 jit_solution(12692379530985334180)
XLA Ops:
  0.6 4.1 %shard_map.180 = (bf16[192,256]{1,0:T(8,128)(2,1)S(1)}, bf16[192,256]{1,0:T(8,128)(2,1)S(1)}, bf16[8,224,256]{2,1,0:T(8,128)(2,1)}, bf16[12288,128]{1,0:T(8,128)(2,1)}) custom-call(s32[1]{0:T(128)} %bitcast.place_ref, bf16[192,128]{1,0:T(8,128)(2,1)} %key_nope_hbm.1, bf16[32,192]{1,0:T(8,128)(2,1)} %bitcast.25, bf16[64,192]{1,0:T(8,128)(2,1)} %bitcast.24, ...), custom_call_target="tpu_custom_call" | custom-call | tf_op jit(solution)/shard_map/pallas_call | solution.py:681
  4.8 8.8 %collective-permute-start = (bf16[12288,128]{1,0:T(8,128)(2,1)}, bf16[12288,128]{1,0:T(8,128)(2,1)}, u32[]{:S(2)}, u32[]{:S(2)}) collective-permute-start(bf16[12288,128]{1,0:T(8,128)(2,1)} %get-tuple-element.62.own_ref), channel_id=1, source_target_pairs={{0,32},{32,0},{64,96},{96,64},{128,160},{160,128},{192,224},{224,1... | collective-permute-start | bytes 9437192 | tf_op jit(solution)/shard_map/ppermute | solution.py:675
  13.6 3.6 %all-to-all-start = ((bf16[8,224,256]{2,1,0:T(8,128)(2,1)}), bf16[8,224,256]{2,1,0:T(8,128)(2,1)S(1)}, u32[]{:S(2)}, u32[]{:S(2)}) async-start(bf16[8,224,256]{2,1,0:T(8,128)(2,1)} %get-tuple-element.45), calls=%async_computation | async-start | bytes 1835008 | tf_op jit(solution)/shard_map/all_to_all | solution.py:649
  17.1 1.5 shard_map.181
  18.6 0.8 copy-done
  19.4 0.8 copy-done.2
  20.3 0.8 copy-done.3
  21.1 0.6 copy-done.8
  21.8 10.7 %all-to-all-done.same_ref = bf16[8,224,256]{2,1,0:T(8,128)(2,1)S(1)} async-done(((bf16[8,224,256]{2,1,0:T(8,128)(2,1)}), bf16[8,224,256]{2,1,0:T(8,128)(2,1)S(1)}, u32[]{:S(2)}, u32[]{:S(2)}) %all-to-all-start) | async-done | bytes 917536 | tf_op jit(solution)/shard_map/all_to_all | solution.py:649
  32.5 2.7 %collective-permute-start.1 = (bf16[8,224,256]{2,1,0:T(8,128)(2,1)S(1)}, bf16[8,224,256]{2,1,0:T(8,128)(2,1)S(1)}, u32[]{:S(2)}, u32[]{:S(2)}) collective-permute-start(bf16[8,224,256]{2,1,0:T(8,128)(2,1)S(1)} %all-to-all-done.same_ref), channel_id=1, source_target_pairs={{0,32},{32,0},{64,96},{96,64},{128,160},{160,128},{192,224},{224,1... | collective-permute-start | bytes 2752520 | tf_op jit(solution)/shard_map/ppermute | solution.py:675
  35.2 2.0 shard_map.182
  37.1 0.1 collective-permute-done.1.cross_ref
  37.2 3.9 %shard_map.183 = (bf16[192,128]{1,0:T(8,128)(2,1)S(1)}, f32[192,128]{1,0:T(8,128)S(1)}, bf16[1024,128]{1,0:T(8,128)(2,1)S(1)}, bf16[4,384,256]{2,1,0:T(8,128)(2,1)S(1)}, bf16[4,384,128]{2,1,0:T(8,128)(2,1)S(1)}) custom-call(s32[1]{0:T(128)} %bitcast.place_ref, bf16[8,224,256]{2,1,0:T(8,128)(2,1)S(1)} %collective-permute-done.1.cross_ref, ...), custom_call_target="tpu_custom_call" | custom-call | tf_op jit(solution)/shard_map/pallas_call | solution.py:740
  41.2 32.9 %all_to_all.35 = bf16[32,32,128]{2,1,0:T(8,128)(2,1)S(1)} all-to-all(bf16[32,32,128]{2,1,0:T(8,128)(2,1)S(1)} %bitcast.20), channel_id=1, replica_groups=mesh['ctx'=16,'exp'=32] {'exp'}, dimensions={0} | all-to-all | bytes 524288 | tf_op jit(solution)/shard_map/all_to_all | solution.py:649
  74.0 0.4 shard_map.184
  74.4 23.3 %all_to_all.36 = bf16[8,24,4096]{2,1,0:T(8,128)(2,1)S(1)} all-to-all(bf16[8,24,4096]{2,1,0:T(8,128)(2,1)S(1)} %get-tuple-element.60), channel_id=1, replica_groups={{0,64,128,192,256,320,384,448},{32,96,160,224,288,352,416,480},{1,65,12..., dimensions={0} | all-to-all | bytes 3145728 | tf_op jit(solution)/shard_map/all_to_all | solution.py:649
  97.7 7.4 %shard_map.185 = bf16[192,4096]{1,0:T(8,128)(2,1)S(1)} custom-call(bf16[192,4096]{1,0:T(8,128)(2,1)S(1)} %bitcast.16, f32[1,4096]{1,0:T(1,128)S(1)} %get-tuple-element.61.gain_ref, bf16[12288,128]{1,0:T(8,128)(2,1)} %get-tuple-element.62.own_ref, bf16[12288,128]{1,0:T(8,128)(2,1)} %collective-permute-done.other_ref), custom_call_target="tpu_custom_call" | custom-call | tf_op jit(solution)/shard_map/pallas_call | solution.py:773
  105.1 20.6 %all_to_all.37.terms_ref = bf16[8,24,4096]{2,1,0:T(8,128)(2,1)S(1)} all-to-all(bf16[8,24,4096]{2,1,0:T(8,128)(2,1)S(1)} %bitcast.17), channel_id=1, replica_groups={{0,64,128,192,256,320,384,448},{32,96,160,224,288,352,416,480},{1,65,12..., dimensions={0} | all-to-all | bytes 3145728 | tf_op jit(solution)/shard_map/all_to_all | solution.py:649
  125.7 0.5 shard_map.186
  126.2 23.6 %all_to_all.38 = bf16[32,24,128]{2,1,0:T(8,128)(2,1)S(1)} all-to-all(bf16[32,24,128]{2,1,0:T(8,128)(2,1)S(1)} %shard_map.186), channel_id=1, replica_groups=mesh['ctx'=16,'exp'=32] {'exp'}, dimensions={0} | all-to-all | bytes 393216 | tf_op jit(solution)/shard_map/all_to_all | solution.py:649
  149.8 0.9 shard_map.187
  150.7 11.9 %all_to_all.39.grad_same_ref = bf16[8,224,128]{2,1,0:T(8,128)(2,1)S(1)} all-to-all(bf16[8,224,128]{2,1,0:T(8,128)(2,1)S(1)} %get-tuple-element.77), channel_id=1, replica_groups={{0,64,128,192,256,320,384,448},{32,96,160,224,288,352,416,480},{1,65,12..., dimensions={0} | all-to-all | bytes 917504 | tf_op jit(solution)/shard_map/all_to_all | solution.py:649
  162.6 7.9 %collective-permute-start.2 = (bf16[8,224,128]{2,1,0:T(8,128)(2,1)S(1)}, bf16[8,224,128]{2,1,0:T(8,128)(2,1)S(1)}, u32[]{:S(2)}, u32[]{:S(2)}) collective-permute-start(bf16[8,224,128]{2,1,0:T(8,128)(2,1)S(1)} %all_to_all.39.grad_same_ref), channel_id=1, source_target_pairs={{0,32},{32,0},{64,96},{96,64},{128,160},{160,128},{192,224},{224,1... | collective-permute-start | bytes 1376264 | tf_op jit(solution)/shard_map/ppermute | solution.py:675
  170.5 3.1 %shard_map.189 = (f32[2,192,256]{2,1,0:T(8,128)S(1)}, f32[2,192,128]{2,1,0:T(8,128)S(1)}) custom-call(s32[1]{0:T(128)} %bitcast.place_ref, bf16[8,224,256]{2,1,0:T(8,128)(2,1)S(1)} %all-to-all-done.same_ref, bf16[8,224,128]{2,1,0:T(8,128)(2,1)S(1)} %all_to_all.39.grad_same_ref, bf16[192,256]{1,0:T(8,128)(2,1)S(1)} %get-tuple-element.52.own_key_ref, ...), custom_call_target="tpu_custom_call" | custom-call | tf_op jit(solution)/shard_map/pallas_call | solution.py:794
  173.6 3.9 %shard_map.190 = (bf16[192,128]{1,0:T(8,128)(2,1)}, bf16[192,128]{1,0:T(8,128)(2,1)}, bf16[48,128]{1,0:T(8,128)(2,1)S(1)}) custom-call(s32[1]{0:T(128)} %bitcast.place_ref, bf16[8,224,256]{2,1,0:T(8,128)(2,1)S(1)} %collective-permute-done.1.cross_ref, bf16[8,224,128]{2,1,0:T(8,128)(2,1)S(1)} %collective-permute-done.2.grad_cross_ref, ...), custom_call_target="tpu_custom_call" | custom-call | tf_op jit(solution)/shard_map/pallas_call | solution.py:805
  177.5 2.3 %collective-permute-start.3 = (bf16[48,128]{1,0:T(8,128)(2,1)S(1)}, bf16[48,128]{1,0:T(8,128)(2,1)S(1)}, u32[]{:S(2)}, u32[]{:S(2)}) collective-permute-start(bf16[48,128]{1,0:T(8,128)(2,1)S(1)} %get-tuple-element.81.own_ref), channel_id=1, source_target_pairs={{0,16},{1,17},{2,18},{3,19},{4,20},{5,21},{6,22},{7,23},{8,24},{9,... | collective-permute-start | bytes 36872 | tf_op jit(solution)/shard_map/ppermute | solution.py:814
  179.8 2.1 %collective-permute-done.3.other_ref = bf16[48,128]{1,0:T(8,128)(2,1)S(1)} collective-permute-done((bf16[48,128]{1,0:T(8,128)(2,1)S(1)}, bf16[48,128]{1,0:T(8,128)(2,1)S(1)}, u32[]{:S(2)}, u32[]{:S(2)}) %collective-permute-start.3) | collective-permute-done | bytes 12320 | tf_op jit(solution)/shard_map/ppermute | solution.py:814
  182.0 0.7 shard_map.191
  182.6 3.5 %all-to-all-start.6 = ((bf16[16,48,128]{2,1,0:T(8,128)(2,1)}), bf16[16,48,128]{2,1,0:T(8,128)(2,1)S(1)}, u32[]{:S(2)}, u32[]{:S(2)}) async-start(bf16[16,48,128]{2,1,0:T(8,128)(2,1)} %shard_map.191), calls=%async_computation.6 | async-start | bytes 393216 | tf_op jit(solution)/shard_map/all_to_all | solution.py:649
  186.2 2.1 %shard_map.188 = (bf16[192,128]{1,0:T(8,128)(2,1)}, bf16[64,192]{1,0:T(8,128)(2,1)}) custom-call(s32[1]{0:T(128)} %bitcast.place_ref, bf16[4,384,256]{2,1,0:T(8,128)(2,1)S(1)} %get-tuple-element.71.same_keys_ref, bf16[4,384,128]{2,1,0:T(8,128)(2,1)S(1)} %get-tuple-element.54.same_vals_ref, bf16[4,384,256]{2,1,0:T(8,128)(2,1)S(1)} %get-tuple-element.72.cross_keys_ref, ...), custom_call_target="tpu_custom_call" | custom-call | tf_op jit(solution)/shard_map/pallas_call | solution.py:822
  188.3 10.3 %all-to-all-done.6.terms_ref = bf16[16,48,128]{2,1,0:T(8,128)(2,1)S(1)} async-done(((bf16[16,48,128]{2,1,0:T(8,128)(2,1)}), bf16[16,48,128]{2,1,0:T(8,128)(2,1)S(1)}, u32[]{:S(2)}, u32[]{:S(2)}) %all-to-all-start.6) | async-done | bytes 196640 | tf_op jit(solution)/shard_map/all_to_all | solution.py:649
  198.5 0.9 shard_map.192
  (20 shorter events, 0.0 us)
Async XLA Ops:
  4.8 27.7 %collective-permute-start = (bf16[12288,128]{1,0:T(8,128)(2,1)}, bf16[12288,128]{1,0:T(8,128)(2,1)}, u32[]{:S(2)}, u32[]{:S(2)}) collective-permute-start(bf16[12288,128]{1,0:T(8,128)(2,1)} %get-tuple-element.62.own_ref), channel_id=1, source_target_pairs={{0,32},{32,0},{64,96},{96,64},{128,160},{160,128},{192,224},{224,1... | collective-permute-start | bytes 9437192 | tf_op jit(solution)/shard_map/ppermute | solution.py:675
  13.6 18.9 %all-to-all-start = ((bf16[8,224,256]{2,1,0:T(8,128)(2,1)}), bf16[8,224,256]{2,1,0:T(8,128)(2,1)S(1)}, u32[]{:S(2)}, u32[]{:S(2)}) async-start(bf16[8,224,256]{2,1,0:T(8,128)(2,1)} %get-tuple-element.45), calls=%async_computation | async-start | bytes 1835008 | tf_op jit(solution)/shard_map/all_to_all | solution.py:649
  18.6 0.8 copy-start
  19.4 0.8 copy-start.2
  20.3 0.9 copy-start.3
  21.1 0.6 copy-start.8
  32.5 4.8 %collective-permute-start.1 = (bf16[8,224,256]{2,1,0:T(8,128)(2,1)S(1)}, bf16[8,224,256]{2,1,0:T(8,128)(2,1)S(1)}, u32[]{:S(2)}, u32[]{:S(2)}) collective-permute-start(bf16[8,224,256]{2,1,0:T(8,128)(2,1)S(1)} %all-to-all-done.same_ref), channel_id=1, source_target_pairs={{0,32},{32,0},{64,96},{96,64},{128,160},{160,128},{192,224},{224,1... | collective-permute-start | bytes 2752520 | tf_op jit(solution)/shard_map/ppermute | solution.py:675
  125.7 24.1 %copy-start.1 = (bf16[2,192,768]{2,1,0:T(8,128)(2,1)S(1)}, bf16[2,192,768]{2,1,0:T(8,128)(2,1)}, u32[]{:S(2)}) copy-start(bf16[2,192,768]{2,1,0:T(8,128)(2,1)} %copy-done) | copy-start | bytes 1769476
  125.7 24.1 %copy-start.4 = (bf16[192,128]{1,0:T(8,128)(2,1)S(1)}, bf16[192,128]{1,0:T(8,128)(2,1)}, u32[]{:S(2)}) copy-start(bf16[192,128]{1,0:T(8,128)(2,1)} %hidden_ref.3) | copy-start | bytes 147460
  125.7 24.1 %copy-start.5 = (bf16[192,128]{1,0:T(8,128)(2,1)S(1)}, bf16[192,128]{1,0:T(8,128)(2,1)}, u32[]{:S(2)}) copy-start(bf16[192,128]{1,0:T(8,128)(2,1)} %cotangent_ref.3) | copy-start | bytes 147460
  125.7 24.1 %copy-start.9 = (f32[192,128]{1,0:T(8,128)S(1)}, f32[192,128]{1,0:T(8,128)}, u32[]{:S(2)}) copy-start(f32[192,128]{1,0:T(8,128)} %copy-done.8) | copy-start | bytes 294916
  150.7 11.9 %copy-start.6 = (f32[192,128]{1,0:T(8,128)}, f32[192,128]{1,0:T(8,128)S(1)}, u32[]{:S(2)}) copy-start(f32[192,128]{1,0:T(8,128)S(1)} %get-tuple-element.74.stats_ref) | copy-start | bytes 294916
  162.6 11.0 %collective-permute-start.2 = (bf16[8,224,128]{2,1,0:T(8,128)(2,1)S(1)}, bf16[8,224,128]{2,1,0:T(8,128)(2,1)S(1)}, u32[]{:S(2)}, u32[]{:S(2)}) collective-permute-start(bf16[8,224,128]{2,1,0:T(8,128)(2,1)S(1)} %all_to_all.39.grad_same_ref), channel_id=1, source_target_pairs={{0,32},{32,0},{64,96},{96,64},{128,160},{160,128},{192,224},{224,1... | collective-permute-start | bytes 1376264 | tf_op jit(solution)/shard_map/ppermute | solution.py:675
  173.6 12.6 %copy-start.7 = (f32[192,128]{1,0:T(8,128)S(1)}, f32[192,128]{1,0:T(8,128)}, u32[]{:S(2)}) copy-start(f32[192,128]{1,0:T(8,128)} %copy-done.6) | copy-start | bytes 294916
  173.6 12.6 %copy-start.10 = (bf16[192,128]{1,0:T(8,128)(2,1)S(1)}, bf16[192,128]{1,0:T(8,128)(2,1)}, u32[]{:S(2)}) copy-start(bf16[192,128]{1,0:T(8,128)(2,1)} %get-tuple-element.39.grad_ref) | copy-start | bytes 147460
  177.5 4.4 %collective-permute-start.3 = (bf16[48,128]{1,0:T(8,128)(2,1)S(1)}, bf16[48,128]{1,0:T(8,128)(2,1)S(1)}, u32[]{:S(2)}, u32[]{:S(2)}) collective-permute-start(bf16[48,128]{1,0:T(8,128)(2,1)S(1)} %get-tuple-element.81.own_ref), channel_id=1, source_target_pairs={{0,16},{1,17},{2,18},{3,19},{4,20},{5,21},{6,22},{7,23},{8,24},{9,... | collective-permute-start | bytes 36872 | tf_op jit(solution)/shard_map/ppermute | solution.py:814
  182.6 15.9 %all-to-all-start.6 = ((bf16[16,48,128]{2,1,0:T(8,128)(2,1)}), bf16[16,48,128]{2,1,0:T(8,128)(2,1)S(1)}, u32[]{:S(2)}, u32[]{:S(2)}) async-start(bf16[16,48,128]{2,1,0:T(8,128)(2,1)} %shard_map.191), calls=%async_computation.6 | async-start | bytes 393216 | tf_op jit(solution)/shard_map/all_to_all | solution.py:649

commit v8 on v6

--- a/solution.py
+++ b/solution.py
@@ -321,7 +321,9 @@
         for copy in range(rows_ref.shape[0]):
             rows_ref[copy, :, at] = tile
         pieces = received_ref[start : start + TALL, :].astype(f32)[PAIR : PAIR + 3]
-        gain_ref[:, at] = pieces[0:1] + pieces[1:2] + pieces[2:3]
+        gain = pieces[0:1] + pieces[1:2] + pieces[2:3]
+        gain_ref[0:1, at] = gain
+        gain_ref[1:2, at] = 1.0 / gain
 
 
 def expert_kernel(rows_ref, gain_ref, own_ref, other_ref, out_ref):
@@ -346,7 +348,7 @@
     for index in range(D // wide):
         at = slice(index * wide, (index + 1) * wide)
         rows = rows_ref[:, at]
-        hidden = rows.astype(f32) / gain_ref[:, at]
+        hidden = rows.astype(f32) * gain_ref[1:2, at]
         squares = squares + hidden * hidden
         gate_val = gate_val + nn_dot(rows, side_by_side(0, index))
         up_val = up_val + nn_dot(rows, side_by_side(D, index))
@@ -373,9 +375,9 @@
     for index in range(1, terms_ref.shape[0]):
         total = total + terms_ref[index].astype(f32)
     raised = own_ref[...].astype(f32)
-    gain = gain_ref[...]
+    gain = gain_ref[0:1, :]
     back = jnp.concatenate([total[CAP:], total[:CAP]], 0)
-    hidden = raised / gain
+    hidden = raised * gain_ref[1:2, :]
     inverse = lax.rsqrt(jnp.sum(hidden * hidden, 1, keepdims=True) / D + norm_eps)
     cross = jnp.sum(back * raised, 1, keepdims=True) / D
     grad = inverse * (back * gain - hidden * (inverse * inverse * cross))
@@ -691,8 +693,6 @@
     )
     own = (own_key_rows, own_query_rows, held(values))
     same = exchange(messages, "ctx", by_core)
-    weights = (weights, swap(weights))
-    same, weights = lax.optimization_barrier((same, weights))
     cross = swap(same)
 
     chunks = half // 2
@@ -732,11 +732,13 @@
         *(held(value) for value in (hidden_in, norm_gain.reshape(1, width))),
         *(held(value) for value in (route, affinity, cotangent)),
     )
+    send, weights = lax.optimization_barrier((send, weights))
+    weights = (weights, swap(weights))
     received = exchange(send.reshape(experts, TALL, width), "exp").reshape(-1, width)
     rows_all, own_rows, gain = call(
         unfold_kernel,
         6,
-        (shape_of(half, PAIR, D), shape_of(PAIR, D), shape_of(1, D, dtype=f32)),
+        (shape_of(half, PAIR, D), shape_of(PAIR, D), shape_of(2, D, dtype=f32)),
         count=1,
     )(received)
     rows_all = exchange(rows_all, "ctx", by_core).reshape(half * PAIR, D)

time: 199 us -> 198 us (level)
  starting transfers between devices: 25.6 us -> 21.4 us
  blocking collectives: 130 us -> 134 us
    ppermute x3, starting transfers between devices: 19.8 us -> 15.6 us  [swap(): return lax.ppermute(value, 'ctx', across)]
    all_to_all x6, blocking collectives: 130 us -> 134 us  [exchange(): lax.all_to_all(blocks, axis, 0, 0, tiled=True, axis_index_groups=groups)]
where the time goes in v8:
time: 198 us; the launch traced here: 195 us
  blocking collectives  134 us (68%)
  Pallas kernels  25.5 us (13%)
  starting transfers between devices  21.4 us (11%)
  waiting for transfers between devices  12.5 us (6%)
    all_to_all x6, blocking collectives, exchange(): lax.all_to_all(blocks, axis, 0, 0, tiled=True, axis_index_groups=groups)  134 us
    ppermute x3, starting transfers between devices, swap(): return lax.ppermute(value, 'ctx', across)  15.6 us
    all_to_all x1, waiting for transfers between devices, exchange(): lax.all_to_all(blocks, axis, 0, 0, tiled=True, axis_index_groups=groups)  10.3 us
    pallas_call x1, Pallas kernels, per_device(): call(expert_kernel, 24, shape_of(half * PAIR, D), count=4)  4.56 us
  transfers between devices with their start and end apart: 5, of which 3 were waited for; matrix products, arithmetic and copies ran while one was open for 0% of the time, Pallas kernels for 4%

profile of v8, /device:TPU:1, one launch (start us, length us, event | category | flops | bytes accessed | tf_op | source)
XLA Modules:
  0.0 194.5 jit_solution(732879043953231301)
XLA Ops:
  0.6 2.2 %shard_map.180 = (bf16[192,256]{1,0:T(8,128)(2,1)S(1)}, bf16[192,256]{1,0:T(8,128)(2,1)S(1)}, bf16[8,224,256]{2,1,0:T(8,128)(2,1)S(1)}, bf16[12288,128]{1,0:T(8,128)(2,1)S(1)}) custom-call(s32[1]{0:T(128)} %bitcast.place_ref, bf16[192,128]{1,0:T(8,128)(2,1)} %key_nope_hbm.1, bf16[32,192]{1,0:T(8,128)(2,1)} %bitcast.29, bf16[64,192]{1,0:T(8,128)(2,1)} %bitcast.28, ...), custom_call_target="tpu_custom_call" | custom-call | tf_op jit(solution)/shard_map/pallas_call | solution.py:669
  2.8 20.3 %all_to_all.35.same_ref = bf16[8,224,256]{2,1,0:T(8,128)(2,1)S(1)} all-to-all(bf16[8,224,256]{2,1,0:T(8,128)(2,1)S(1)} %get-tuple-element.36), channel_id=1, replica_groups={{0,64,128,192,256,320,384,448},{32,96,160,224,288,352,416,480},{1,65,12..., dimensions={0} | all-to-all | bytes 1835008 | tf_op jit(solution)/shard_map/all_to_all | solution.py:637
  23.1 5.5 %collective-permute-start = (bf16[8,224,256]{2,1,0:T(8,128)(2,1)S(1)}, bf16[8,224,256]{2,1,0:T(8,128)(2,1)S(1)}, u32[]{:S(2)}, u32[]{:S(2)}) collective-permute-start(bf16[8,224,256]{2,1,0:T(8,128)(2,1)S(1)} %all_to_all.35.same_ref), channel_id=1, source_target_pairs={{0,32},{32,0},{64,96},{96,64},{128,160},{160,128},{192,224},{224,1... | collective-permute-start | bytes 2752520 | tf_op jit(solution)/shard_map/ppermute | solution.py:663
  28.6 2.0 %shard_map.181 = (bf16[4,384,256]{2,1,0:T(8,128)(2,1)S(1)}, bf16[4,384,128]{2,1,0:T(8,128)(2,1)S(1)}, f32[2,4,192,384]{3,2,1,0:T(8,128)S(1)}, f32[2,192,384]{2,1,0:T(8,128)S(1)}) custom-call(s32[1]{0:T(128)} %bitcast.place_ref, bf16[8,224,256]{2,1,0:T(8,128)(2,1)S(1)} %all_to_all.35.same_ref, bf16[192,256]{1,0:T(8,128)(2,1)S(1)} %get-tuple-element.37.own_key_ref, ...), custom_call_target="tpu_custom_call" | custom-call | tf_op jit(solution)/shard_map/pallas_call | solution.py:699
  30.5 0.1 collective-permute-done.cross_ref
  30.7 3.8 %shard_map.182 = (bf16[192,128]{1,0:T(8,128)(2,1)S(1)}, f32[192,128]{1,0:T(8,128)S(1)}, bf16[1024,128]{1,0:T(8,128)(2,1)S(1)}, bf16[4,384,256]{2,1,0:T(8,128)(2,1)S(1)}, bf16[4,384,128]{2,1,0:T(8,128)(2,1)S(1)}) custom-call(s32[1]{0:T(128)} %bitcast.place_ref, bf16[8,224,256]{2,1,0:T(8,128)(2,1)S(1)} %collective-permute-done.cross_ref, ...), custom_call_target="tpu_custom_call" | custom-call | tf_op jit(solution)/shard_map/pallas_call | solution.py:712
  34.4 2.3 %collective-permute-start.1 = (bf16[12288,128]{1,0:T(8,128)(2,1)S(1)}, bf16[12288,128]{1,0:T(8,128)(2,1)S(1)}, u32[]{:S(2)}, u32[]{:S(2)}) collective-permute-start(bf16[12288,128]{1,0:T(8,128)(2,1)S(1)} %get-tuple-element.47.own_ref), channel_id=1, source_target_pairs={{0,32},{32,0},{64,96},{96,64},{128,160},{160,128},{192,224},{224,1... | collective-permute-start | bytes 9437192 | tf_op jit(solution)/shard_map/ppermute | solution.py:663
  36.7 35.9 %all_to_all.36 = bf16[32,32,128]{2,1,0:T(8,128)(2,1)S(1)} all-to-all(bf16[32,32,128]{2,1,0:T(8,128)(2,1)S(1)} %bitcast.20), channel_id=1, replica_groups=mesh['ctx'=16,'exp'=32] {'exp'}, dimensions={0} | all-to-all | bytes 524288 | tf_op jit(solution)/shard_map/all_to_all | solution.py:637
  72.6 0.4 shard_map.183
  73.0 22.3 %all_to_all.37 = bf16[8,24,4096]{2,1,0:T(8,128)(2,1)S(1)} all-to-all(bf16[8,24,4096]{2,1,0:T(8,128)(2,1)S(1)} %get-tuple-element.45), channel_id=1, replica_groups={{0,64,128,192,256,320,384,448},{32,96,160,224,288,352,416,480},{1,65,12..., dimensions={0} | all-to-all | bytes 3145728 | tf_op jit(solution)/shard_map/all_to_all | solution.py:637
  95.3 0.0 collective-permute-done.1.other_ref
  95.3 4.6 %shard_map.184 = bf16[192,4096]{1,0:T(8,128)(2,1)S(1)} custom-call(bf16[192,4096]{1,0:T(8,128)(2,1)S(1)} %bitcast.16, f32[2,4096]{1,0:T(2,128)S(1)} %get-tuple-element.46.gain_ref, bf16[12288,128]{1,0:T(8,128)(2,1)S(1)} %get-tuple-element.47.own_ref, bf16[12288,128]{1,0:T(8,128)(2,1)S(1)} %collective-permute-done.1.other_ref), custom_call_target="tpu_custom_call" | custom-call | tf_op jit(solution)/shard_map/pallas_call | solution.py:745
  99.9 21.4 %all_to_all.38.terms_ref = bf16[8,24,4096]{2,1,0:T(8,128)(2,1)S(1)} all-to-all(bf16[8,24,4096]{2,1,0:T(8,128)(2,1)S(1)} %bitcast.17), channel_id=1, replica_groups={{0,64,128,192,256,320,384,448},{32,96,160,224,288,352,416,480},{1,65,12..., dimensions={0} | all-to-all | bytes 3145728 | tf_op jit(solution)/shard_map/all_to_all | solution.py:637
  121.3 0.4 shard_map.185
  121.7 22.6 %all_to_all.39 = bf16[32,24,128]{2,1,0:T(8,128)(2,1)S(1)} all-to-all(bf16[32,24,128]{2,1,0:T(8,128)(2,1)S(1)} %shard_map.185), channel_id=1, replica_groups=mesh['ctx'=16,'exp'=32] {'exp'}, dimensions={0} | all-to-all | bytes 393216 | tf_op jit(solution)/shard_map/all_to_all | solution.py:637
  144.3 0.0 copy-done
  144.3 0.0 copy-done.1
  144.3 0.0 copy-done.3
  144.3 1.5 shard_map.186
  145.9 11.9 %all_to_all.40.grad_same_ref = bf16[8,224,128]{2,1,0:T(8,128)(2,1)S(1)} all-to-all(bf16[8,224,128]{2,1,0:T(8,128)(2,1)S(1)} %get-tuple-element.59), channel_id=1, replica_groups={{0,64,128,192,256,320,384,448},{32,96,160,224,288,352,416,480},{1,65,12..., dimensions={0} | all-to-all | bytes 917504 | tf_op jit(solution)/shard_map/all_to_all | solution.py:637
  157.8 7.9 %collective-permute-start.2 = (bf16[8,224,128]{2,1,0:T(8,128)(2,1)S(1)}, bf16[8,224,128]{2,1,0:T(8,128)(2,1)S(1)}, u32[]{:S(2)}, u32[]{:S(2)}) collective-permute-start(bf16[8,224,128]{2,1,0:T(8,128)(2,1)S(1)} %all_to_all.40.grad_same_ref), channel_id=1, source_target_pairs={{0,32},{32,0},{64,96},{96,64},{128,160},{160,128},{192,224},{224,1... | collective-permute-start | bytes 1376264 | tf_op jit(solution)/shard_map/ppermute | solution.py:663
  165.6 3.1 %shard_map.188 = (f32[2,192,256]{2,1,0:T(8,128)S(1)}, f32[2,192,128]{2,1,0:T(8,128)S(1)}) custom-call(s32[1]{0:T(128)} %bitcast.place_ref, bf16[8,224,256]{2,1,0:T(8,128)(2,1)S(1)} %all_to_all.35.same_ref, bf16[8,224,128]{2,1,0:T(8,128)(2,1)S(1)} %all_to_all.40.grad_same_ref, bf16[192,256]{1,0:T(8,128)(2,1)S(1)} %get-tuple-element.37.own_key_ref, ...), custom_call_target="tpu_custom_call" | custom-call | tf_op jit(solution)/shard_map/pallas_call | solution.py:766
  168.8 0.0 copy-start.2
  168.8 0.0 collective-permute-done.2.grad_cross_ref
  168.8 3.8 %shard_map.189 = (bf16[192,128]{1,0:T(8,128)(2,1)}, bf16[192,128]{1,0:T(8,128)(2,1)}, bf16[48,128]{1,0:T(8,128)(2,1)S(1)}) custom-call(s32[1]{0:T(128)} %bitcast.place_ref, bf16[8,224,256]{2,1,0:T(8,128)(2,1)S(1)} %collective-permute-done.cross_ref, bf16[8,224,128]{2,1,0:T(8,128)(2,1)S(1)} %collective-permute-done.2.grad_cross_ref, ...), custom_call_target="tpu_custom_call" | custom-call | tf_op jit(solution)/shard_map/pallas_call | solution.py:777
  172.6 2.3 %collective-permute-start.3 = (bf16[48,128]{1,0:T(8,128)(2,1)S(1)}, bf16[48,128]{1,0:T(8,128)(2,1)S(1)}, u32[]{:S(2)}, u32[]{:S(2)}) collective-permute-start(bf16[48,128]{1,0:T(8,128)(2,1)S(1)} %get-tuple-element.63.own_ref), channel_id=1, source_target_pairs={{0,16},{1,17},{2,18},{3,19},{4,20},{5,21},{6,22},{7,23},{8,24},{9,... | collective-permute-start | bytes 36872 | tf_op jit(solution)/shard_map/ppermute | solution.py:786
  174.9 2.1 %collective-permute-done.3.other_ref = bf16[48,128]{1,0:T(8,128)(2,1)S(1)} collective-permute-done((bf16[48,128]{1,0:T(8,128)(2,1)S(1)}, bf16[48,128]{1,0:T(8,128)(2,1)S(1)}, u32[]{:S(2)}, u32[]{:S(2)}) %collective-permute-start.3) | collective-permute-done | bytes 12320 | tf_op jit(solution)/shard_map/ppermute | solution.py:786
  177.0 0.7 shard_map.190
  177.7 3.5 %all-to-all-start.6 = ((bf16[16,48,128]{2,1,0:T(8,128)(2,1)}), bf16[16,48,128]{2,1,0:T(8,128)(2,1)S(1)}, u32[]{:S(2)}, u32[]{:S(2)}) async-start(bf16[16,48,128]{2,1,0:T(8,128)(2,1)} %shard_map.190), calls=%async_computation.6 | async-start | bytes 393216 | tf_op jit(solution)/shard_map/all_to_all | solution.py:637
  181.3 2.1 %shard_map.187 = (bf16[192,128]{1,0:T(8,128)(2,1)}, bf16[64,192]{1,0:T(8,128)(2,1)}) custom-call(s32[1]{0:T(128)} %bitcast.place_ref, bf16[4,384,256]{2,1,0:T(8,128)(2,1)S(1)} %get-tuple-element.53.same_keys_ref, bf16[4,384,128]{2,1,0:T(8,128)(2,1)S(1)} %get-tuple-element.39.same_vals_ref, bf16[4,384,256]{2,1,0:T(8,128)(2,1)S(1)} %get-tuple-element.54.cross_keys_ref, ...), custom_call_target="tpu_custom_call" | custom-call | tf_op jit(solution)/shard_map/pallas_call | solution.py:794
  183.4 10.3 %all-to-all-done.6.terms_ref = bf16[16,48,128]{2,1,0:T(8,128)(2,1)S(1)} async-done(((bf16[16,48,128]{2,1,0:T(8,128)(2,1)}), bf16[16,48,128]{2,1,0:T(8,128)(2,1)S(1)}, u32[]{:S(2)}, u32[]{:S(2)}) %all-to-all-start.6) | async-done | bytes 196640 | tf_op jit(solution)/shard_map/all_to_all | solution.py:637
  193.6 0.9 shard_map.191
  (6 shorter events, 0.0 us)
Async XLA Ops:
  23.1 7.6 %collective-permute-start = (bf16[8,224,256]{2,1,0:T(8,128)(2,1)S(1)}, bf16[8,224,256]{2,1,0:T(8,128)(2,1)S(1)}, u32[]{:S(2)}, u32[]{:S(2)}) collective-permute-start(bf16[8,224,256]{2,1,0:T(8,128)(2,1)S(1)} %all_to_all.35.same_ref), channel_id=1, source_target_pairs={{0,32},{32,0},{64,96},{96,64},{128,160},{160,128},{192,224},{224,1... | collective-permute-start | bytes 2752520 | tf_op jit(solution)/shard_map/ppermute | solution.py:663
  34.4 60.9 %collective-permute-start.1 = (bf16[12288,128]{1,0:T(8,128)(2,1)S(1)}, bf16[12288,128]{1,0:T(8,128)(2,1)S(1)}, u32[]{:S(2)}, u32[]{:S(2)}) collective-permute-start(bf16[12288,128]{1,0:T(8,128)(2,1)S(1)} %get-tuple-element.47.own_ref), channel_id=1, source_target_pairs={{0,32},{32,0},{64,96},{96,64},{128,160},{160,128},{192,224},{224,1... | collective-permute-start | bytes 9437192 | tf_op jit(solution)/shard_map/ppermute | solution.py:663
  121.3 23.1 %copy-start = (bf16[192,128]{1,0:T(8,128)(2,1)S(1)}, bf16[192,128]{1,0:T(8,128)(2,1)}, u32[]{:S(2)}) copy-start(bf16[192,128]{1,0:T(8,128)(2,1)} %hidden_ref.3) | copy-start | bytes 147460
  121.3 23.1 %copy-start.1 = (bf16[192,128]{1,0:T(8,128)(2,1)S(1)}, bf16[192,128]{1,0:T(8,128)(2,1)}, u32[]{:S(2)}) copy-start(bf16[192,128]{1,0:T(8,128)(2,1)} %cotangent_ref.3) | copy-start | bytes 147460
  121.3 23.1 %copy-start.3 = (f32[192,8]{0,1:T(8,128)S(1)}, f32[192,8]{0,1:T(8,128)}, u32[]{:S(2)}) copy-start(f32[192,8]{0,1:T(8,128)} %param.21) | copy-start | bytes 18436
  121.3 23.1 %copy-start.4 = (s32[192]{0:T(256)S(1)}, s32[192]{0:T(256)}, u32[]{:S(2)}) copy-start(s32[192]{0:T(256)} %param.20) | copy-start | bytes 2308
  157.8 11.0 %collective-permute-start.2 = (bf16[8,224,128]{2,1,0:T(8,128)(2,1)S(1)}, bf16[8,224,128]{2,1,0:T(8,128)(2,1)S(1)}, u32[]{:S(2)}, u32[]{:S(2)}) collective-permute-start(bf16[8,224,128]{2,1,0:T(8,128)(2,1)S(1)} %all_to_all.40.grad_same_ref), channel_id=1, source_target_pairs={{0,32},{32,0},{64,96},{96,64},{128,160},{160,128},{192,224},{224,1... | collective-permute-start | bytes 1376264 | tf_op jit(solution)/shard_map/ppermute | solution.py:663
  168.8 12.5 %copy-start.2 = (bf16[192,128]{1,0:T(8,128)(2,1)S(1)}, bf16[192,128]{1,0:T(8,128)(2,1)}, u32[]{:S(2)}) copy-start(bf16[192,128]{1,0:T(8,128)(2,1)} %get-tuple-element.30.grad_ref) | copy-start | bytes 147460
  172.6 4.4 %collective-permute-start.3 = (bf16[48,128]{1,0:T(8,128)(2,1)S(1)}, bf16[48,128]{1,0:T(8,128)(2,1)S(1)}, u32[]{:S(2)}, u32[]{:S(2)}) collective-permute-start(bf16[48,128]{1,0:T(8,128)(2,1)S(1)} %get-tuple-element.63.own_ref), channel_id=1, source_target_pairs={{0,16},{1,17},{2,18},{3,19},{4,20},{5,21},{6,22},{7,23},{8,24},{9,... | collective-permute-start | bytes 36872 | tf_op jit(solution)/shard_map/ppermute | solution.py:786
  177.7 15.9 %all-to-all-start.6 = ((bf16[16,48,128]{2,1,0:T(8,128)(2,1)}), bf16[16,48,128]{2,1,0:T(8,128)(2,1)S(1)}, u32[]{:S(2)}, u32[]{:S(2)}) async-start(bf16[16,48,128]{2,1,0:T(8,128)(2,1)} %shard_map.190), calls=%async_computation.6 | async-start | bytes 393216 | tf_op jit(solution)/shard_map/all_to_all | solution.py:637

commit v9 on v8

--- a/solution.py
+++ b/solution.py
@@ -22,6 +22,7 @@
 route_scale = 2.5
 masked_low = -1e30
 score_scale = 1.0 / math.sqrt(NOPE + ROPE)
+log2_e = math.log2(math.e)
 
 bf16 = jnp.bfloat16
 f32 = jnp.float32
@@ -140,13 +141,9 @@
     query_rope_hbm,
     query_nope_hbm,
     values_hbm,
-    gate_hbm,
-    up_hbm,
-    down_hbm,
     own_key_ref,
     own_query_ref,
     message_ref,
-    weights_ref,
     key_nope_ref,
     key_rope_ref,
     query_rope_ref,
@@ -165,16 +162,7 @@
         pltpu.make_async_copy(source, target, sems.at[index])
         for index, (source, target) in enumerate(pairs)
     ]
-    moves = [(gate_hbm, weights_ref.at[0:D, :]), (up_hbm, weights_ref.at[D : 2 * D, :])]
-    for index in range(D // LANES):
-        start = 2 * D + index * LANES
-        source = down_hbm.at[:, index * LANES : (index + 1) * LANES]
-        moves.append((source, weights_ref.at[start : start + LANES, :]))
-    moves = [
-        pltpu.make_async_copy(source, target, sems.at[len(pairs) + index])
-        for index, (source, target) in enumerate(moves)
-    ]
-    for copy in copies + moves:
+    for copy in copies:
         copy.start()
     for copy in copies:
         copy.wait()
@@ -201,9 +189,6 @@
             message_ref[index, 0:rows, :] = own_query_ref[...]
             message_ref[index, rows:, :] = empty
 
-    for copy in moves:
-        copy.wait()
-
 
 def unpack_messages(messages_ref, keys_ref, vals_ref, rows):
     for index in range(messages_ref.shape[0]):
@@ -221,8 +206,7 @@
     for index in range(keys_ref.shape[0]):
         visible = lead <= chunk_start(place, rows, index, cross)
         for head in range(2):
-            scores = nt_dot(queries[head], keys_ref[index]) * score_scale
-            scores = jnp.where(visible, scores, masked_low)
+            scores = jnp.where(visible, nt_dot(queries[head], keys_ref[index]), masked_low)
             scores_ref[head, index] = scores
             tops[head] = scores if tops[head] is None else jnp.maximum(tops[head], scores)
     return tops
@@ -234,11 +218,27 @@
     own_key_ref,
     own_query_ref,
     values_ref,
+    gate_hbm,
+    up_hbm,
+    down_hbm,
     keys_ref,
     vals_ref,
     scores_ref,
     tops_ref,
+    weights_ref,
+    sems,
 ):
+    moves = [(gate_hbm, weights_ref.at[0:D, :]), (up_hbm, weights_ref.at[D : 2 * D, :])]
+    for index in range(D // LANES):
+        start = 2 * D + index * LANES
+        source = down_hbm.at[:, index * LANES : (index + 1) * LANES]
+        moves.append((source, weights_ref.at[start : start + LANES, :]))
+    moves = [
+        pltpu.make_async_copy(source, target, sems.at[index])
+        for index, (source, target) in enumerate(moves)
+    ]
+    for copy in moves:
+        copy.start()
     rows = own_key_ref.shape[0]
     place = place_ref[0]
     unpack_messages(same_ref, keys_ref, vals_ref, rows)
@@ -250,6 +250,8 @@
     tops = score_chunks(place, queries, keys_ref, scores_ref, [None, None], False)
     for head in range(2):
         tops_ref[head] = tops[head]
+    for copy in moves:
+        copy.wait()
 
 
 def forward_kernel(
@@ -285,10 +287,10 @@
         mixed = jnp.zeros((rows, LANES), f32)
         for some_scores, some_vals in ((same_scores_ref, same_vals_ref), (scores_ref, vals_ref)):
             for index in range(some_vals.shape[0]):
-                weights = jnp.exp(some_scores[head, index] - top)
+                weights = jnp.exp2((some_scores[head, index] - top) * (score_scale * log2_e))
                 total = total + weights
                 mixed = mixed + nn_dot(weights.astype(bf16), some_vals[index])
-        state.extend([top, jnp.sum(total, 1, keepdims=True), mixed])
+        state.extend([top * score_scale, jnp.sum(total, 1, keepdims=True), mixed])
     first = lanes_of((rows, LANES)) < VDIM
     attended = jnp.where(first, state[2] / state[1], state[5] / state[4]).astype(bf16)
     attended_ref[...] = attended
@@ -467,8 +469,8 @@
             keys, vals = keys_ref[index], vals_ref[index]
             for head in range(2):
                 dot = stats_ref[:, 2 * head : 2 * head + 1]
-                log = stats_ref[:, 2 * head + 1 : 2 * head + 2]
-                prob = jnp.exp(nt_dot(query_ref[head], keys) * score_scale - log)
+                log = stats_ref[:, 2 * head + 1 : 2 * head + 2] * log2_e
+                prob = jnp.exp2(nt_dot(query_ref[head], keys) * (score_scale * log2_e) - log)
                 prob = jnp.where(visible, prob, 0.0)
                 grad_prob = nt_dot(grads_ref[head], vals)
                 grad_score = (prob * (grad_prob - dot)).astype(bf16)
@@ -520,7 +522,8 @@
             at = 6 * head
             dot = lines[at : at + 1] + lines[at + 1 : at + 2] + lines[at + 2 : at + 3]
             log = lines[at + 3 : at + 4] + lines[at + 4 : at + 5] + lines[at + 5 : at + 6]
-            prob = jnp.exp(nt_dot(keys[head], queries) * score_scale - log)
+            prob = nt_dot(keys[head], queries) * (score_scale * log2_e)
+            prob = jnp.exp2(prob - log * log2_e)
             prob = jnp.where(visible, prob, 0.0)
             grad_prob = nt_dot(vals[head], grads)
             grad_score = (prob * (grad_prob - dot)).astype(bf16)
@@ -613,12 +616,12 @@
     out_ref[...] = out.astype(bf16)
 
 
-def call(body, limit, outs, scratch=(), scalars=0, count=0, space=pltpu.VMEM):
-    place = [pl.BlockSpec(memory_space=pltpu.SMEM)] * scalars
+def call(body, limit, outs, scratch=(), scalars=0, count=0, far=0):
+    spaces = [pltpu.SMEM] * scalars + [pltpu.VMEM] * count + [pltpu.HBM] * far
     return pl.pallas_call(
         body,
         out_shape=outs,
-        in_specs=place + [pl.BlockSpec(memory_space=space)] * count,
+        in_specs=[pl.BlockSpec(memory_space=space) for space in spaces],
         out_specs=jax.tree.map(lambda _: pl.BlockSpec(memory_space=pltpu.VMEM), outs),
         scratch_shapes=list(scratch),
         compiler_params=pltpu.CompilerParams(vmem_limit_bytes=limit * MIB),
@@ -666,14 +669,13 @@
     route = expert_route.reshape(1, rows)
     affinity = affinity.T
     tall = rows + ROPE
-    own_key_rows, own_query_rows, messages, weights = call(
+    own_key_rows, own_query_rows, messages = call(
         pack_kernel,
-        12,
+        6,
         (
             shape_of(rows, 2 * width),
             shape_of(rows, 2 * width),
             shape_of(half, tall, 2 * width),
-            shape_of(3 * D, LANES),
         ),
         [
             pltpu.VMEM((rows, width), bf16),
@@ -681,34 +683,40 @@
             pltpu.VMEM((2 * ROPE, rows), bf16),
             pltpu.VMEM((rows, width), bf16),
             pltpu.VMEM((rows, width), bf16),
-            pltpu.SemaphoreType.DMA((7 + D // LANES,)),
+            pltpu.SemaphoreType.DMA((5,)),
         ],
         1,
-        8,
-        pltpu.HBM,
+        0,
+        5,
     )(
         place,
         *(held(value) for value in (key_nope, key_rope.T, query_rope.T, query_nope, values)),
-        *(held(value[0]) for value in (gate_weight, up_weight, down_weight)),
     )
     own = (own_key_rows, own_query_rows, held(values))
     same = exchange(messages, "ctx", by_core)
     cross = swap(same)
 
     chunks = half // 2
-    same_keys, same_vals, same_scores, tops = call(
+    same_keys, same_vals, same_scores, tops, weights = call(
         same_scores_kernel,
-        20,
+        26,
         (
             shape_of(chunks, 2 * rows, 2 * width),
             shape_of(chunks, 2 * rows, width),
             shape_of(2, chunks, rows, 2 * rows, dtype=f32),
             shape_of(2, rows, 2 * rows, dtype=f32),
+            shape_of(3 * D, LANES),
         ),
-        (),
+        [pltpu.SemaphoreType.DMA((2 + D // LANES,))],
         1,
         4,
-    )(place, same, *own)
+        3,
+    )(
+        place,
+        same,
+        *own,
+        *(held(value[0]) for value in (gate_weight, up_weight, down_weight)),
+    )
     attended, logs, send, cross_keys, cross_vals = call(
         functools.partial(forward_kernel, experts),
         20,

time: 198 us -> 199 us (level)
  transfers between devices with their start and end apart: 5 -> 5, of which waited for: 3 -> 2; matrix products, arithmetic and copies ran while one was open for 0% -> 0% of each run, Pallas kernels for 4% -> 5%
where the time goes in v9:
time: 199 us; the launch traced here: 195 us
  blocking collectives  134 us (67%)
  Pallas kernels  26.1 us (13%)
  starting transfers between devices  21.2 us (11%)
  waiting for transfers between devices  12.4 us (6%)
    all_to_all x6, blocking collectives, exchange(): lax.all_to_all(blocks, axis, 0, 0, tiled=True, axis_index_groups=groups)  134 us
    ppermute x3, starting transfers between devices, swap(): return lax.ppermute(value, 'ctx', across)  15.3 us
    all_to_all x1, waiting for transfers between devices, exchange(): lax.all_to_all(blocks, axis, 0, 0, tiled=True, axis_index_groups=groups)  10.3 us
    pallas_call x1, Pallas kernels, per_device(): call(expert_kernel, 24, shape_of(half * PAIR, D), count=4)  4.64 us
  transfers between devices with their start and end apart: 5, of which 2 were waited for; matrix products, arithmetic and copies ran while one was open for 0% of the time, Pallas kernels for 5%

profile of v9, /device:TPU:1, one launch (start us, length us, event | category | flops | bytes accessed | tf_op | source)
XLA Modules:
  0.0 194.7 jit_solution(5811466451092851845)
XLA Ops:
  0.6 1.3 shard_map.180
  1.9 20.2 %all_to_all.35.same_ref = bf16[8,224,256]{2,1,0:T(8,128)(2,1)S(1)} all-to-all(bf16[8,224,256]{2,1,0:T(8,128)(2,1)S(1)} %get-tuple-element.36), channel_id=1, replica_groups={{0,64,128,192,256,320,384,448},{32,96,160,224,288,352,416,480},{1,65,12..., dimensions={0} | all-to-all | bytes 1835008 | tf_op jit(solution)/shard_map/all_to_all | solution.py:640
  22.1 5.5 %collective-permute-start = (bf16[8,224,256]{2,1,0:T(8,128)(2,1)S(1)}, bf16[8,224,256]{2,1,0:T(8,128)(2,1)S(1)}, u32[]{:S(2)}, u32[]{:S(2)}) collective-permute-start(bf16[8,224,256]{2,1,0:T(8,128)(2,1)S(1)} %all_to_all.35.same_ref), channel_id=1, source_target_pairs={{0,32},{32,0},{64,96},{96,64},{128,160},{160,128},{192,224},{224,1... | collective-permute-start | bytes 2752520 | tf_op jit(solution)/shard_map/ppermute | solution.py:666
  27.7 3.4 %shard_map.181 = (bf16[4,384,256]{2,1,0:T(8,128)(2,1)S(1)}, bf16[4,384,128]{2,1,0:T(8,128)(2,1)S(1)}, f32[2,4,192,384]{3,2,1,0:T(8,128)S(1)}, f32[2,192,384]{2,1,0:T(8,128)S(1)}, bf16[12288,128]{1,0:T(8,128)(2,1)S(1)}) custom-call(s32[1]{0:T(128)} %bitcast.place_ref, bf16[8,224,256]{2,1,0:T(8,128)(2,1)S(1)} %all_to_all.35.same_ref, ...), custom_call_target="tpu_custom_call" | custom-call | tf_op jit(solution)/shard_map/pallas_call | solution.py:700
  31.1 0.0 collective-permute-done.cross_ref
  31.1 3.7 %shard_map.182 = (bf16[192,128]{1,0:T(8,128)(2,1)S(1)}, f32[192,128]{1,0:T(8,128)S(1)}, bf16[1024,128]{1,0:T(8,128)(2,1)S(1)}, bf16[4,384,256]{2,1,0:T(8,128)(2,1)S(1)}, bf16[4,384,128]{2,1,0:T(8,128)(2,1)S(1)}) custom-call(s32[1]{0:T(128)} %bitcast.place_ref, bf16[8,224,256]{2,1,0:T(8,128)(2,1)S(1)} %collective-permute-done.cross_ref, ...), custom_call_target="tpu_custom_call" | custom-call | tf_op jit(solution)/shard_map/pallas_call | solution.py:720
  34.8 1.9 collective-permute-start.1
  36.7 35.3 %all_to_all.36 = bf16[32,32,128]{2,1,0:T(8,128)(2,1)S(1)} all-to-all(bf16[32,32,128]{2,1,0:T(8,128)(2,1)S(1)} %bitcast.20), channel_id=1, replica_groups=mesh['ctx'=16,'exp'=32] {'exp'}, dimensions={0} | all-to-all | bytes 524288 | tf_op jit(solution)/shard_map/all_to_all | solution.py:640
  72.1 0.4 shard_map.183
  72.5 22.4 %all_to_all.37 = bf16[8,24,4096]{2,1,0:T(8,128)(2,1)S(1)} all-to-all(bf16[8,24,4096]{2,1,0:T(8,128)(2,1)S(1)} %get-tuple-element.45), channel_id=1, replica_groups={{0,64,128,192,256,320,384,448},{32,96,160,224,288,352,416,480},{1,65,12..., dimensions={0} | all-to-all | bytes 3145728 | tf_op jit(solution)/shard_map/all_to_all | solution.py:640
  94.9 0.0 collective-permute-done.1.other_ref
  94.9 4.6 %shard_map.184 = bf16[192,4096]{1,0:T(8,128)(2,1)S(1)} custom-call(bf16[192,4096]{1,0:T(8,128)(2,1)S(1)} %bitcast.16, f32[2,4096]{1,0:T(2,128)S(1)} %get-tuple-element.46.gain_ref, bf16[12288,128]{1,0:T(8,128)(2,1)S(1)} %get-tuple-element.47.own_ref, bf16[12288,128]{1,0:T(8,128)(2,1)S(1)} %collective-permute-done.1.other_ref), custom_call_target="tpu_custom_call" | custom-call | tf_op jit(solution)/shard_map/pallas_call | solution.py:753
  99.5 20.6 %all_to_all.38.terms_ref = bf16[8,24,4096]{2,1,0:T(8,128)(2,1)S(1)} all-to-all(bf16[8,24,4096]{2,1,0:T(8,128)(2,1)S(1)} %bitcast.17), channel_id=1, replica_groups={{0,64,128,192,256,320,384,448},{32,96,160,224,288,352,416,480},{1,65,12..., dimensions={0} | all-to-all | bytes 3145728 | tf_op jit(solution)/shard_map/all_to_all | solution.py:640
  120.1 0.4 shard_map.185
  120.5 23.9 %all_to_all.39 = bf16[32,24,128]{2,1,0:T(8,128)(2,1)S(1)} all-to-all(bf16[32,24,128]{2,1,0:T(8,128)(2,1)S(1)} %shard_map.185), channel_id=1, replica_groups=mesh['ctx'=16,'exp'=32] {'exp'}, dimensions={0} | all-to-all | bytes 393216 | tf_op jit(solution)/shard_map/all_to_all | solution.py:640
  144.4 0.0 copy-done
  144.4 0.0 copy-done.1
  144.4 0.0 copy-done.3
  144.4 1.5 shard_map.186
  146.0 11.9 %all_to_all.40.grad_same_ref = bf16[8,224,128]{2,1,0:T(8,128)(2,1)S(1)} all-to-all(bf16[8,224,128]{2,1,0:T(8,128)(2,1)S(1)} %get-tuple-element.59), channel_id=1, replica_groups={{0,64,128,192,256,320,384,448},{32,96,160,224,288,352,416,480},{1,65,12..., dimensions={0} | all-to-all | bytes 917504 | tf_op jit(solution)/shard_map/all_to_all | solution.py:640
  157.9 7.9 %collective-permute-start.2 = (bf16[8,224,128]{2,1,0:T(8,128)(2,1)S(1)}, bf16[8,224,128]{2,1,0:T(8,128)(2,1)S(1)}, u32[]{:S(2)}, u32[]{:S(2)}) collective-permute-start(bf16[8,224,128]{2,1,0:T(8,128)(2,1)S(1)} %all_to_all.40.grad_same_ref), channel_id=1, source_target_pairs={{0,32},{32,0},{64,96},{96,64},{128,160},{160,128},{192,224},{224,1... | collective-permute-start | bytes 1376264 | tf_op jit(solution)/shard_map/ppermute | solution.py:666
  165.7 3.1 %shard_map.188 = (f32[2,192,256]{2,1,0:T(8,128)S(1)}, f32[2,192,128]{2,1,0:T(8,128)S(1)}) custom-call(s32[1]{0:T(128)} %bitcast.place_ref, bf16[8,224,256]{2,1,0:T(8,128)(2,1)S(1)} %all_to_all.35.same_ref, bf16[8,224,128]{2,1,0:T(8,128)(2,1)S(1)} %all_to_all.40.grad_same_ref, bf16[192,256]{1,0:T(8,128)(2,1)S(1)} %get-tuple-element.37.own_key_ref, ...), custom_call_target="tpu_custom_call" | custom-call | tf_op jit(solution)/shard_map/pallas_call | solution.py:774
  168.9 0.0 copy-start.2
  168.9 0.0 collective-permute-done.2.grad_cross_ref
  168.9 3.9 %shard_map.189 = (bf16[192,128]{1,0:T(8,128)(2,1)}, bf16[192,128]{1,0:T(8,128)(2,1)}, bf16[48,128]{1,0:T(8,128)(2,1)S(1)}) custom-call(s32[1]{0:T(128)} %bitcast.place_ref, bf16[8,224,256]{2,1,0:T(8,128)(2,1)S(1)} %collective-permute-done.cross_ref, bf16[8,224,128]{2,1,0:T(8,128)(2,1)S(1)} %collective-permute-done.2.grad_cross_ref, ...), custom_call_target="tpu_custom_call" | custom-call | tf_op jit(solution)/shard_map/pallas_call | solution.py:785
  172.8 2.3 %collective-permute-start.3 = (bf16[48,128]{1,0:T(8,128)(2,1)S(1)}, bf16[48,128]{1,0:T(8,128)(2,1)S(1)}, u32[]{:S(2)}, u32[]{:S(2)}) collective-permute-start(bf16[48,128]{1,0:T(8,128)(2,1)S(1)} %get-tuple-element.63.own_ref), channel_id=1, source_target_pairs={{0,16},{1,17},{2,18},{3,19},{4,20},{5,21},{6,22},{7,23},{8,24},{9,... | collective-permute-start | bytes 36872 | tf_op jit(solution)/shard_map/ppermute | solution.py:794
  175.1 2.1 %collective-permute-done.3.other_ref = bf16[48,128]{1,0:T(8,128)(2,1)S(1)} collective-permute-done((bf16[48,128]{1,0:T(8,128)(2,1)S(1)}, bf16[48,128]{1,0:T(8,128)(2,1)S(1)}, u32[]{:S(2)}, u32[]{:S(2)}) %collective-permute-start.3) | collective-permute-done | bytes 12320 | tf_op jit(solution)/shard_map/ppermute | solution.py:794
  177.2 0.7 shard_map.190
  177.9 3.5 %all-to-all-start.6 = ((bf16[16,48,128]{2,1,0:T(8,128)(2,1)}), bf16[16,48,128]{2,1,0:T(8,128)(2,1)S(1)}, u32[]{:S(2)}, u32[]{:S(2)}) async-start(bf16[16,48,128]{2,1,0:T(8,128)(2,1)} %shard_map.190), calls=%async_computation.6 | async-start | bytes 393216 | tf_op jit(solution)/shard_map/all_to_all | solution.py:640
  181.4 2.1 %shard_map.187 = (bf16[192,128]{1,0:T(8,128)(2,1)}, bf16[64,192]{1,0:T(8,128)(2,1)}) custom-call(s32[1]{0:T(128)} %bitcast.place_ref, bf16[4,384,256]{2,1,0:T(8,128)(2,1)S(1)} %get-tuple-element.53.same_keys_ref, bf16[4,384,128]{2,1,0:T(8,128)(2,1)S(1)} %get-tuple-element.39.same_vals_ref, bf16[4,384,256]{2,1,0:T(8,128)(2,1)S(1)} %get-tuple-element.54.cross_keys_ref, ...), custom_call_target="tpu_custom_call" | custom-call | tf_op jit(solution)/shard_map/pallas_call | solution.py:802
  183.5 10.3 %all-to-all-done.6.terms_ref = bf16[16,48,128]{2,1,0:T(8,128)(2,1)S(1)} async-done(((bf16[16,48,128]{2,1,0:T(8,128)(2,1)}), bf16[16,48,128]{2,1,0:T(8,128)(2,1)S(1)}, u32[]{:S(2)}, u32[]{:S(2)}) %all-to-all-start.6) | async-done | bytes 196640 | tf_op jit(solution)/shard_map/all_to_all | solution.py:640
  193.8 0.9 shard_map.191
  (6 shorter events, 0.0 us)
Async XLA Ops:
  22.1 8.9 %collective-permute-start = (bf16[8,224,256]{2,1,0:T(8,128)(2,1)S(1)}, bf16[8,224,256]{2,1,0:T(8,128)(2,1)S(1)}, u32[]{:S(2)}, u32[]{:S(2)}) collective-permute-start(bf16[8,224,256]{2,1,0:T(8,128)(2,1)S(1)} %all_to_all.35.same_ref), channel_id=1, source_target_pairs={{0,32},{32,0},{64,96},{96,64},{128,160},{160,128},{192,224},{224,1... | collective-permute-start | bytes 2752520 | tf_op jit(solution)/shard_map/ppermute | solution.py:666
  34.8 60.1 %collective-permute-start.1 = (bf16[12288,128]{1,0:T(8,128)(2,1)S(1)}, bf16[12288,128]{1,0:T(8,128)(2,1)S(1)}, u32[]{:S(2)}, u32[]{:S(2)}) collective-permute-start(bf16[12288,128]{1,0:T(8,128)(2,1)S(1)} %get-tuple-element.47.own_ref), channel_id=1, source_target_pairs={{0,32},{32,0},{64,96},{96,64},{128,160},{160,128},{192,224},{224,1... | collective-permute-start | bytes 9437192 | tf_op jit(solution)/shard_map/ppermute | solution.py:666
  120.1 24.3 %copy-start = (bf16[192,128]{1,0:T(8,128)(2,1)S(1)}, bf16[192,128]{1,0:T(8,128)(2,1)}, u32[]{:S(2)}) copy-start(bf16[192,128]{1,0:T(8,128)(2,1)} %hidden_ref.3) | copy-start | bytes 147460
  120.1 24.3 %copy-start.1 = (bf16[192,128]{1,0:T(8,128)(2,1)S(1)}, bf16[192,128]{1,0:T(8,128)(2,1)}, u32[]{:S(2)}) copy-start(bf16[192,128]{1,0:T(8,128)(2,1)} %cotangent_ref.3) | copy-start | bytes 147460
  120.1 24.3 %copy-start.3 = (f32[192,8]{0,1:T(8,128)S(1)}, f32[192,8]{0,1:T(8,128)}, u32[]{:S(2)}) copy-start(f32[192,8]{0,1:T(8,128)} %param.21) | copy-start | bytes 18436
  120.1 24.3 %copy-start.4 = (s32[192]{0:T(256)S(1)}, s32[192]{0:T(256)}, u32[]{:S(2)}) copy-start(s32[192]{0:T(256)} %param.20) | copy-start | bytes 2308
  157.9 11.0 %collective-permute-start.2 = (bf16[8,224,128]{2,1,0:T(8,128)(2,1)S(1)}, bf16[8,224,128]{2,1,0:T(8,128)(2,1)S(1)}, u32[]{:S(2)}, u32[]{:S(2)}) collective-permute-start(bf16[8,224,128]{2,1,0:T(8,128)(2,1)S(1)} %all_to_all.40.grad_same_ref), channel_id=1, source_target_pairs={{0,32},{32,0},{64,96},{96,64},{128,160},{160,128},{192,224},{224,1... | collective-permute-start | bytes 1376264 | tf_op jit(solution)/shard_map/ppermute | solution.py:666
  168.9 12.5 %copy-start.2 = (bf16[192,128]{1,0:T(8,128)(2,1)S(1)}, bf16[192,128]{1,0:T(8,128)(2,1)}, u32[]{:S(2)}) copy-start(bf16[192,128]{1,0:T(8,128)(2,1)} %get-tuple-element.30.grad_ref) | copy-start | bytes 147460
  172.8 4.4 %collective-permute-start.3 = (bf16[48,128]{1,0:T(8,128)(2,1)S(1)}, bf16[48,128]{1,0:T(8,128)(2,1)S(1)}, u32[]{:S(2)}, u32[]{:S(2)}) collective-permute-start(bf16[48,128]{1,0:T(8,128)(2,1)S(1)} %get-tuple-element.63.own_ref), channel_id=1, source_target_pairs={{0,16},{1,17},{2,18},{3,19},{4,20},{5,21},{6,22},{7,23},{8,24},{9,... | collective-permute-start | bytes 36872 | tf_op jit(solution)/shard_map/ppermute | solution.py:794
  177.9 15.9 %all-to-all-start.6 = ((bf16[16,48,128]{2,1,0:T(8,128)(2,1)}), bf16[16,48,128]{2,1,0:T(8,128)(2,1)S(1)}, u32[]{:S(2)}, u32[]{:S(2)}) async-start(bf16[16,48,128]{2,1,0:T(8,128)(2,1)} %shard_map.190), calls=%async_computation.6 | async-start | bytes 393216 | tf_op jit(solution)/shard_map/all_to_all | solution.py:640
